TPU v7x, 512 devices: a whole 4x4x16 slice. The times are simulated.
512 devices in a mesh: grid: 64 (over y, z_lo, core), band: 8 (over z_hi, x).
Axes of the slice: x: 4, y: 4, z: 16 (z_hi: 2, z_lo: 8; z = z_hi * 8 + z_lo), core: 2. Of those that a mesh axis runs over, the one named last changes fastest.
Arguments:
- orbitals: bfloat16 [32, 64, 16, 32, 128], P('band', 'grid'), may hold values from -7 to 7
- occupations: float32 [32], P('band'), may hold values from 0.5 to 2
- density_in: float32 [64, 16, 32, 128], P('grid'), may hold values from 0.4 to 18
- history_in: bfloat16 [8, 64, 16, 32, 128], P(None, 'grid'), may hold values from 0.29882812 to 3
- history_res: bfloat16 [8, 64, 16, 32, 128], P(None, 'grid'), may hold values from -16 to 16
- screening: float32 [1], replicated, may hold values from 1.5 to 4
Outputs:
- density_next: float32 [64, 16, 32, 128], P('grid')
- residual: float32 [64, 16, 32, 128], P('grid')
All inputs are finite; a program needn't handle non-finite values.
Results may differ from a plain program's by a relative error of at most 0.0003.
Values sent between devices are 32-bit elements; how exact they have to be, the bound alone decides.
A program may use at most 64 MiB of HBM per device.

v0:
```python
import jax
import jax.numpy as jnp
from jax import lax
from jax.sharding import PartitionSpec as P

SWEEPS = 4


mixing_weight = 0.5


def partner(value, axis, apart):
    mask = 2**apart
    pairs = [(source, source ^ mask) for source in range(lax.axis_size(axis))]
    return lax.ppermute(value, axis, pairs)


def shifted(block, axis, distance):
    devices = range(lax.axis_size(axis))
    route = [(i - distance, i) for i in devices if i - distance in devices]
    return lax.ppermute(block, axis, route)


def fetch_whole(field, bit_list):
    for bit in bit_list:
        field = partner(field, "grid", bit)
    return field


def symmetrize(field, fetch, bits_x, bits_y, bits_z):
    field = 0.5 * (field + jnp.flip(fetch(field, bits_x), 1))
    field = 0.5 * (field + jnp.flip(fetch(field, bits_y), 2))
    field = 0.5 * (field + jnp.flip(fetch(field, bits_z), 3))
    return field


def neighbour(face, offset):
    return shifted(face, "grid", offset)


def local(orbitals, occupations, density_in, history_in, history_res, screening):
    n_grid = lax.axis_size("grid")
    grid_bits = n_grid.bit_length() - 1
    waves = orbitals.astype(jnp.float32)
    partial_value = jnp.sum(occupations[:, None, None, None, None] * waves * waves, 0)
    rho_out = lax.psum(partial_value, "band")
    rho_sym = symmetrize(rho_out, fetch_whole, list(range(4, grid_bits)), [2, 3], [0, 1])
    depth = history_res.shape[0]
    res_hist = history_res.astype(jnp.float32)
    charges = lax.psum(jnp.stack([jnp.sum(rho_sym), jnp.sum(density_in)]), "grid")
    scale = charges[1] / charges[0]
    residual = scale * rho_sym - density_in
    vectors = jnp.concatenate([res_hist, residual[None]], 0).reshape(depth + 1, -1)
    local_gram = jnp.dot(vectors, vectors.T, precision=lax.Precision.HIGHEST)
    gram = lax.psum(local_gram, "grid")
    lower = jnp.linalg.cholesky(gram)
    solved = jax.scipy.linalg.cho_solve((lower, True), jnp.ones((depth + 1,), jnp.float32))
    coefficients = solved / jnp.sum(solved)
    rho_opt = (
        jnp.einsum(
            "m,mgxyz->gxyz",
            coefficients[:depth],
            history_in.astype(jnp.float32),
            precision=lax.Precision.HIGHEST,
        )
        + coefficients[depth] * density_in
    )
    res_opt = (
        jnp.einsum("m,mgxyz->gxyz", coefficients[:depth], res_hist, precision=lax.Precision.HIGHEST)
        + coefficients[depth] * residual
    )
    kappa = screening[0]
    index = lax.axis_index("grid")
    block_x = index // 16
    block_y = index // 4 % 4
    block_z = index % 4
    keep_xlow = (block_x > 0).astype(jnp.float32)
    keep_ylow = (block_y > 0).astype(jnp.float32)
    keep_yhigh = (block_y < 3).astype(jnp.float32)
    keep_zlow = (block_z > 0).astype(jnp.float32)
    keep_zhigh = (block_z < 3).astype(jnp.float32)
    source = res_opt[0]
    field_u = jnp.zeros_like(source)
    for sweep in range(SWEEPS):
        x_low = neighbour(field_u[-1:], 16) * keep_xlow
        x_high = neighbour(field_u[:1], -16)
        y_low = neighbour(field_u[:, -1:], 4) * keep_ylow
        y_high = neighbour(field_u[:, :1], -4) * keep_yhigh
        z_low = neighbour(field_u[:, :, -1:], 1) * keep_zlow
        z_high = neighbour(field_u[:, :, :1], -1) * keep_zhigh
        along_x = jnp.concatenate([x_low, field_u, x_high], 0)
        along_y = jnp.concatenate([y_low, field_u, y_high], 1)
        along_z = jnp.concatenate([z_low, field_u, z_high], 2)
        beside = along_x[:-2] + along_x[2:]
        beside = beside + along_y[:, :-2] + along_y[:, 2:]
        beside = beside + along_z[:, :, :-2] + along_z[:, :, 2:]
        field_u = (source + beside) / (6.0 + kappa)
    density_next = rho_opt + mixing_weight * (res_opt - kappa * field_u[None])
    return (density_next, residual)


def solution(mesh):
    in_specs = (
        P("band", "grid", None, None, None),
        P("band"),
        P("grid", None, None, None),
        P(None, "grid", None, None, None),
        P(None, "grid", None, None, None),
        P(),
    )
    out_specs = (P("grid", None, None, None), P("grid", None, None, None))
    return jax.shard_map(local, mesh=mesh, in_specs=in_specs, out_specs=out_specs, check_vma=False)
```

profile of v0, /device:TPU:1, one launch (start us, length us, event | category | flops | bytes accessed | tf_op | source)
XLA Modules:
  0.0 780.3 jit_solution(13246422287680302552)
XLA Ops:
  7.2 2.1 fusion.4
  9.4 153.7 %all-reduce.8.cloned.1.call-done = f32[1,16,32,128]{3,2,1,0:T(8,128)} async-done(((f32[1,16,32,128]{3,2,1,0:T(8,128)}), f32[1,16,32,128]{3,2,1,0:T(8,128)}) %all-reduce.8.cloned.1.call-update) | async-done | bytes 262160 | tf_op jit(solution)/shard_map/psum | solution.py:46
  163.1 3.1 collective-permute-start
  166.2 4.2 collective-permute-done
  170.4 4.6 collective-permute-start.1
  175.0 6.7 collective-permute-done.1
  182.8 2.2 collective-permute-start.2
  186.3 4.9 collective-permute-start.8
  191.9 9.7 %collective-permute-start.11 = (f32[16,32,1]{2,1,0:T(8,128)}, f32[16,32,1]{2,1,0:T(8,128)}, u32[]{:S(2)}, u32[]{:S(2)}) collective-permute-start(f32[16,32,1]{2,1,0:T(8,128)} %broadcast.114), channel_id=1, source_target_pairs={{8,0},{16,8},{24,16},{32,24},{40,32},{48,40},{56,48},{64,56},{72,6... | collective-permute-start | bytes 6152 | tf_op jit(solution)/shard_map/ppermute | solution.py:21
  201.6 2.3 collective-permute-start.10
  205.3 4.5 collective-permute-start.3
  209.8 1.9 copy_convert_fusion
  211.7 26.8 %collective-permute-done.3 = f32[1,16,32,128]{3,2,1,0:T(8,128)S(1)} collective-permute-done((f32[1,16,32,128]{3,2,1,0:T(8,128)S(1)}, f32[1,16,32,128]{3,2,1,0:T(8,128)S(1)}, u32[]{:S(2)}, u32[]{:S(2)}) %collective-permute-start.3) | collective-permute-done | bytes 262176 | tf_op jit(solution)/shard_map/ppermute | solution.py:15
  238.5 3.1 collective-permute-start.6
  241.8 3.2 collective-permute-start.4
  247.3 1.9 collective-permute-start.5
  249.2 8.0 %collective-permute-done.5 = f32[1,16,32,128]{3,2,1,0:T(8,128)} collective-permute-done((f32[1,16,32,128]{3,2,1,0:T(8,128)S(1)}, f32[1,16,32,128]{3,2,1,0:T(8,128)}, u32[]{:S(2)}, u32[]{:S(2)}) %collective-permute-start.5) | collective-permute-done | bytes 262176 | tf_op jit(solution)/shard_map/ppermute | solution.py:15
  260.9 210.5 %psum.22 = f32[2]{0:T(128)S(1)} all-reduce(f32[2]{0:T(128)S(1)} %pad_maximum_fusion.18), channel_id=1, replica_groups=mesh['grid'=64,'band'=8] {'grid'}, use_global_device_ids=true, to_apply=%region_4.5 | all-reduce | flops 2 | bytes 16 | tf_op jit(solution)/shard_map/psum | solution.py:50
  474.4 8.0 %fusion.3 = f32[9,9]{0,1:T(8,128)S(1)} fusion(f32[1,1,16,32,128]{4,0,3,2,1:T(1,128)S(1)} %bitcast.88, f32[8,1,16,32,128]{4,0,3,2,1:T(8,128)} %copy_convert_fusion), kind=kOutput, calls=%fused_computation.5 | convolution fusion | flops 64290816 | bytes 2359620 | tf_op jit(solution)/shard_map/dot_general | solution.py:54
  482.3 216.7 %psum.23 = f32[9,9]{0,1:T(8,128)S(1)} all-reduce(f32[9,9]{0,1:T(8,128)S(1)} %fusion.3), channel_id=1, replica_groups=mesh['grid'=64,'band'=8] {'grid'}, use_global_device_ids=true, to_apply=%region_5.6 | all-reduce | flops 81 | bytes 648 | tf_op jit(solution)/shard_map/psum | solution.py:55
  708.4 2.4 collective-permute-start.17
  712.1 4.9 collective-permute-start.14
  721.0 3.0 collective-permute-done.13
  724.5 4.9 collective-permute-start.22
  729.4 1.9 collective-permute-start.23
  732.6 4.9 collective-permute-start.20
  740.3 3.0 collective-permute-done.19
  743.8 5.6 collective-permute-start.28
  749.5 7.0 collective-permute-start.29
  757.7 4.9 collective-permute-start.26
  762.6 4.7 collective-permute-start.24
  768.8 3.0 collective-permute-done.25
  (102 shorter events, 35.1 us)
Async XLA Ops:
  7.2 711.1 %copy-start = (bf16[8,1,16,32,128]{4,3,2,1,0:T(8,128)(2,1)S(1)}, bf16[8,1,16,32,128]{4,3,2,1,0:T(8,128)(2,1)}, u32[]{:S(2)}) copy-start(bf16[8,1,16,32,128]{4,3,2,1,0:T(8,128)(2,1)} %param.9) | copy-start | bytes 3145732
  7.2 155.9 %all-reduce.8.cloned.1.call-start = ((), (), s32[]{:S(2)}) async-start(), calls=%async_computation | async-start | bytes 524288 | tf_op jit(solution)/shard_map/psum | solution.py:46
  163.1 7.3 collective-permute-start
  170.4 11.3 %collective-permute-start.1 = (f32[1,16,32,128]{3,2,1,0:T(8,128)S(1)}, f32[1,16,32,128]{3,2,1,0:T(8,128)S(1)}, u32[]{:S(2)}, u32[]{:S(2)}) collective-permute-start(f32[1,16,32,128]{3,2,1,0:T(8,128)S(1)} %collective-permute-done), channel_id=1, source_target_pairs={{0,256},{8,264},{16,272},{24,280},{32,288},{40,296},{48,304},{56,3... | collective-permute-start | bytes 786440 | tf_op jit(solution)/shard_map/ppermute | solution.py:15
  182.8 22.5 %collective-permute-start.2 = (f32[1,16,32,128]{3,2,1,0:T(8,128)S(1)}, f32[1,16,32,128]{3,2,1,0:T(8,128)S(1)}, u32[]{:S(2)}, u32[]{:S(2)}) collective-permute-start(f32[1,16,32,128]{3,2,1,0:T(8,128)S(1)} %add_multiply_fusion.1), channel_id=1, source_target_pairs={{0,32},{8,40},{16,48},{24,56},{32,0},{40,8},{48,16},{56,24},{64,96... | collective-permute-start | bytes 786440 | tf_op jit(solution)/shard_map/ppermute | solution.py:15
  185.0 64.2 %collective-permute-start.9 = (f32[16,1,128]{2,1,0:T(1,128)S(1)}, f32[16,1,128]{2,1,0:T(1,128)S(1)}, u32[]{:S(2)}, u32[]{:S(2)}) collective-permute-start(f32[16,1,128]{2,1,0:T(1,128)S(1)} %broadcast.113), channel_id=1, source_target_pairs={{32,0},{40,8},{48,16},{56,24},{64,32},{72,40},{80,48},{88,56},{96,... | collective-permute-start | bytes 24584 | tf_op jit(solution)/shard_map/ppermute | solution.py:21
  186.3 62.9 %collective-permute-start.8 = (f32[16,1,128]{2,1,0:T(1,128)S(1)}, f32[16,1,128]{2,1,0:T(1,128)S(1)}, u32[]{:S(2)}, u32[]{:S(2)}) collective-permute-start(f32[16,1,128]{2,1,0:T(1,128)S(1)} %broadcast.113), channel_id=1, source_target_pairs={{0,32},{8,40},{16,48},{24,56},{32,64},{40,72},{48,80},{56,88},{64,... | collective-permute-start | bytes 24584 | tf_op jit(solution)/shard_map/ppermute | solution.py:21
  191.9 49.9 %collective-permute-start.11 = (f32[16,32,1]{2,1,0:T(8,128)}, f32[16,32,1]{2,1,0:T(8,128)}, u32[]{:S(2)}, u32[]{:S(2)}) collective-permute-start(f32[16,32,1]{2,1,0:T(8,128)} %broadcast.114), channel_id=1, source_target_pairs={{8,0},{16,8},{24,16},{32,24},{40,32},{48,40},{56,48},{64,56},{72,6... | collective-permute-start | bytes 6152 | tf_op jit(solution)/shard_map/ppermute | solution.py:21
  201.6 44.3 %collective-permute-start.10 = (f32[16,32,1]{2,1,0:T(8,128)}, f32[16,32,1]{2,1,0:T(8,128)S(1)}, u32[]{:S(2)}, u32[]{:S(2)}) collective-permute-start(f32[16,32,1]{2,1,0:T(8,128)} %broadcast.114), channel_id=1, source_target_pairs={{0,8},{8,16},{16,24},{24,32},{32,40},{40,48},{48,56},{56,64},{64,7... | collective-permute-start | bytes 6152 | tf_op jit(solution)/shard_map/ppermute | solution.py:21
  205.3 33.2 %collective-permute-start.3 = (f32[1,16,32,128]{3,2,1,0:T(8,128)S(1)}, f32[1,16,32,128]{3,2,1,0:T(8,128)S(1)}, u32[]{:S(2)}, u32[]{:S(2)}) collective-permute-start(f32[1,16,32,128]{3,2,1,0:T(8,128)S(1)} %collective-permute-done.2), channel_id=1, source_target_pairs={{0,64},{8,72},{16,80},{24,88},{32,96},{40,104},{48,112},{56,120},{... | collective-permute-start | bytes 786440 | tf_op jit(solution)/shard_map/ppermute | solution.py:15
  238.5 22.4 %collective-permute-start.6 = (f32[1,32,128]{2,1,0:T(8,128)S(1)}, f32[1,32,128]{2,1,0:T(8,128)S(1)}, u32[]{:S(2)}, u32[]{:S(2)}) collective-permute-start(f32[1,32,128]{2,1,0:T(8,128)S(1)} %broadcast.112), channel_id=1, source_target_pairs={{0,128},{8,136},{16,144},{24,152},{32,160},{40,168},{48,176},{56,1... | collective-permute-start | bytes 49160 | tf_op jit(solution)/shard_map/ppermute | solution.py:21
  241.8 5.5 collective-permute-start.4
  245.9 459.6 %collective-permute-start.7 = (f32[1,32,128]{2,1,0:T(8,128)S(1)}, f32[1,32,128]{2,1,0:T(8,128)S(1)}, u32[]{:S(2)}, u32[]{:S(2)}) collective-permute-start(f32[1,32,128]{2,1,0:T(8,128)S(1)} %broadcast.112), channel_id=1, source_target_pairs={{128,0},{136,8},{144,16},{152,24},{160,32},{168,40},{176,48},{184,... | collective-permute-start | bytes 49160 | tf_op jit(solution)/shard_map/ppermute | solution.py:21
  247.3 9.9 %collective-permute-start.5 = (f32[1,16,32,128]{3,2,1,0:T(8,128)S(1)}, f32[1,16,32,128]{3,2,1,0:T(8,128)}, u32[]{:S(2)}, u32[]{:S(2)}) collective-permute-start(f32[1,16,32,128]{3,2,1,0:T(8,128)S(1)} %collective-permute-done.4), channel_id=1, source_target_pairs={{0,16},{8,24},{16,0},{24,8},{32,48},{40,56},{48,32},{56,40},{64,80... | collective-permute-start | bytes 786440 | tf_op jit(solution)/shard_map/ppermute | solution.py:15
  706.4 13.1 %collective-permute-start.16 = (f32[16,32,1]{2,1,0:T(8,128)S(1)}, f32[16,32,1]{2,1,0:T(8,128)S(1)}, u32[]{:S(2)}, u32[]{:S(2)}) collective-permute-start(f32[16,32,1]{2,1,0:T(8,128)S(1)} %get-tuple-element.22), channel_id=1, source_target_pairs={{0,8},{8,16},{16,24},{24,32},{32,40},{40,48},{48,56},{56,64},{64,7... | collective-permute-start | bytes 6152 | tf_op jit(solution)/shard_map/ppermute | solution.py:21
  708.4 12.5 %collective-permute-start.17 = (f32[16,32,1]{2,1,0:T(8,128)S(1)}, f32[16,32,1]{2,1,0:T(8,128)S(1)}, u32[]{:S(2)}, u32[]{:S(2)}) collective-permute-start(f32[16,32,1]{2,1,0:T(8,128)S(1)} %get-tuple-element.23), channel_id=1, source_target_pairs={{8,0},{16,8},{24,16},{32,24},{40,32},{48,40},{56,48},{64,56},{72,6... | collective-permute-start | bytes 6152 | tf_op jit(solution)/shard_map/ppermute | solution.py:21
  710.8 10.2 %collective-permute-start.15 = (f32[16,1,128]{2,1,0:T(1,128)S(1)}, f32[16,1,128]{2,1,0:T(1,128)S(1)}, u32[]{:S(2)}, u32[]{:S(2)}) collective-permute-start(f32[16,1,128]{2,1,0:T(1,128)S(1)} %get-tuple-element.21), channel_id=1, source_target_pairs={{32,0},{40,8},{48,16},{56,24},{64,32},{72,40},{80,48},{88,56},{96,... | collective-permute-start | bytes 24584 | tf_op jit(solution)/shard_map/ppermute | solution.py:21
  712.1 8.9 %collective-permute-start.14 = (f32[16,1,128]{2,1,0:T(1,128)S(1)}, f32[16,1,128]{2,1,0:T(1,128)S(1)}, u32[]{:S(2)}, u32[]{:S(2)}) collective-permute-start(f32[16,1,128]{2,1,0:T(1,128)S(1)} %get-tuple-element.20), channel_id=1, source_target_pairs={{0,32},{8,40},{16,48},{24,56},{32,64},{40,72},{48,80},{56,88},{64,... | collective-permute-start | bytes 24584 | tf_op jit(solution)/shard_map/ppermute | solution.py:21
  717.0 4.0 collective-permute-start.12
  719.6 4.5 collective-permute-start.13
  724.5 14.4 %collective-permute-start.22 = (f32[16,32,1]{2,1,0:T(8,128)S(1)}, f32[16,32,1]{2,1,0:T(8,128)S(1)}, u32[]{:S(2)}, u32[]{:S(2)}) collective-permute-start(f32[16,32,1]{2,1,0:T(8,128)S(1)} %get-tuple-element.16), channel_id=1, source_target_pairs={{0,8},{8,16},{16,24},{24,32},{32,40},{40,48},{48,56},{56,64},{64,7... | collective-permute-start | bytes 6152 | tf_op jit(solution)/shard_map/ppermute | solution.py:21
  729.4 10.8 %collective-permute-start.23 = (f32[16,32,1]{2,1,0:T(8,128)S(1)}, f32[16,32,1]{2,1,0:T(8,128)S(1)}, u32[]{:S(2)}, u32[]{:S(2)}) collective-permute-start(f32[16,32,1]{2,1,0:T(8,128)S(1)} %get-tuple-element.17), channel_id=1, source_target_pairs={{8,0},{16,8},{24,16},{32,24},{40,32},{48,40},{56,48},{64,56},{72,6... | collective-permute-start | bytes 6152 | tf_op jit(solution)/shard_map/ppermute | solution.py:21
  731.3 8.9 %collective-permute-start.21 = (f32[16,1,128]{2,1,0:T(1,128)S(1)}, f32[16,1,128]{2,1,0:T(1,128)S(1)}, u32[]{:S(2)}, u32[]{:S(2)}) collective-permute-start(f32[16,1,128]{2,1,0:T(1,128)S(1)} %get-tuple-element.15), channel_id=1, source_target_pairs={{32,0},{40,8},{48,16},{56,24},{64,32},{72,40},{80,48},{88,56},{96,... | collective-permute-start | bytes 24584 | tf_op jit(solution)/shard_map/ppermute | solution.py:21
  732.6 7.7 collective-permute-start.20
  737.5 2.8 collective-permute-start.18
  738.9 4.5 collective-permute-start.19
  743.8 23.5 %collective-permute-start.28 = (f32[16,32,1]{2,1,0:T(8,128)S(1)}, f32[16,32,1]{2,1,0:T(8,128)S(1)}, u32[]{:S(2)}, u32[]{:S(2)}) collective-permute-start(f32[16,32,1]{2,1,0:T(8,128)S(1)} %get-tuple-element.10), channel_id=1, source_target_pairs={{0,8},{8,16},{16,24},{24,32},{32,40},{40,48},{48,56},{56,64},{64,7... | collective-permute-start | bytes 6152 | tf_op jit(solution)/shard_map/ppermute | solution.py:21
  749.5 19.2 %collective-permute-start.29 = (f32[16,32,1]{2,1,0:T(8,128)S(1)}, f32[16,32,1]{2,1,0:T(8,128)S(1)}, u32[]{:S(2)}, u32[]{:S(2)}) collective-permute-start(f32[16,32,1]{2,1,0:T(8,128)S(1)} %get-tuple-element.11), channel_id=1, source_target_pairs={{8,0},{16,8},{24,16},{32,24},{40,32},{48,40},{56,48},{64,56},{72,6... | collective-permute-start | bytes 6152 | tf_op jit(solution)/shard_map/ppermute | solution.py:21
  756.4 12.3 %collective-permute-start.27 = (f32[16,1,128]{2,1,0:T(1,128)S(1)}, f32[16,1,128]{2,1,0:T(1,128)S(1)}, u32[]{:S(2)}, u32[]{:S(2)}) collective-permute-start(f32[16,1,128]{2,1,0:T(1,128)S(1)} %get-tuple-element.9), channel_id=1, source_target_pairs={{32,0},{40,8},{48,16},{56,24},{64,32},{72,40},{80,48},{88,56},{96,... | collective-permute-start | bytes 24584 | tf_op jit(solution)/shard_map/ppermute | solution.py:21
  757.7 11.0 %collective-permute-start.26 = (f32[16,1,128]{2,1,0:T(1,128)S(1)}, f32[16,1,128]{2,1,0:T(1,128)S(1)}, u32[]{:S(2)}, u32[]{:S(2)}) collective-permute-start(f32[16,1,128]{2,1,0:T(1,128)S(1)} %get-tuple-element.8), channel_id=1, source_target_pairs={{0,32},{8,40},{16,48},{24,56},{32,64},{40,72},{48,80},{56,88},{64,... | collective-permute-start | bytes 24584 | tf_op jit(solution)/shard_map/ppermute | solution.py:21
  762.6 6.1 collective-permute-start.24
  767.3 4.5 collective-permute-start.25
  (3 other events, 630.5 us)
Sparse Core Ops, SparseCore 0:
  11.5 151.5 all-reduce.7
where the time goes:
time: 787 us; the launch traced here: 780 us
  blocking collectives  427 us (54%)
  waiting for transfers between devices  209 us (27%)
  starting transfers between devices  95.5 us (12%)
  other arithmetic  17 us (2%)
  between operations  16.8 us (2%)
  matrix products  11.4 us (1%)
    psum x1, blocking collectives, local(): gram = lax.psum(local_gram, 'grid')  217 us
    psum x1, blocking collectives, local(): lax.psum(jnp.stack([jnp.sum(rho_sym), jnp.sum(density_in)]), 'grid')  210 us
    psum x1, waiting for transfers between devices, local(): rho_out = lax.psum(partial_value, 'band')  154 us
    ppermute x24, starting transfers between devices, shifted(): return lax.ppermute(block, axis, route)  76.1 us
    ppermute x6, waiting for transfers between devices, partner(): return lax.ppermute(value, axis, pairs)  45.7 us
    ppermute x6, starting transfers between devices, partner(): return lax.ppermute(value, axis, pairs)  19.4 us
  transfers between devices with their start and end apart: 31, of which 8 were waited for; matrix products, arithmetic and copies ran while one was open for 3% of the time, Pallas kernels for 0%

commit v1 on v0

--- a/solution.py
+++ b/solution.py
@@ -1,16 +1,96 @@
+import functools
+
 import jax
 import jax.numpy as jnp
 from jax import lax
+from jax.experimental import pallas as pl
+from jax.experimental.pallas import tpu as pltpu
 from jax.sharding import PartitionSpec as P
 
 SWEEPS = 4
-
+MESH = pl.DeviceIdType.MESH
 
 mixing_weight = 0.5
 
 
-def partner(value, axis, apart):
-    mask = 2**apart
+def _grid_sum_kernel(n, x_ref, o_ref, buf, send_sem, recv_sem):
+    me = lax.axis_index("grid")
+    band = lax.axis_index("band")
+    barrier = pltpu.get_barrier_semaphore()
+
+    def greet(k, c):
+        peer = lax.rem(me + k, n)
+        pl.semaphore_signal(barrier, inc=1, device_id=(peer, band), device_id_type=MESH)
+        return c
+
+    lax.fori_loop(1, n, greet, 0)
+    pl.semaphore_wait(barrier, n - 1)
+
+    def send(k, c):
+        peer = lax.rem(me + k, n)
+        pltpu.make_async_remote_copy(
+            src_ref=x_ref,
+            dst_ref=buf.at[me],
+            send_sem=send_sem.at[peer],
+            recv_sem=recv_sem.at[me],
+            device_id=(peer, band),
+            device_id_type=MESH,
+        ).start()
+        return c
+
+    lax.fori_loop(1, n, send, 0)
+    buf[me] = x_ref[...]
+
+    def wait(k, c):
+        peer = lax.rem(me + k, n)
+        pltpu.make_async_remote_copy(
+            src_ref=x_ref,
+            dst_ref=buf.at[me],
+            send_sem=send_sem.at[peer],
+            recv_sem=recv_sem.at[me],
+            device_id=(peer, band),
+            device_id_type=MESH,
+        ).wait_send()
+        pltpu.make_async_remote_copy(
+            src_ref=x_ref,
+            dst_ref=buf.at[peer],
+            send_sem=send_sem.at[peer],
+            recv_sem=recv_sem.at[peer],
+            device_id=(peer, band),
+            device_id_type=MESH,
+        ).wait_recv()
+        return c
+
+    lax.fori_loop(1, n, wait, 0)
+
+    def add(p, acc):
+        return acc + buf[p]
+
+    o_ref[...] = lax.fori_loop(1, n, add, buf[0])
+
+
+def grid_sum(vec, collective_id):
+    n = lax.axis_size("grid")
+    return pl.pallas_call(
+        functools.partial(_grid_sum_kernel, n),
+        out_shape=jax.ShapeDtypeStruct(vec.shape, jnp.float32),
+        in_specs=[pl.BlockSpec(memory_space=pltpu.VMEM)],
+        out_specs=pl.BlockSpec(memory_space=pltpu.VMEM),
+        scratch_shapes=[
+            pltpu.VMEM((n,) + vec.shape, jnp.float32),
+            pltpu.SemaphoreType.DMA((n,)),
+            pltpu.SemaphoreType.DMA((n,)),
+        ],
+        compiler_params=pltpu.CompilerParams(collective_id=collective_id, has_side_effects=True),
+    )(vec)
+
+
+def pack(values):
+    flat = jnp.concatenate([v.reshape(-1) for v in values])
+    return jnp.pad(flat, (0, 1024 - flat.shape[0])).reshape(8, 128)
+
+
+def partner(value, axis, mask):
     pairs = [(source, source ^ mask) for source in range(lax.axis_size(axis))]
     return lax.ppermute(value, axis, pairs)
 
@@ -21,16 +101,10 @@
     return lax.ppermute(block, axis, route)
 
 
-def fetch_whole(field, bit_list):
-    for bit in bit_list:
-        field = partner(field, "grid", bit)
-    return field
-
-
-def symmetrize(field, fetch, bits_x, bits_y, bits_z):
-    field = 0.5 * (field + jnp.flip(fetch(field, bits_x), 1))
-    field = 0.5 * (field + jnp.flip(fetch(field, bits_y), 2))
-    field = 0.5 * (field + jnp.flip(fetch(field, bits_z), 3))
+def symmetrize(field):
+    field = 0.5 * (field + jnp.flip(partner(field, "grid", 48), 1))
+    field = 0.5 * (field + jnp.flip(partner(field, "grid", 12), 2))
+    field = 0.5 * (field + jnp.flip(partner(field, "grid", 3), 3))
     return field
 
 
@@ -39,20 +113,18 @@
 
 
 def local(orbitals, occupations, density_in, history_in, history_res, screening):
-    n_grid = lax.axis_size("grid")
-    grid_bits = n_grid.bit_length() - 1
     waves = orbitals.astype(jnp.float32)
     partial_value = jnp.sum(occupations[:, None, None, None, None] * waves * waves, 0)
     rho_out = lax.psum(partial_value, "band")
-    rho_sym = symmetrize(rho_out, fetch_whole, list(range(4, grid_bits)), [2, 3], [0, 1])
+    rho_sym = symmetrize(rho_out)
     depth = history_res.shape[0]
     res_hist = history_res.astype(jnp.float32)
-    charges = lax.psum(jnp.stack([jnp.sum(rho_sym), jnp.sum(density_in)]), "grid")
-    scale = charges[1] / charges[0]
+    charges = grid_sum(pack([jnp.sum(rho_sym), jnp.sum(density_in)]), 1)
+    scale = charges[0, 1] / charges[0, 0]
     residual = scale * rho_sym - density_in
     vectors = jnp.concatenate([res_hist, residual[None]], 0).reshape(depth + 1, -1)
     local_gram = jnp.dot(vectors, vectors.T, precision=lax.Precision.HIGHEST)
-    gram = lax.psum(local_gram, "grid")
+    gram = grid_sum(pack([local_gram]), 2).reshape(-1)[: (depth + 1) ** 2].reshape(depth + 1, depth + 1)
     lower = jnp.linalg.cholesky(gram)
     solved = jax.scipy.linalg.cho_solve((lower, True), jnp.ones((depth + 1,), jnp.float32))
     coefficients = solved / jnp.sum(solved)

time: 787 us -> 380 us (0.48)
  blocking collectives: 427 us -> 0 us
  Pallas kernels: 0 us -> 59 us
  waiting for transfers between devices: 209 us -> 165 us
    psum x2 -> x0, blocking collectives: 427 us -> none  [the longest x1 217 us: local(): gram = lax.psum(local_gram, 'grid')]
    pallas_call x0 -> x2, Pallas kernels: none -> 59 us  [grid_sum(): pl.pallas_call(functools.partial(_grid_sum_kernel, n), out_shape=jax.Shap...]
    ppermute x6 -> x3, waiting for transfers between devices: 45.7 us -> 17 us  [partner(): return lax.ppermute(value, axis, pairs)]
    psum x1, waiting for transfers between devices: 154 us -> 139 us  [local(): rho_out = lax.psum(partial_value, 'band')]
    ppermute x24, starting transfers between devices: 76.1 us -> 88.4 us  [shifted(): return lax.ppermute(block, axis, route)]
    ppermute x6 -> x3, starting transfers between devices: 19.4 us -> 14.4 us  [partner(): return lax.ppermute(value, axis, pairs)]
  transfers between devices with their start and end apart: 31 -> 28, of which waited for: 8 -> 6; matrix products, arithmetic and copies ran while one was open for 3% -> 7% of each run, Pallas kernels for 0% -> 16%
where the time goes in v1:
time: 380 us; the launch traced here: 374 us
  waiting for transfers between devices  165 us (43%)
  starting transfers between devices  103 us (27%)
  Pallas kernels  59 us (16%)
  between operations  16.8 us (4%)
  other arithmetic  15.4 us (4%)
  matrix products  11.1 us (3%)
  local copies, waits for them, and re-layouts  4.21 us (1%)
    psum x1, waiting for transfers between devices, local(): rho_out = lax.psum(partial_value, 'band')  139 us
    ppermute x24, starting transfers between devices, shifted(): return lax.ppermute(block, axis, route)  88.4 us
    pallas_call x2, Pallas kernels, grid_sum(): pl.pallas_call(functools.partial(_grid_sum_kernel, n), out_shape=jax.Shap...  59 us
    ppermute x3, waiting for transfers between devices, partner(): return lax.ppermute(value, axis, pairs)  17 us
    ppermute x3, starting transfers between devices, partner(): return lax.ppermute(value, axis, pairs)  14.4 us
    ppermute x24, waiting for transfers between devices, shifted(): return lax.ppermute(block, axis, route)  9.2 us
    dot_general x1, matrix products, local(): local_gram = jnp.dot(vectors, vectors.T, precision=lax.Precision.HIGHEST)  7.7 us
  transfers between devices with their start and end apart: 28, of which 6 were waited for; matrix products, arithmetic and copies ran while one was open for 7% of the time, Pallas kernels for 16%

profile of v1, /device:TPU:1, one launch (start us, length us, event | category | flops | bytes accessed | tf_op | source)
XLA Modules:
  0.0 374.2 jit_solution(14504343117727942798)
XLA Ops:
  7.2 2.1 fusion.4
  10.7 6.4 %collective-permute-start.5 = (f32[16,1,128]{2,1,0:T(1,128)S(1)}, f32[16,1,128]{2,1,0:T(1,128)S(1)}, u32[]{:S(2)}, u32[]{:S(2)}) collective-permute-start(f32[16,1,128]{2,1,0:T(1,128)S(1)} %broadcast.117), channel_id=1, source_target_pairs={{0,32},{8,40},{16,48},{24,56},{32,64},{40,72},{48,80},{56,88},{64,... | collective-permute-start | bytes 24584 | tf_op jit(solution)/shard_map/ppermute | solution.py:101
  17.1 7.9 %collective-permute-start.8 = (f32[16,32,1]{2,1,0:T(8,128)S(1)}, f32[16,32,1]{2,1,0:T(8,128)S(1)}, u32[]{:S(2)}, u32[]{:S(2)}) collective-permute-start(f32[16,32,1]{2,1,0:T(8,128)S(1)} %broadcast.118), channel_id=1, source_target_pairs={{8,0},{16,8},{24,16},{32,24},{40,32},{48,40},{56,48},{64,56},{72,6... | collective-permute-start | bytes 6152 | tf_op jit(solution)/shard_map/ppermute | solution.py:101
  24.9 1.9 collective-permute-start.7
  26.9 138.6 %all-reduce.10.cloned.1.call-done = f32[1,16,32,128]{3,2,1,0:T(8,128)} async-done(((f32[1,16,32,128]{3,2,1,0:T(8,128)}), f32[1,16,32,128]{3,2,1,0:T(8,128)}) %all-reduce.10.cloned.1.call-update) | async-done | bytes 262160 | tf_op jit(solution)/shard_map/psum | solution.py:118
  165.5 4.5 %collective-permute-start = (f32[1,16,32,128]{3,2,1,0:T(8,128)}, f32[1,16,32,128]{3,2,1,0:T(8,128)S(1)}, u32[]{:S(2)}, u32[]{:S(2)}) collective-permute-start(f32[1,16,32,128]{3,2,1,0:T(8,128)} %all-reduce.10.cloned.1.call-done), channel_id=1, source_target_pairs={{0,384},{8,392},{16,400},{24,408},{32,416},{40,424},{48,432},{56,4... | collective-permute-start | bytes 786440 | tf_op jit(solution)/shard_map/ppermute | solution.py:95
  170.0 3.2 copy_convert_fusion
  174.5 1.9 collective-permute-start.3
  177.7 2.6 collective-permute-start.1
  180.4 13.0 %collective-permute-done.1 = f32[1,16,32,128]{3,2,1,0:T(8,128)S(1)} collective-permute-done((f32[1,16,32,128]{3,2,1,0:T(8,128)S(1)}, f32[1,16,32,128]{3,2,1,0:T(8,128)S(1)}, u32[]{:S(2)}, u32[]{:S(2)}) %collective-permute-start.1) | collective-permute-done | bytes 262176 | tf_op jit(solution)/shard_map/ppermute | solution.py:95
  193.6 7.3 %collective-permute-start.2 = (f32[1,16,32,128]{3,2,1,0:T(8,128)S(1)}, f32[1,16,32,128]{3,2,1,0:T(8,128)S(1)}, u32[]{:S(2)}, u32[]{:S(2)}) collective-permute-start(f32[1,16,32,128]{3,2,1,0:T(8,128)S(1)} %add_multiply_fusion), channel_id=1, source_target_pairs={{0,24},{8,16},{16,8},{24,0},{32,56},{40,48},{48,40},{56,32},{64,88... | collective-permute-start | bytes 786440 | tf_op jit(solution)/shard_map/ppermute | solution.py:95
  200.9 4.0 %collective-permute-done.2 = f32[1,16,32,128]{3,2,1,0:T(8,128)S(1)} collective-permute-done((f32[1,16,32,128]{3,2,1,0:T(8,128)S(1)}, f32[1,16,32,128]{3,2,1,0:T(8,128)S(1)}, u32[]{:S(2)}, u32[]{:S(2)}) %collective-permute-start.2) | collective-permute-done | bytes 262176 | tf_op jit(solution)/shard_map/ppermute | solution.py:95
  205.7 1.9 fusion.46.x_ref
  207.6 35.2 %shard_map.77 = f32[8,128]{1,0:T(8,128)} custom-call(f32[8,128]{1,0:T(8,128)} %fusion.46.x_ref), custom_call_target="tpu_custom_call" | custom-call | tf_op jit(solution)/shard_map/pallas_call | solution.py:74
  245.5 7.7 %fusion.3 = f32[9,9]{1,0:T(8,128)S(1)} fusion(f32[1,1,16,32,128]{4,0,3,2,1:T(1,128)S(1)} %bitcast.95, f32[8,1,16,32,128]{4,0,3,2,1:T(8,128)} %copy_convert_fusion), kind=kOutput, calls=%fused_computation.5 | convolution fusion | flops 64290816 | bytes 2359620 | tf_op jit(solution)/shard_map/dot_general | solution.py:126
  253.9 23.8 %shard_map.78 = f32[8,128]{1,0:T(8,128)} custom-call(f32[8,128]{1,0:T(8,128)} %pad_bitcast_fusion.x_ref), custom_call_target="tpu_custom_call" | custom-call | tf_op jit(solution)/shard_map/pallas_call | solution.py:74
  285.9 2.6 collective-permute-start.13
  288.5 1.9 collective-permute-start.14
  291.7 4.9 %collective-permute-start.11 = (f32[16,1,128]{2,1,0:T(1,128)S(1)}, f32[16,1,128]{2,1,0:T(1,128)S(1)}, u32[]{:S(2)}, u32[]{:S(2)}) collective-permute-start(f32[16,1,128]{2,1,0:T(1,128)S(1)} %get-tuple-element.20), channel_id=1, source_target_pairs={{0,32},{8,40},{16,48},{24,56},{32,64},{40,72},{48,80},{56,88},{64,... | collective-permute-start | bytes 24584 | tf_op jit(solution)/shard_map/ppermute | solution.py:101
  296.6 5.0 %collective-permute-start.9 = (f32[1,32,128]{2,1,0:T(8,128)S(1)}, f32[1,32,128]{2,1,0:T(8,128)S(1)}, u32[]{:S(2)}, u32[]{:S(2)}) collective-permute-start(f32[1,32,128]{2,1,0:T(8,128)S(1)} %get-tuple-element.18), channel_id=1, source_target_pairs={{0,128},{8,136},{16,144},{24,152},{32,160},{40,168},{48,176},{56,1... | collective-permute-start | bytes 49160 | tf_op jit(solution)/shard_map/ppermute | solution.py:101
  304.3 3.0 collective-permute-done.10
  307.8 5.4 %collective-permute-start.19 = (f32[16,32,1]{2,1,0:T(8,128)S(1)}, f32[16,32,1]{2,1,0:T(8,128)S(1)}, u32[]{:S(2)}, u32[]{:S(2)}) collective-permute-start(f32[16,32,1]{2,1,0:T(8,128)S(1)} %get-tuple-element.16), channel_id=1, source_target_pairs={{0,8},{8,16},{16,24},{24,32},{32,40},{40,48},{48,56},{56,64},{64,7... | collective-permute-start | bytes 6152 | tf_op jit(solution)/shard_map/ppermute | solution.py:101
  313.2 6.4 %collective-permute-start.20 = (f32[16,32,1]{2,1,0:T(8,128)S(1)}, f32[16,32,1]{2,1,0:T(8,128)S(1)}, u32[]{:S(2)}, u32[]{:S(2)}) collective-permute-start(f32[16,32,1]{2,1,0:T(8,128)S(1)} %get-tuple-element.17), channel_id=1, source_target_pairs={{8,0},{16,8},{24,16},{32,24},{40,32},{48,40},{56,48},{64,56},{72,6... | collective-permute-start | bytes 6152 | tf_op jit(solution)/shard_map/ppermute | solution.py:101
  320.9 4.9 %collective-permute-start.17 = (f32[16,1,128]{2,1,0:T(1,128)S(1)}, f32[16,1,128]{2,1,0:T(1,128)S(1)}, u32[]{:S(2)}, u32[]{:S(2)}) collective-permute-start(f32[16,1,128]{2,1,0:T(1,128)S(1)} %get-tuple-element.14), channel_id=1, source_target_pairs={{0,32},{8,40},{16,48},{24,56},{32,64},{40,72},{48,80},{56,88},{64,... | collective-permute-start | bytes 24584 | tf_op jit(solution)/shard_map/ppermute | solution.py:101
  325.8 6.1 %collective-permute-start.15 = (f32[1,32,128]{2,1,0:T(8,128)S(1)}, f32[1,32,128]{2,1,0:T(8,128)S(1)}, u32[]{:S(2)}, u32[]{:S(2)}) collective-permute-start(f32[1,32,128]{2,1,0:T(8,128)S(1)} %get-tuple-element.12), channel_id=1, source_target_pairs={{0,128},{8,136},{16,144},{24,152},{32,160},{40,168},{48,176},{56,1... | collective-permute-start | bytes 49160 | tf_op jit(solution)/shard_map/ppermute | solution.py:101
  333.4 3.0 collective-permute-done.16
  336.9 3.1 collective-permute-start.25
  340.0 8.2 %collective-permute-start.26 = (f32[16,32,1]{2,1,0:T(8,128)S(1)}, f32[16,32,1]{2,1,0:T(8,128)S(1)}, u32[]{:S(2)}, u32[]{:S(2)}) collective-permute-start(f32[16,32,1]{2,1,0:T(8,128)S(1)} %get-tuple-element.11), channel_id=1, source_target_pairs={{8,0},{16,8},{24,16},{32,24},{40,32},{48,40},{56,48},{64,56},{72,6... | collective-permute-start | bytes 6152 | tf_op jit(solution)/shard_map/ppermute | solution.py:101
  349.6 4.9 %collective-permute-start.23 = (f32[16,1,128]{2,1,0:T(1,128)S(1)}, f32[16,1,128]{2,1,0:T(1,128)S(1)}, u32[]{:S(2)}, u32[]{:S(2)}) collective-permute-start(f32[16,1,128]{2,1,0:T(1,128)S(1)} %get-tuple-element.8), channel_id=1, source_target_pairs={{0,32},{8,40},{16,48},{24,56},{32,64},{40,72},{48,80},{56,88},{64,... | collective-permute-start | bytes 24584 | tf_op jit(solution)/shard_map/ppermute | solution.py:101
  354.5 6.7 %collective-permute-start.21 = (f32[1,32,128]{2,1,0:T(8,128)S(1)}, f32[1,32,128]{2,1,0:T(8,128)S(1)}, u32[]{:S(2)}, u32[]{:S(2)}) collective-permute-start(f32[1,32,128]{2,1,0:T(8,128)S(1)} %get-tuple-element.6), channel_id=1, source_target_pairs={{0,128},{8,136},{16,144},{24,152},{32,160},{40,168},{48,176},{56,1... | collective-permute-start | bytes 49160 | tf_op jit(solution)/shard_map/ppermute | solution.py:101
  362.6 3.0 collective-permute-done.22
  365.7 1.7 fusion.23
  (102 shorter events, 24.6 us)
Async XLA Ops:
  7.2 294.4 %copy-start = (bf16[8,1,16,32,128]{4,3,2,1,0:T(8,128)(2,1)S(1)}, bf16[8,1,16,32,128]{4,3,2,1,0:T(8,128)(2,1)}, u32[]{:S(2)}) copy-start(bf16[8,1,16,32,128]{4,3,2,1,0:T(8,128)(2,1)} %param.9) | copy-start | bytes 3145732
  7.2 166.0 %copy-start.2 = (f32[1,16,32,128]{3,2,1,0:T(8,128)S(1)}, f32[1,16,32,128]{3,2,1,0:T(8,128)}, u32[]{:S(2)}) copy-start(f32[1,16,32,128]{3,2,1,0:T(8,128)} %param.8) | copy-start | bytes 786436
  7.2 158.3 %all-reduce.10.cloned.1.call-start = ((), (), s32[]{:S(2)}) async-start(), calls=%async_computation | async-start | bytes 524288 | tf_op jit(solution)/shard_map/psum | solution.py:118
  9.4 171.1 %collective-permute-start.6 = (f32[16,1,128]{2,1,0:T(1,128)S(1)}, f32[16,1,128]{2,1,0:T(1,128)S(1)}, u32[]{:S(2)}, u32[]{:S(2)}) collective-permute-start(f32[16,1,128]{2,1,0:T(1,128)S(1)} %broadcast.117), channel_id=1, source_target_pairs={{32,0},{40,8},{48,16},{56,24},{64,32},{72,40},{80,48},{88,56},{96,... | collective-permute-start | bytes 24584 | tf_op jit(solution)/shard_map/ppermute | solution.py:101
  10.7 190.2 %collective-permute-start.5 = (f32[16,1,128]{2,1,0:T(1,128)S(1)}, f32[16,1,128]{2,1,0:T(1,128)S(1)}, u32[]{:S(2)}, u32[]{:S(2)}) collective-permute-start(f32[16,1,128]{2,1,0:T(1,128)S(1)} %broadcast.117), channel_id=1, source_target_pairs={{0,32},{8,40},{16,48},{24,56},{32,64},{40,72},{48,80},{56,88},{64,... | collective-permute-start | bytes 24584 | tf_op jit(solution)/shard_map/ppermute | solution.py:101
  17.1 157.4 %collective-permute-start.8 = (f32[16,32,1]{2,1,0:T(8,128)S(1)}, f32[16,32,1]{2,1,0:T(8,128)S(1)}, u32[]{:S(2)}, u32[]{:S(2)}) collective-permute-start(f32[16,32,1]{2,1,0:T(8,128)S(1)} %broadcast.118), channel_id=1, source_target_pairs={{8,0},{16,8},{24,16},{32,24},{40,32},{48,40},{56,48},{64,56},{72,6... | collective-permute-start | bytes 6152 | tf_op jit(solution)/shard_map/ppermute | solution.py:101
  24.9 152.8 %collective-permute-start.7 = (f32[16,32,1]{2,1,0:T(8,128)S(1)}, f32[16,32,1]{2,1,0:T(8,128)S(1)}, u32[]{:S(2)}, u32[]{:S(2)}) collective-permute-start(f32[16,32,1]{2,1,0:T(8,128)S(1)} %broadcast.118), channel_id=1, source_target_pairs={{0,8},{8,16},{16,24},{24,32},{32,40},{40,48},{48,56},{56,64},{64,7... | collective-permute-start | bytes 6152 | tf_op jit(solution)/shard_map/ppermute | solution.py:101
  165.5 10.9 %collective-permute-start = (f32[1,16,32,128]{3,2,1,0:T(8,128)}, f32[1,16,32,128]{3,2,1,0:T(8,128)S(1)}, u32[]{:S(2)}, u32[]{:S(2)}) collective-permute-start(f32[1,16,32,128]{3,2,1,0:T(8,128)} %all-reduce.10.cloned.1.call-done), channel_id=1, source_target_pairs={{0,384},{8,392},{16,400},{24,408},{32,416},{40,424},{48,432},{56,4... | collective-permute-start | bytes 786440 | tf_op jit(solution)/shard_map/ppermute | solution.py:95
  174.5 26.4 %collective-permute-start.3 = (f32[1,32,128]{2,1,0:T(8,128)S(1)}, f32[1,32,128]{2,1,0:T(8,128)S(1)}, u32[]{:S(2)}, u32[]{:S(2)}) collective-permute-start(f32[1,32,128]{2,1,0:T(8,128)S(1)} %broadcast.116), channel_id=1, source_target_pairs={{0,128},{8,136},{16,144},{24,152},{32,160},{40,168},{48,176},{56,1... | collective-permute-start | bytes 49160 | tf_op jit(solution)/shard_map/ppermute | solution.py:101
  176.4 108.5 %collective-permute-start.4 = (f32[1,32,128]{2,1,0:T(8,128)S(1)}, f32[1,32,128]{2,1,0:T(8,128)S(1)}, u32[]{:S(2)}, u32[]{:S(2)}) collective-permute-start(f32[1,32,128]{2,1,0:T(8,128)S(1)} %broadcast.116), channel_id=1, source_target_pairs={{128,0},{136,8},{144,16},{152,24},{160,32},{168,40},{176,48},{184,... | collective-permute-start | bytes 49160 | tf_op jit(solution)/shard_map/ppermute | solution.py:101
  177.7 15.7 %collective-permute-start.1 = (f32[1,16,32,128]{3,2,1,0:T(8,128)S(1)}, f32[1,16,32,128]{3,2,1,0:T(8,128)S(1)}, u32[]{:S(2)}, u32[]{:S(2)}) collective-permute-start(f32[1,16,32,128]{3,2,1,0:T(8,128)S(1)} %add_multiply_fusion.1), channel_id=1, source_target_pairs={{0,96},{8,104},{16,112},{24,120},{32,64},{40,72},{48,80},{56,88},{... | collective-permute-start | bytes 786440 | tf_op jit(solution)/shard_map/ppermute | solution.py:95
  193.6 11.3 %collective-permute-start.2 = (f32[1,16,32,128]{3,2,1,0:T(8,128)S(1)}, f32[1,16,32,128]{3,2,1,0:T(8,128)S(1)}, u32[]{:S(2)}, u32[]{:S(2)}) collective-permute-start(f32[1,16,32,128]{3,2,1,0:T(8,128)S(1)} %add_multiply_fusion), channel_id=1, source_target_pairs={{0,24},{8,16},{16,8},{24,0},{32,56},{40,48},{48,40},{56,32},{64,88... | collective-permute-start | bytes 786440 | tf_op jit(solution)/shard_map/ppermute | solution.py:95
  245.5 39.4 %copy-start.3 = (f32[1,16,32,128]{3,2,1,0:T(8,128)}, f32[1,16,32,128]{3,2,1,0:T(8,128)S(1)}, u32[]{:S(2)}) copy-start(f32[1,16,32,128]{3,2,1,0:T(8,128)S(1)} %multiply_subtract_fusion) | copy-start | bytes 786436
  245.5 37.5 %copy-start.1 = (bf16[8,1,16,32,128]{4,3,2,1,0:T(8,128)(2,1)S(1)}, bf16[8,1,16,32,128]{4,3,2,1,0:T(8,128)(2,1)}, u32[]{:S(2)}) copy-start(bf16[8,1,16,32,128]{4,3,2,1,0:T(8,128)(2,1)} %param.10) | copy-start | bytes 3145732
  285.9 17.0 %collective-permute-start.13 = (f32[16,32,1]{2,1,0:T(8,128)S(1)}, f32[16,32,1]{2,1,0:T(8,128)S(1)}, u32[]{:S(2)}, u32[]{:S(2)}) collective-permute-start(f32[16,32,1]{2,1,0:T(8,128)S(1)} %get-tuple-element.22), channel_id=1, source_target_pairs={{0,8},{8,16},{16,24},{24,32},{32,40},{40,48},{48,56},{56,64},{64,7... | collective-permute-start | bytes 6152 | tf_op jit(solution)/shard_map/ppermute | solution.py:101
  288.5 15.7 %collective-permute-start.14 = (f32[16,32,1]{2,1,0:T(8,128)S(1)}, f32[16,32,1]{2,1,0:T(8,128)S(1)}, u32[]{:S(2)}, u32[]{:S(2)}) collective-permute-start(f32[16,32,1]{2,1,0:T(8,128)S(1)} %get-tuple-element.23), channel_id=1, source_target_pairs={{8,0},{16,8},{24,16},{32,24},{40,32},{48,40},{56,48},{64,56},{72,6... | collective-permute-start | bytes 6152 | tf_op jit(solution)/shard_map/ppermute | solution.py:101
  290.4 13.9 %collective-permute-start.12 = (f32[16,1,128]{2,1,0:T(1,128)S(1)}, f32[16,1,128]{2,1,0:T(1,128)S(1)}, u32[]{:S(2)}, u32[]{:S(2)}) collective-permute-start(f32[16,1,128]{2,1,0:T(1,128)S(1)} %get-tuple-element.21), channel_id=1, source_target_pairs={{32,0},{40,8},{48,16},{56,24},{64,32},{72,40},{80,48},{88,56},{96,... | collective-permute-start | bytes 24584 | tf_op jit(solution)/shard_map/ppermute | solution.py:101
  291.7 12.6 %collective-permute-start.11 = (f32[16,1,128]{2,1,0:T(1,128)S(1)}, f32[16,1,128]{2,1,0:T(1,128)S(1)}, u32[]{:S(2)}, u32[]{:S(2)}) collective-permute-start(f32[16,1,128]{2,1,0:T(1,128)S(1)} %get-tuple-element.20), channel_id=1, source_target_pairs={{0,32},{8,40},{16,48},{24,56},{32,64},{40,72},{48,80},{56,88},{64,... | collective-permute-start | bytes 24584 | tf_op jit(solution)/shard_map/ppermute | solution.py:101
  296.6 7.7 %collective-permute-start.9 = (f32[1,32,128]{2,1,0:T(8,128)S(1)}, f32[1,32,128]{2,1,0:T(8,128)S(1)}, u32[]{:S(2)}, u32[]{:S(2)}) collective-permute-start(f32[1,32,128]{2,1,0:T(8,128)S(1)} %get-tuple-element.18), channel_id=1, source_target_pairs={{0,128},{8,136},{16,144},{24,152},{32,160},{40,168},{48,176},{56,1... | collective-permute-start | bytes 49160 | tf_op jit(solution)/shard_map/ppermute | solution.py:101
  302.9 4.5 %collective-permute-start.10 = (f32[1,32,128]{2,1,0:T(8,128)S(1)}, f32[1,32,128]{2,1,0:T(8,128)S(1)}, u32[]{:S(2)}, u32[]{:S(2)}) collective-permute-start(f32[1,32,128]{2,1,0:T(8,128)S(1)} %get-tuple-element.19), channel_id=1, source_target_pairs={{128,0},{136,8},{144,16},{152,24},{160,32},{168,40},{176,48},{184,... | collective-permute-start | bytes 49160 | tf_op jit(solution)/shard_map/ppermute | solution.py:101
  307.8 24.1 %collective-permute-start.19 = (f32[16,32,1]{2,1,0:T(8,128)S(1)}, f32[16,32,1]{2,1,0:T(8,128)S(1)}, u32[]{:S(2)}, u32[]{:S(2)}) collective-permute-start(f32[16,32,1]{2,1,0:T(8,128)S(1)} %get-tuple-element.16), channel_id=1, source_target_pairs={{0,8},{8,16},{16,24},{24,32},{32,40},{40,48},{48,56},{56,64},{64,7... | collective-permute-start | bytes 6152 | tf_op jit(solution)/shard_map/ppermute | solution.py:101
  313.2 20.1 %collective-permute-start.20 = (f32[16,32,1]{2,1,0:T(8,128)S(1)}, f32[16,32,1]{2,1,0:T(8,128)S(1)}, u32[]{:S(2)}, u32[]{:S(2)}) collective-permute-start(f32[16,32,1]{2,1,0:T(8,128)S(1)} %get-tuple-element.17), channel_id=1, source_target_pairs={{8,0},{16,8},{24,16},{32,24},{40,32},{48,40},{56,48},{64,56},{72,6... | collective-permute-start | bytes 6152 | tf_op jit(solution)/shard_map/ppermute | solution.py:101
  319.6 13.7 %collective-permute-start.18 = (f32[16,1,128]{2,1,0:T(1,128)S(1)}, f32[16,1,128]{2,1,0:T(1,128)S(1)}, u32[]{:S(2)}, u32[]{:S(2)}) collective-permute-start(f32[16,1,128]{2,1,0:T(1,128)S(1)} %get-tuple-element.15), channel_id=1, source_target_pairs={{32,0},{40,8},{48,16},{56,24},{64,32},{72,40},{80,48},{88,56},{96,... | collective-permute-start | bytes 24584 | tf_op jit(solution)/shard_map/ppermute | solution.py:101
  320.9 12.4 %collective-permute-start.17 = (f32[16,1,128]{2,1,0:T(1,128)S(1)}, f32[16,1,128]{2,1,0:T(1,128)S(1)}, u32[]{:S(2)}, u32[]{:S(2)}) collective-permute-start(f32[16,1,128]{2,1,0:T(1,128)S(1)} %get-tuple-element.14), channel_id=1, source_target_pairs={{0,32},{8,40},{16,48},{24,56},{32,64},{40,72},{48,80},{56,88},{64,... | collective-permute-start | bytes 24584 | tf_op jit(solution)/shard_map/ppermute | solution.py:101
  325.8 7.6 %collective-permute-start.15 = (f32[1,32,128]{2,1,0:T(8,128)S(1)}, f32[1,32,128]{2,1,0:T(8,128)S(1)}, u32[]{:S(2)}, u32[]{:S(2)}) collective-permute-start(f32[1,32,128]{2,1,0:T(8,128)S(1)} %get-tuple-element.12), channel_id=1, source_target_pairs={{0,128},{8,136},{16,144},{24,152},{32,160},{40,168},{48,176},{56,1... | collective-permute-start | bytes 49160 | tf_op jit(solution)/shard_map/ppermute | solution.py:101
  332.0 4.5 %collective-permute-start.16 = (f32[1,32,128]{2,1,0:T(8,128)S(1)}, f32[1,32,128]{2,1,0:T(8,128)S(1)}, u32[]{:S(2)}, u32[]{:S(2)}) collective-permute-start(f32[1,32,128]{2,1,0:T(8,128)S(1)} %get-tuple-element.13), channel_id=1, source_target_pairs={{128,0},{136,8},{144,16},{152,24},{160,32},{168,40},{176,48},{184,... | collective-permute-start | bytes 49160 | tf_op jit(solution)/shard_map/ppermute | solution.py:101
  336.9 24.3 %collective-permute-start.25 = (f32[16,32,1]{2,1,0:T(8,128)S(1)}, f32[16,32,1]{2,1,0:T(8,128)S(1)}, u32[]{:S(2)}, u32[]{:S(2)}) collective-permute-start(f32[16,32,1]{2,1,0:T(8,128)S(1)} %get-tuple-element.10), channel_id=1, source_target_pairs={{0,8},{8,16},{16,24},{24,32},{32,40},{40,48},{48,56},{56,64},{64,7... | collective-permute-start | bytes 6152 | tf_op jit(solution)/shard_map/ppermute | solution.py:101
  340.0 22.5 %collective-permute-start.26 = (f32[16,32,1]{2,1,0:T(8,128)S(1)}, f32[16,32,1]{2,1,0:T(8,128)S(1)}, u32[]{:S(2)}, u32[]{:S(2)}) collective-permute-start(f32[16,32,1]{2,1,0:T(8,128)S(1)} %get-tuple-element.11), channel_id=1, source_target_pairs={{8,0},{16,8},{24,16},{32,24},{40,32},{48,40},{56,48},{64,56},{72,6... | collective-permute-start | bytes 6152 | tf_op jit(solution)/shard_map/ppermute | solution.py:101
  348.3 14.3 %collective-permute-start.24 = (f32[16,1,128]{2,1,0:T(1,128)S(1)}, f32[16,1,128]{2,1,0:T(1,128)S(1)}, u32[]{:S(2)}, u32[]{:S(2)}) collective-permute-start(f32[16,1,128]{2,1,0:T(1,128)S(1)} %get-tuple-element.9), channel_id=1, source_target_pairs={{32,0},{40,8},{48,16},{56,24},{64,32},{72,40},{80,48},{88,56},{96,... | collective-permute-start | bytes 24584 | tf_op jit(solution)/shard_map/ppermute | solution.py:101
  349.6 13.0 %collective-permute-start.23 = (f32[16,1,128]{2,1,0:T(1,128)S(1)}, f32[16,1,128]{2,1,0:T(1,128)S(1)}, u32[]{:S(2)}, u32[]{:S(2)}) collective-permute-start(f32[16,1,128]{2,1,0:T(1,128)S(1)} %get-tuple-element.8), channel_id=1, source_target_pairs={{0,32},{8,40},{16,48},{24,56},{32,64},{40,72},{48,80},{56,88},{64,... | collective-permute-start | bytes 24584 | tf_op jit(solution)/shard_map/ppermute | solution.py:101
  354.5 8.1 %collective-permute-start.21 = (f32[1,32,128]{2,1,0:T(8,128)S(1)}, f32[1,32,128]{2,1,0:T(8,128)S(1)}, u32[]{:S(2)}, u32[]{:S(2)}) collective-permute-start(f32[1,32,128]{2,1,0:T(8,128)S(1)} %get-tuple-element.6), channel_id=1, source_target_pairs={{0,128},{8,136},{16,144},{24,152},{32,160},{40,168},{48,176},{56,1... | collective-permute-start | bytes 49160 | tf_op jit(solution)/shard_map/ppermute | solution.py:101
  361.2 4.5 %collective-permute-start.22 = (f32[1,32,128]{2,1,0:T(8,128)S(1)}, f32[1,32,128]{2,1,0:T(8,128)S(1)}, u32[]{:S(2)}, u32[]{:S(2)}) collective-permute-start(f32[1,32,128]{2,1,0:T(8,128)S(1)} %get-tuple-element.7), channel_id=1, source_target_pairs={{128,0},{136,8},{144,16},{152,24},{160,32},{168,40},{176,48},{184,... | collective-permute-start | bytes 49160 | tf_op jit(solution)/shard_map/ppermute | solution.py:101
  (1 other events, 12.2 us)
Sparse Core Ops, SparseCore 0:
  11.5 153.9 all-reduce.9

commit v2 on v1

--- a/solution.py
+++ b/solution.py
@@ -85,6 +85,85 @@
     )(vec)
 
 
+def _band_sum_kernel(x_ref, o_ref, q_in, q_sum, e_in, t_quarter, full, s1, r1, s2, r2, s3, r3, s4, r4):
+    g = lax.axis_index("grid")
+    b = lax.axis_index("band")
+    zhi = b // 4
+    x = b % 4
+    other = (1 - zhi) * 4 + x
+    barrier = pltpu.get_barrier_semaphore()
+    for k in range(1, 4):
+        pl.semaphore_signal(barrier, inc=1, device_id=(g, zhi * 4 + lax.rem(x + k, 4)), device_id_type=MESH)
+    pl.semaphore_signal(barrier, inc=1, device_id=(g, other), device_id_type=MESH)
+    pl.semaphore_wait(barrier, 4)
+
+    def remote(src, dst, ssem, rsem, peer):
+        return pltpu.make_async_remote_copy(
+            src_ref=src, dst_ref=dst, send_sem=ssem, recv_sem=rsem, device_id=(g, peer), device_id_type=MESH
+        )
+
+    q = x_ref.shape[0] // 4
+    e = q // 2
+    out1 = []
+    for k in range(1, 4):
+        px = lax.rem(x + k, 4)
+        c = remote(x_ref.at[pl.ds(px * q, q)], q_in.at[x], s1.at[k], r1.at[x], zhi * 4 + px)
+        c.start()
+        out1.append(c)
+    q_in[x] = x_ref[pl.ds(x * q, q)]
+    for c in out1:
+        c.wait_send()
+    for k in range(1, 4):
+        sx = lax.rem(x + k, 4)
+        remote(x_ref.at[pl.ds(0, q)], q_in.at[sx], s1.at[k], r1.at[sx], zhi * 4 + sx).wait_recv()
+    q_sum[...] = ((q_in[0] + q_in[1]) + q_in[2]) + q_in[3]
+    c2 = remote(q_sum.at[pl.ds((1 - zhi) * e, e)], e_in.at[zhi], s2, r2, other)
+    c2.start()
+    e_in[zhi] = q_sum[pl.ds(zhi * e, e)]
+    c2.wait_send()
+    remote(q_sum.at[pl.ds(0, e)], e_in.at[1 - zhi], s2, r2, other).wait_recv()
+    t_quarter[pl.ds(zhi * e, e)] = e_in[0] + e_in[1]
+    c3 = remote(t_quarter.at[pl.ds(zhi * e, e)], t_quarter.at[pl.ds(zhi * e, e)], s3, r3, other)
+    c3.start()
+    c3.wait_send()
+    remote(t_quarter.at[pl.ds(0, e)], t_quarter.at[pl.ds((1 - zhi) * e, e)], s3, r3, other).wait_recv()
+    out4 = []
+    for k in range(1, 4):
+        px = lax.rem(x + k, 4)
+        c = remote(t_quarter, full.at[pl.ds(x * q, q)], s4.at[k], r4.at[x], zhi * 4 + px)
+        c.start()
+        out4.append(c)
+    full[pl.ds(x * q, q)] = t_quarter[...]
+    for c in out4:
+        c.wait_send()
+    for k in range(1, 4):
+        sx = lax.rem(x + k, 4)
+        remote(t_quarter, full.at[pl.ds(sx * q, q)], s4.at[k], r4.at[sx], zhi * 4 + sx).wait_recv()
+    o_ref[...] = full[...]
+
+
+def band_sum(part):
+    rows = part.shape[0]
+    q, e = rows // 4, rows // 8
+    rest = part.shape[1:]
+    dma = pltpu.SemaphoreType.DMA
+    return pl.pallas_call(
+        _band_sum_kernel,
+        out_shape=jax.ShapeDtypeStruct(part.shape, jnp.float32),
+        in_specs=[pl.BlockSpec(memory_space=pltpu.VMEM)],
+        out_specs=pl.BlockSpec(memory_space=pltpu.VMEM),
+        scratch_shapes=[
+            pltpu.VMEM((4, q) + rest, jnp.float32),
+            pltpu.VMEM((q,) + rest, jnp.float32),
+            pltpu.VMEM((2, e) + rest, jnp.float32),
+            pltpu.VMEM((q,) + rest, jnp.float32),
+            pltpu.VMEM(part.shape, jnp.float32),
+            dma((4,)), dma((4,)), dma(()), dma(()), dma(()), dma(()), dma((4,)), dma((4,)),
+        ],
+        compiler_params=pltpu.CompilerParams(collective_id=3, has_side_effects=True),
+    )(part)
+
+
 def pack(values):
     flat = jnp.concatenate([v.reshape(-1) for v in values])
     return jnp.pad(flat, (0, 1024 - flat.shape[0])).reshape(8, 128)
@@ -115,7 +194,7 @@
 def local(orbitals, occupations, density_in, history_in, history_res, screening):
     waves = orbitals.astype(jnp.float32)
     partial_value = jnp.sum(occupations[:, None, None, None, None] * waves * waves, 0)
-    rho_out = lax.psum(partial_value, "band")
+    rho_out = band_sum(partial_value[0])[None]
     rho_sym = symmetrize(rho_out)
     depth = history_res.shape[0]
     res_hist = history_res.astype(jnp.float32)

time: 380 us -> 269 us (0.71)
  the two profiles are of different devices: /device:TPU:1 before, /device:TPU:4 now
where the time goes in v2:
time: 269 us; the launch traced here: 268 us
  starting transfers between devices  106 us (39%)
  Pallas kernels  97.3 us (36%)
  waiting for transfers between devices  29.3 us (11%)
  other arithmetic  16.1 us (6%)
  matrix products  11.2 us (4%)
  local copies, waits for them, and re-layouts  4.94 us (2%)
  between operations  3.32 us (1%)
    ppermute x24, starting transfers between devices, shifted(): return lax.ppermute(block, axis, route)  87.6 us
    pallas_call x2, Pallas kernels, grid_sum(): pl.pallas_call(functools.partial(_grid_sum_kernel, n), out_shape=jax.Shap...  56.4 us
    pallas_call x1, Pallas kernels, band_sum(): pl.pallas_call(_band_sum_kernel, out_shape=jax.ShapeDtypeStruct(part.shap...  40.9 us
    ppermute x3, starting transfers between devices, partner(): return lax.ppermute(value, axis, pairs)  18 us
    ppermute x3, waiting for transfers between devices, partner(): return lax.ppermute(value, axis, pairs)  16.7 us
    ppermute x24, waiting for transfers between devices, shifted(): return lax.ppermute(block, axis, route)  12.6 us
    dot_general x1, matrix products, local(): local_gram = jnp.dot(vectors, vectors.T, precision=lax.Precision.HIGHEST)  7.69 us
  transfers between devices with their start and end apart: 27, of which 5 were waited for; matrix products, arithmetic and copies ran while one was open for 11% of the time, Pallas kernels for 36%

profile of v2, /device:TPU:4, one launch (start us, length us, event | category | flops | bytes accessed | tf_op | source)
XLA Modules:
  0.0 267.8 jit_solution(12830672928940828153)
XLA Ops:
  0.7 1.4 collective-permute-start.6
  2.1 5.8 %collective-permute-start.5 = (f32[16,1,128]{2,1,0:T(1,128)S(1)}, f32[16,1,128]{2,1,0:T(1,128)S(1)}, u32[]{:S(2)}, u32[]{:S(2)}) collective-permute-start(f32[16,1,128]{2,1,0:T(1,128)S(1)} %broadcast.117), channel_id=1, source_target_pairs={{0,32},{8,40},{16,48},{24,56},{32,64},{40,72},{48,80},{56,88},{64,... | collective-permute-start | bytes 24584 | tf_op jit(solution)/shard_map/ppermute | solution.py:180
  8.6 1.4 collective-permute-start.8
  10.1 3.7 %collective-permute-start.7 = (f32[16,32,1]{2,1,0:T(8,128)}, f32[16,32,1]{2,1,0:T(8,128)}, u32[]{:S(2)}, u32[]{:S(2)}) collective-permute-start(f32[16,32,1]{2,1,0:T(8,128)} %broadcast.118), channel_id=1, source_target_pairs={{0,8},{8,16},{16,24},{24,32},{32,40},{40,48},{48,56},{56,64},{64,7... | collective-permute-start | bytes 6152 | tf_op jit(solution)/shard_map/ppermute | solution.py:180
  13.8 2.0 fusion.4.x_ref
  15.8 40.9 %shard_map.77 = f32[16,32,128]{2,1,0:T(8,128)} custom-call(f32[16,32,128]{2,1,0:T(8,128)} %fusion.4.x_ref), custom_call_target="tpu_custom_call" | custom-call | tf_op jit(solution)/shard_map/pallas_call | solution.py:150
  56.7 11.4 %collective-permute-start = (f32[1,16,32,128]{3,2,1,0:T(8,128)}, f32[1,16,32,128]{3,2,1,0:T(8,128)S(1)}, u32[]{:S(2)}, u32[]{:S(2)}) collective-permute-start(f32[1,16,32,128]{3,2,1,0:T(8,128)} %bitcast.95), channel_id=1, source_target_pairs={{0,384},{8,392},{16,400},{24,408},{32,416},{40,424},{48,432},{56,4... | collective-permute-start | bytes 786440 | tf_op jit(solution)/shard_map/ppermute | solution.py:174
  68.2 2.0 copy_convert_fusion
  71.5 1.7 collective-permute-start.3
  74.7 4.7 %collective-permute-start.1 = (f32[1,16,32,128]{3,2,1,0:T(8,128)S(1)}, f32[1,16,32,128]{3,2,1,0:T(8,128)S(1)}, u32[]{:S(2)}, u32[]{:S(2)}) collective-permute-start(f32[1,16,32,128]{3,2,1,0:T(8,128)S(1)} %add_multiply_fusion.1), channel_id=1, source_target_pairs={{0,96},{8,104},{16,112},{24,120},{32,64},{40,72},{48,80},{56,88},{... | collective-permute-start | bytes 786440 | tf_op jit(solution)/shard_map/ppermute | solution.py:174
  79.4 1.7 broadcast_multiply_fusion.7
  81.1 11.0 %collective-permute-done.1 = f32[1,16,32,128]{3,2,1,0:T(8,128)S(1)} collective-permute-done((f32[1,16,32,128]{3,2,1,0:T(8,128)S(1)}, f32[1,16,32,128]{3,2,1,0:T(8,128)S(1)}, u32[]{:S(2)}, u32[]{:S(2)}) %collective-permute-start.1) | collective-permute-done | bytes 262176 | tf_op jit(solution)/shard_map/ppermute | solution.py:174
  92.2 1.9 collective-permute-start.2
  94.2 5.7 %collective-permute-done.2 = f32[1,16,32,128]{3,2,1,0:T(8,128)S(1)} collective-permute-done((f32[1,16,32,128]{3,2,1,0:T(8,128)S(1)}, f32[1,16,32,128]{3,2,1,0:T(8,128)S(1)}, u32[]{:S(2)}, u32[]{:S(2)}) %collective-permute-start.2) | collective-permute-done | bytes 262176 | tf_op jit(solution)/shard_map/ppermute | solution.py:174
  100.7 2.0 fusion.46.x_ref
  102.7 32.3 %shard_map.78 = f32[8,128]{1,0:T(8,128)} custom-call(f32[8,128]{1,0:T(8,128)} %fusion.46.x_ref), custom_call_target="tpu_custom_call" | custom-call | tf_op jit(solution)/shard_map/pallas_call | solution.py:74
  134.9 1.3 fusion.63
  137.6 7.7 %fusion.3 = f32[9,9]{1,0:T(8,128)S(1)} fusion(f32[1,1,16,32,128]{4,0,3,2,1:T(1,128)S(1)} %bitcast.98, f32[8,1,16,32,128]{4,0,3,2,1:T(8,128)} %copy_convert_fusion), kind=kOutput, calls=%fused_computation.5 | convolution fusion | flops 64290816 | bytes 2359620 | tf_op jit(solution)/shard_map/dot_general | solution.py:205
  146.0 24.1 %shard_map.79 = f32[8,128]{1,0:T(8,128)} custom-call(f32[8,128]{1,0:T(8,128)} %pad_bitcast_fusion.x_ref), custom_call_target="tpu_custom_call" | custom-call | tf_op jit(solution)/shard_map/pallas_call | solution.py:74
  178.6 2.0 collective-permute-start.13
  183.3 5.5 %collective-permute-start.11 = (f32[16,1,128]{2,1,0:T(1,128)S(1)}, f32[16,1,128]{2,1,0:T(1,128)S(1)}, u32[]{:S(2)}, u32[]{:S(2)}) collective-permute-start(f32[16,1,128]{2,1,0:T(1,128)S(1)} %get-tuple-element.20), channel_id=1, source_target_pairs={{0,32},{8,40},{16,48},{24,56},{32,64},{40,72},{48,80},{56,88},{64,... | collective-permute-start | bytes 24584 | tf_op jit(solution)/shard_map/ppermute | solution.py:180
  188.8 12.5 %collective-permute-start.9 = (f32[1,32,128]{2,1,0:T(8,128)S(1)}, f32[1,32,128]{2,1,0:T(8,128)S(1)}, u32[]{:S(2)}, u32[]{:S(2)}) collective-permute-start(f32[1,32,128]{2,1,0:T(8,128)S(1)} %get-tuple-element.18), channel_id=1, source_target_pairs={{0,128},{8,136},{16,144},{24,152},{32,160},{40,168},{48,176},{56,1... | collective-permute-start | bytes 49160 | tf_op jit(solution)/shard_map/ppermute | solution.py:180
  204.1 4.2 %collective-permute-done.10 = f32[1,32,128]{2,1,0:T(8,128)S(1)} collective-permute-done((f32[1,32,128]{2,1,0:T(8,128)S(1)}, f32[1,32,128]{2,1,0:T(8,128)S(1)}, u32[]{:S(2)}, u32[]{:S(2)}) %collective-permute-start.10) | collective-permute-done | bytes 16416 | tf_op jit(solution)/shard_map/ppermute | solution.py:180
  208.7 1.3 collective-permute-start.19
  212.6 5.5 %collective-permute-start.17 = (f32[16,1,128]{2,1,0:T(1,128)S(1)}, f32[16,1,128]{2,1,0:T(1,128)S(1)}, u32[]{:S(2)}, u32[]{:S(2)}) collective-permute-start(f32[16,1,128]{2,1,0:T(1,128)S(1)} %get-tuple-element.14), channel_id=1, source_target_pairs={{0,32},{8,40},{16,48},{24,56},{32,64},{40,72},{48,80},{56,88},{64,... | collective-permute-start | bytes 24584 | tf_op jit(solution)/shard_map/ppermute | solution.py:180
  218.1 13.1 %collective-permute-start.15 = (f32[1,32,128]{2,1,0:T(8,128)S(1)}, f32[1,32,128]{2,1,0:T(8,128)S(1)}, u32[]{:S(2)}, u32[]{:S(2)}) collective-permute-start(f32[1,32,128]{2,1,0:T(8,128)S(1)} %get-tuple-element.12), channel_id=1, source_target_pairs={{0,128},{8,136},{16,144},{24,152},{32,160},{40,168},{48,176},{56,1... | collective-permute-start | bytes 49160 | tf_op jit(solution)/shard_map/ppermute | solution.py:180
  232.7 4.2 %collective-permute-done.16 = f32[1,32,128]{2,1,0:T(8,128)S(1)} collective-permute-done((f32[1,32,128]{2,1,0:T(8,128)S(1)}, f32[1,32,128]{2,1,0:T(8,128)S(1)}, u32[]{:S(2)}, u32[]{:S(2)}) %collective-permute-start.16) | collective-permute-done | bytes 16416 | tf_op jit(solution)/shard_map/ppermute | solution.py:180
  237.4 1.3 collective-permute-start.25
  241.3 5.5 %collective-permute-start.23 = (f32[16,1,128]{2,1,0:T(1,128)S(1)}, f32[16,1,128]{2,1,0:T(1,128)S(1)}, u32[]{:S(2)}, u32[]{:S(2)}) collective-permute-start(f32[16,1,128]{2,1,0:T(1,128)S(1)} %get-tuple-element.8), channel_id=1, source_target_pairs={{0,32},{8,40},{16,48},{24,56},{32,64},{40,72},{48,80},{56,88},{64,... | collective-permute-start | bytes 24584 | tf_op jit(solution)/shard_map/ppermute | solution.py:180
  246.8 13.7 %collective-permute-start.21 = (f32[1,32,128]{2,1,0:T(8,128)S(1)}, f32[1,32,128]{2,1,0:T(8,128)S(1)}, u32[]{:S(2)}, u32[]{:S(2)}) collective-permute-start(f32[1,32,128]{2,1,0:T(8,128)S(1)} %get-tuple-element.6), channel_id=1, source_target_pairs={{0,128},{8,136},{16,144},{24,152},{32,160},{40,168},{48,176},{56,1... | collective-permute-start | bytes 49160 | tf_op jit(solution)/shard_map/ppermute | solution.py:180
  261.9 4.2 %collective-permute-done.22 = f32[1,32,128]{2,1,0:T(8,128)S(1)} collective-permute-done((f32[1,32,128]{2,1,0:T(8,128)S(1)}, f32[1,32,128]{2,1,0:T(8,128)S(1)}, u32[]{:S(2)}, u32[]{:S(2)}) %collective-permute-start.22) | collective-permute-done | bytes 16416 | tf_op jit(solution)/shard_map/ppermute | solution.py:180
  266.1 1.7 fusion.23
  (102 shorter events, 26.9 us)
Async XLA Ops:
  0.6 200.7 %copy-start = (bf16[8,1,16,32,128]{4,3,2,1,0:T(8,128)(2,1)S(1)}, bf16[8,1,16,32,128]{4,3,2,1,0:T(8,128)(2,1)}, u32[]{:S(2)}) copy-start(bf16[8,1,16,32,128]{4,3,2,1,0:T(8,128)(2,1)} %param.9) | copy-start | bytes 3145732
  0.6 67.5 %copy-start.1 = (bf16[8,1,16,32,128]{4,3,2,1,0:T(8,128)(2,1)S(1)}, bf16[8,1,16,32,128]{4,3,2,1,0:T(8,128)(2,1)}, u32[]{:S(2)}) copy-start(bf16[8,1,16,32,128]{4,3,2,1,0:T(8,128)(2,1)} %param.10) | copy-start | bytes 3145732
  0.7 80.4 %collective-permute-start.6 = (f32[16,1,128]{2,1,0:T(1,128)S(1)}, f32[16,1,128]{2,1,0:T(1,128)S(1)}, u32[]{:S(2)}, u32[]{:S(2)}) collective-permute-start(f32[16,1,128]{2,1,0:T(1,128)S(1)} %broadcast.117), channel_id=1, source_target_pairs={{32,0},{40,8},{48,16},{56,24},{64,32},{72,40},{80,48},{88,56},{96,... | collective-permute-start | bytes 24584 | tf_op jit(solution)/shard_map/ppermute | solution.py:180
  2.1 92.0 %collective-permute-start.5 = (f32[16,1,128]{2,1,0:T(1,128)S(1)}, f32[16,1,128]{2,1,0:T(1,128)S(1)}, u32[]{:S(2)}, u32[]{:S(2)}) collective-permute-start(f32[16,1,128]{2,1,0:T(1,128)S(1)} %broadcast.117), channel_id=1, source_target_pairs={{0,32},{8,40},{16,48},{24,56},{32,64},{40,72},{48,80},{56,88},{64,... | collective-permute-start | bytes 24584 | tf_op jit(solution)/shard_map/ppermute | solution.py:180
  8.6 61.5 %copy-start.2 = (f32[1,16,32,128]{3,2,1,0:T(8,128)S(1)}, f32[1,16,32,128]{3,2,1,0:T(8,128)}, u32[]{:S(2)}) copy-start(f32[1,16,32,128]{3,2,1,0:T(8,128)} %param.8) | copy-start | bytes 786436
  8.6 62.9 %collective-permute-start.8 = (f32[16,32,1]{2,1,0:T(8,128)}, f32[16,32,1]{2,1,0:T(8,128)S(1)}, u32[]{:S(2)}, u32[]{:S(2)}) collective-permute-start(f32[16,32,1]{2,1,0:T(8,128)} %broadcast.118), channel_id=1, source_target_pairs={{8,0},{16,8},{24,16},{32,24},{40,32},{48,40},{56,48},{64,56},{72,6... | collective-permute-start | bytes 6152 | tf_op jit(solution)/shard_map/ppermute | solution.py:180
  10.1 64.6 %collective-permute-start.7 = (f32[16,32,1]{2,1,0:T(8,128)}, f32[16,32,1]{2,1,0:T(8,128)}, u32[]{:S(2)}, u32[]{:S(2)}) collective-permute-start(f32[16,32,1]{2,1,0:T(8,128)} %broadcast.118), channel_id=1, source_target_pairs={{0,8},{8,16},{16,24},{24,32},{32,40},{40,48},{48,56},{56,64},{64,7... | collective-permute-start | bytes 6152 | tf_op jit(solution)/shard_map/ppermute | solution.py:180
  56.7 16.6 %collective-permute-start = (f32[1,16,32,128]{3,2,1,0:T(8,128)}, f32[1,16,32,128]{3,2,1,0:T(8,128)S(1)}, u32[]{:S(2)}, u32[]{:S(2)}) collective-permute-start(f32[1,16,32,128]{3,2,1,0:T(8,128)} %bitcast.95), channel_id=1, source_target_pairs={{0,384},{8,392},{16,400},{24,408},{32,416},{40,424},{48,432},{56,4... | collective-permute-start | bytes 786440 | tf_op jit(solution)/shard_map/ppermute | solution.py:174
  71.5 22.6 %collective-permute-start.3 = (f32[1,32,128]{2,1,0:T(8,128)S(1)}, f32[1,32,128]{2,1,0:T(8,128)S(1)}, u32[]{:S(2)}, u32[]{:S(2)}) collective-permute-start(f32[1,32,128]{2,1,0:T(8,128)S(1)} %broadcast.116), channel_id=1, source_target_pairs={{0,128},{8,136},{16,144},{24,152},{32,160},{40,168},{48,176},{56,1... | collective-permute-start | bytes 49160 | tf_op jit(solution)/shard_map/ppermute | solution.py:180
  73.3 104.3 %collective-permute-start.4 = (f32[1,32,128]{2,1,0:T(8,128)S(1)}, f32[1,32,128]{2,1,0:T(8,128)S(1)}, u32[]{:S(2)}, u32[]{:S(2)}) collective-permute-start(f32[1,32,128]{2,1,0:T(8,128)S(1)} %broadcast.116), channel_id=1, source_target_pairs={{128,0},{136,8},{144,16},{152,24},{160,32},{168,40},{176,48},{184,... | collective-permute-start | bytes 49160 | tf_op jit(solution)/shard_map/ppermute | solution.py:180
  74.7 17.4 %collective-permute-start.1 = (f32[1,16,32,128]{3,2,1,0:T(8,128)S(1)}, f32[1,16,32,128]{3,2,1,0:T(8,128)S(1)}, u32[]{:S(2)}, u32[]{:S(2)}) collective-permute-start(f32[1,16,32,128]{3,2,1,0:T(8,128)S(1)} %add_multiply_fusion.1), channel_id=1, source_target_pairs={{0,96},{8,104},{16,112},{24,120},{32,64},{40,72},{48,80},{56,88},{... | collective-permute-start | bytes 786440 | tf_op jit(solution)/shard_map/ppermute | solution.py:174
  92.2 7.7 %collective-permute-start.2 = (f32[1,16,32,128]{3,2,1,0:T(8,128)S(1)}, f32[1,16,32,128]{3,2,1,0:T(8,128)S(1)}, u32[]{:S(2)}, u32[]{:S(2)}) collective-permute-start(f32[1,16,32,128]{3,2,1,0:T(8,128)S(1)} %add_multiply_fusion), channel_id=1, source_target_pairs={{0,24},{8,16},{16,8},{24,0},{32,56},{40,48},{48,40},{56,32},{64,88... | collective-permute-start | bytes 786440 | tf_op jit(solution)/shard_map/ppermute | solution.py:174
  137.6 40.0 %copy-start.5 = (f32[1,16,32,128]{3,2,1,0:T(8,128)}, f32[1,16,32,128]{3,2,1,0:T(8,128)S(1)}, u32[]{:S(2)}) copy-start(f32[1,16,32,128]{3,2,1,0:T(8,128)S(1)} %multiply_subtract_fusion) | copy-start | bytes 786436
  137.6 40.0 %copy-start.4 = (f32[16,32,1]{2,1,0:T(8,128)S(1)}, f32[16,32,1]{2,1,0:T(8,128)}, u32[]{:S(2)}) copy-start(f32[16,32,1]{2,1,0:T(8,128)} %broadcast_multiply_fusion.7) | copy-start | bytes 6148
  178.6 24.0 %collective-permute-start.13 = (f32[16,32,1]{2,1,0:T(8,128)S(1)}, f32[16,32,1]{2,1,0:T(8,128)S(1)}, u32[]{:S(2)}, u32[]{:S(2)}) collective-permute-start(f32[16,32,1]{2,1,0:T(8,128)S(1)} %get-tuple-element.22), channel_id=1, source_target_pairs={{0,8},{8,16},{16,24},{24,32},{32,40},{40,48},{48,56},{56,64},{64,7... | collective-permute-start | bytes 6152 | tf_op jit(solution)/shard_map/ppermute | solution.py:180
  180.7 23.3 %collective-permute-start.14 = (f32[16,32,1]{2,1,0:T(8,128)S(1)}, f32[16,32,1]{2,1,0:T(8,128)S(1)}, u32[]{:S(2)}, u32[]{:S(2)}) collective-permute-start(f32[16,32,1]{2,1,0:T(8,128)S(1)} %get-tuple-element.23), channel_id=1, source_target_pairs={{8,0},{16,8},{24,16},{32,24},{40,32},{48,40},{56,48},{64,56},{72,6... | collective-permute-start | bytes 6152 | tf_op jit(solution)/shard_map/ppermute | solution.py:180
  182.0 22.0 %collective-permute-start.12 = (f32[16,1,128]{2,1,0:T(1,128)S(1)}, f32[16,1,128]{2,1,0:T(1,128)S(1)}, u32[]{:S(2)}, u32[]{:S(2)}) collective-permute-start(f32[16,1,128]{2,1,0:T(1,128)S(1)} %get-tuple-element.21), channel_id=1, source_target_pairs={{32,0},{40,8},{48,16},{56,24},{64,32},{72,40},{80,48},{88,56},{96,... | collective-permute-start | bytes 24584 | tf_op jit(solution)/shard_map/ppermute | solution.py:180
  183.3 20.7 %collective-permute-start.11 = (f32[16,1,128]{2,1,0:T(1,128)S(1)}, f32[16,1,128]{2,1,0:T(1,128)S(1)}, u32[]{:S(2)}, u32[]{:S(2)}) collective-permute-start(f32[16,1,128]{2,1,0:T(1,128)S(1)} %get-tuple-element.20), channel_id=1, source_target_pairs={{0,32},{8,40},{16,48},{24,56},{32,64},{40,72},{48,80},{56,88},{64,... | collective-permute-start | bytes 24584 | tf_op jit(solution)/shard_map/ppermute | solution.py:180
  188.8 15.2 %collective-permute-start.9 = (f32[1,32,128]{2,1,0:T(8,128)S(1)}, f32[1,32,128]{2,1,0:T(8,128)S(1)}, u32[]{:S(2)}, u32[]{:S(2)}) collective-permute-start(f32[1,32,128]{2,1,0:T(8,128)S(1)} %get-tuple-element.18), channel_id=1, source_target_pairs={{0,128},{8,136},{16,144},{24,152},{32,160},{40,168},{48,176},{56,1... | collective-permute-start | bytes 49160 | tf_op jit(solution)/shard_map/ppermute | solution.py:180
  202.6 5.6 %collective-permute-start.10 = (f32[1,32,128]{2,1,0:T(8,128)S(1)}, f32[1,32,128]{2,1,0:T(8,128)S(1)}, u32[]{:S(2)}, u32[]{:S(2)}) collective-permute-start(f32[1,32,128]{2,1,0:T(8,128)S(1)} %get-tuple-element.19), channel_id=1, source_target_pairs={{128,0},{136,8},{144,16},{152,24},{160,32},{168,40},{176,48},{184,... | collective-permute-start | bytes 49160 | tf_op jit(solution)/shard_map/ppermute | solution.py:180
  208.7 22.6 %collective-permute-start.19 = (f32[16,32,1]{2,1,0:T(8,128)S(1)}, f32[16,32,1]{2,1,0:T(8,128)S(1)}, u32[]{:S(2)}, u32[]{:S(2)}) collective-permute-start(f32[16,32,1]{2,1,0:T(8,128)S(1)} %get-tuple-element.16), channel_id=1, source_target_pairs={{0,8},{8,16},{16,24},{24,32},{32,40},{40,48},{48,56},{56,64},{64,7... | collective-permute-start | bytes 6152 | tf_op jit(solution)/shard_map/ppermute | solution.py:180
  210.0 22.6 %collective-permute-start.20 = (f32[16,32,1]{2,1,0:T(8,128)S(1)}, f32[16,32,1]{2,1,0:T(8,128)S(1)}, u32[]{:S(2)}, u32[]{:S(2)}) collective-permute-start(f32[16,32,1]{2,1,0:T(8,128)S(1)} %get-tuple-element.17), channel_id=1, source_target_pairs={{8,0},{16,8},{24,16},{32,24},{40,32},{48,40},{56,48},{64,56},{72,6... | collective-permute-start | bytes 6152 | tf_op jit(solution)/shard_map/ppermute | solution.py:180
  211.3 21.3 %collective-permute-start.18 = (f32[16,1,128]{2,1,0:T(1,128)S(1)}, f32[16,1,128]{2,1,0:T(1,128)S(1)}, u32[]{:S(2)}, u32[]{:S(2)}) collective-permute-start(f32[16,1,128]{2,1,0:T(1,128)S(1)} %get-tuple-element.15), channel_id=1, source_target_pairs={{32,0},{40,8},{48,16},{56,24},{64,32},{72,40},{80,48},{88,56},{96,... | collective-permute-start | bytes 24584 | tf_op jit(solution)/shard_map/ppermute | solution.py:180
  212.6 20.1 %collective-permute-start.17 = (f32[16,1,128]{2,1,0:T(1,128)S(1)}, f32[16,1,128]{2,1,0:T(1,128)S(1)}, u32[]{:S(2)}, u32[]{:S(2)}) collective-permute-start(f32[16,1,128]{2,1,0:T(1,128)S(1)} %get-tuple-element.14), channel_id=1, source_target_pairs={{0,32},{8,40},{16,48},{24,56},{32,64},{40,72},{48,80},{56,88},{64,... | collective-permute-start | bytes 24584 | tf_op jit(solution)/shard_map/ppermute | solution.py:180
  218.1 14.6 %collective-permute-start.15 = (f32[1,32,128]{2,1,0:T(8,128)S(1)}, f32[1,32,128]{2,1,0:T(8,128)S(1)}, u32[]{:S(2)}, u32[]{:S(2)}) collective-permute-start(f32[1,32,128]{2,1,0:T(8,128)S(1)} %get-tuple-element.12), channel_id=1, source_target_pairs={{0,128},{8,136},{16,144},{24,152},{32,160},{40,168},{48,176},{56,1... | collective-permute-start | bytes 49160 | tf_op jit(solution)/shard_map/ppermute | solution.py:180
  231.3 5.6 %collective-permute-start.16 = (f32[1,32,128]{2,1,0:T(8,128)S(1)}, f32[1,32,128]{2,1,0:T(8,128)S(1)}, u32[]{:S(2)}, u32[]{:S(2)}) collective-permute-start(f32[1,32,128]{2,1,0:T(8,128)S(1)} %get-tuple-element.13), channel_id=1, source_target_pairs={{128,0},{136,8},{144,16},{152,24},{160,32},{168,40},{176,48},{184,... | collective-permute-start | bytes 49160 | tf_op jit(solution)/shard_map/ppermute | solution.py:180
  237.4 23.2 %collective-permute-start.25 = (f32[16,32,1]{2,1,0:T(8,128)S(1)}, f32[16,32,1]{2,1,0:T(8,128)S(1)}, u32[]{:S(2)}, u32[]{:S(2)}) collective-permute-start(f32[16,32,1]{2,1,0:T(8,128)S(1)} %get-tuple-element.10), channel_id=1, source_target_pairs={{0,8},{8,16},{16,24},{24,32},{32,40},{40,48},{48,56},{56,64},{64,7... | collective-permute-start | bytes 6152 | tf_op jit(solution)/shard_map/ppermute | solution.py:180
  238.7 23.2 %collective-permute-start.26 = (f32[16,32,1]{2,1,0:T(8,128)S(1)}, f32[16,32,1]{2,1,0:T(8,128)S(1)}, u32[]{:S(2)}, u32[]{:S(2)}) collective-permute-start(f32[16,32,1]{2,1,0:T(8,128)S(1)} %get-tuple-element.11), channel_id=1, source_target_pairs={{8,0},{16,8},{24,16},{32,24},{40,32},{48,40},{56,48},{64,56},{72,6... | collective-permute-start | bytes 6152 | tf_op jit(solution)/shard_map/ppermute | solution.py:180
  240.0 21.9 %collective-permute-start.24 = (f32[16,1,128]{2,1,0:T(1,128)S(1)}, f32[16,1,128]{2,1,0:T(1,128)S(1)}, u32[]{:S(2)}, u32[]{:S(2)}) collective-permute-start(f32[16,1,128]{2,1,0:T(1,128)S(1)} %get-tuple-element.9), channel_id=1, source_target_pairs={{32,0},{40,8},{48,16},{56,24},{64,32},{72,40},{80,48},{88,56},{96,... | collective-permute-start | bytes 24584 | tf_op jit(solution)/shard_map/ppermute | solution.py:180
  241.3 20.6 %collective-permute-start.23 = (f32[16,1,128]{2,1,0:T(1,128)S(1)}, f32[16,1,128]{2,1,0:T(1,128)S(1)}, u32[]{:S(2)}, u32[]{:S(2)}) collective-permute-start(f32[16,1,128]{2,1,0:T(1,128)S(1)} %get-tuple-element.8), channel_id=1, source_target_pairs={{0,32},{8,40},{16,48},{24,56},{32,64},{40,72},{48,80},{56,88},{64,... | collective-permute-start | bytes 24584 | tf_op jit(solution)/shard_map/ppermute | solution.py:180
  246.8 15.1 %collective-permute-start.21 = (f32[1,32,128]{2,1,0:T(8,128)S(1)}, f32[1,32,128]{2,1,0:T(8,128)S(1)}, u32[]{:S(2)}, u32[]{:S(2)}) collective-permute-start(f32[1,32,128]{2,1,0:T(8,128)S(1)} %get-tuple-element.6), channel_id=1, source_target_pairs={{0,128},{8,136},{16,144},{24,152},{32,160},{40,168},{48,176},{56,1... | collective-permute-start | bytes 49160 | tf_op jit(solution)/shard_map/ppermute | solution.py:180
  260.5 5.6 %collective-permute-start.22 = (f32[1,32,128]{2,1,0:T(8,128)S(1)}, f32[1,32,128]{2,1,0:T(8,128)S(1)}, u32[]{:S(2)}, u32[]{:S(2)}) collective-permute-start(f32[1,32,128]{2,1,0:T(8,128)S(1)} %get-tuple-element.7), channel_id=1, source_target_pairs={{128,0},{136,8},{144,16},{152,24},{160,32},{168,40},{176,48},{184,... | collective-permute-start | bytes 49160 | tf_op jit(solution)/shard_map/ppermute | solution.py:180
  (1 other events, 17.9 us)

commit v3 on v2

--- a/solution.py
+++ b/solution.py
@@ -225,27 +225,36 @@
     block_x = index // 16
     block_y = index // 4 % 4
     block_z = index % 4
-    keep_xlow = (block_x > 0).astype(jnp.float32)
     keep_ylow = (block_y > 0).astype(jnp.float32)
     keep_yhigh = (block_y < 3).astype(jnp.float32)
     keep_zlow = (block_z > 0).astype(jnp.float32)
     keep_zhigh = (block_z < 3).astype(jnp.float32)
     source = res_opt[0]
-    field_u = jnp.zeros_like(source)
+    h = SWEEPS - 1
+    cx, cy, cz = source.shape
+    ext = jnp.concatenate([neighbour(source[-h:], 16), source, neighbour(source[:h], -16)], 0)
+    ext = jnp.concatenate(
+        [neighbour(ext[:, -h:], 4) * keep_ylow, ext, neighbour(ext[:, :h], -4) * keep_yhigh], 1
+    )
+    ext = jnp.concatenate(
+        [neighbour(ext[:, :, -h:], 1) * keep_zlow, ext, neighbour(ext[:, :, :h], -1) * keep_zhigh], 2
+    )
+
+    def inside(block, size, n_blocks, axis):
+        pos = block * size + lax.broadcasted_iota(jnp.int32, ext.shape, axis) - h
+        return (pos >= 0) & (pos < size * n_blocks)
+
+    mask = (
+        inside(block_x, cx, lax.axis_size("grid") // 16, 0) & inside(block_y, cy, 4, 1) & inside(block_z, cz, 4, 2)
+    ).astype(jnp.float32)
+    field_u = jnp.zeros_like(ext)
     for sweep in range(SWEEPS):
-        x_low = neighbour(field_u[-1:], 16) * keep_xlow
-        x_high = neighbour(field_u[:1], -16)
-        y_low = neighbour(field_u[:, -1:], 4) * keep_ylow
-        y_high = neighbour(field_u[:, :1], -4) * keep_yhigh
-        z_low = neighbour(field_u[:, :, -1:], 1) * keep_zlow
-        z_high = neighbour(field_u[:, :, :1], -1) * keep_zhigh
-        along_x = jnp.concatenate([x_low, field_u, x_high], 0)
-        along_y = jnp.concatenate([y_low, field_u, y_high], 1)
-        along_z = jnp.concatenate([z_low, field_u, z_high], 2)
-        beside = along_x[:-2] + along_x[2:]
-        beside = beside + along_y[:, :-2] + along_y[:, 2:]
-        beside = beside + along_z[:, :, :-2] + along_z[:, :, 2:]
-        field_u = (source + beside) / (6.0 + kappa)
+        padded = jnp.pad(field_u, 1)
+        beside = padded[:-2, 1:-1, 1:-1] + padded[2:, 1:-1, 1:-1]
+        beside = beside + padded[1:-1, :-2, 1:-1] + padded[1:-1, 2:, 1:-1]
+        beside = beside + padded[1:-1, 1:-1, :-2] + padded[1:-1, 1:-1, 2:]
+        field_u = (ext + beside) / (6.0 + kappa) * mask
+    field_u = field_u[h : h + cx, h : h + cy, h : h + cz]
     density_next = rho_opt + mixing_weight * (res_opt - kappa * field_u[None])
     return (density_next, residual)
 

time: 269 us -> 208 us (0.77)
  the two profiles are of different devices: /device:TPU:4 before, /device:TPU:8 now
where the time goes in v3:
time: 208 us
  Pallas kernels  99.3 us (48%)
  starting transfers between devices  41.9 us (20%)
  waiting for transfers between devices  30.5 us (15%)
  other arithmetic  17.9 us (9%)
  matrix products  11.1 us (5%)
  local copies, waits for them, and re-layouts  3.95 us (2%)
  between operations  3.01 us (1%)
    pallas_call x2, Pallas kernels, grid_sum(): pl.pallas_call(functools.partial(_grid_sum_kernel, n), out_shape=jax.Shap...  57.8 us
    pallas_call x1, Pallas kernels, band_sum(): pl.pallas_call(_band_sum_kernel, out_shape=jax.ShapeDtypeStruct(part.shap...  41.5 us
    ppermute x6, starting transfers between devices, shifted(): return lax.ppermute(block, axis, route)  31.5 us
    ppermute x3, waiting for transfers between devices, partner(): return lax.ppermute(value, axis, pairs)  20 us
    ppermute x6, waiting for transfers between devices, shifted(): return lax.ppermute(block, axis, route)  10.5 us
    ppermute x3, starting transfers between devices, partner(): return lax.ppermute(value, axis, pairs)  10.3 us
    dot_general x1, matrix products, local(): local_gram = jnp.dot(vectors, vectors.T, precision=lax.Precision.HIGHEST)  7.7 us
  transfers between devices with their start and end apart: 9, of which 9 were waited for; matrix products, arithmetic and copies ran while one was open for 2% of the time, Pallas kernels for 0%

profile of v3, /device:TPU:8, one launch (start us, length us, event | category | flops | bytes accessed | tf_op | source)
XLA Modules:
  0.0 207.7 jit_solution(3647557970940913771)
XLA Ops:
  0.7 2.2 %fusion.4.x_ref = f32[16,32,128]{2,1,0:T(8,128)} fusion(bf16[4,1,16,32,128]{4,3,2,1,0:T(8,128)(2,1)} %param.6, f32[4]{0:T(128)} %param.7), kind=kLoop, calls=%fused_computation.14 | loop fusion | flops 983040 | bytes 786448 | tf_op jit(solution)/shard_map/reduce_sum | solution.py:196
  2.8 41.5 %shard_map.77 = f32[16,32,128]{2,1,0:T(8,128)} custom-call(f32[16,32,128]{2,1,0:T(8,128)} %fusion.4.x_ref), custom_call_target="tpu_custom_call" | custom-call | tf_op jit(solution)/shard_map/pallas_call | solution.py:150
  44.4 3.5 %collective-permute-start = (f32[1,16,32,128]{3,2,1,0:T(8,128)}, f32[1,16,32,128]{3,2,1,0:T(8,128)S(1)}, u32[]{:S(2)}, u32[]{:S(2)}) collective-permute-start(f32[1,16,32,128]{3,2,1,0:T(8,128)} %bitcast.83), channel_id=1, source_target_pairs={{0,384},{8,392},{16,400},{24,408},{32,416},{40,424},{48,432},{56,4... | collective-permute-start | bytes 786440 | tf_op jit(solution)/shard_map/ppermute | solution.py:174
  47.9 5.0 %collective-permute-done = f32[1,16,32,128]{3,2,1,0:T(8,128)S(1)} collective-permute-done((f32[1,16,32,128]{3,2,1,0:T(8,128)}, f32[1,16,32,128]{3,2,1,0:T(8,128)S(1)}, u32[]{:S(2)}, u32[]{:S(2)}) %collective-permute-start) | collective-permute-done | bytes 262176 | tf_op jit(solution)/shard_map/ppermute | solution.py:174
  52.8 1.0 add_multiply_fusion.1
  53.8 4.9 %collective-permute-start.1 = (f32[1,16,32,128]{3,2,1,0:T(8,128)S(1)}, f32[1,16,32,128]{3,2,1,0:T(8,128)S(1)}, u32[]{:S(2)}, u32[]{:S(2)}) collective-permute-start(f32[1,16,32,128]{3,2,1,0:T(8,128)S(1)} %add_multiply_fusion.1), channel_id=1, source_target_pairs={{0,96},{8,104},{16,112},{24,120},{32,64},{40,72},{48,80},{56,88},{... | collective-permute-start | bytes 786440 | tf_op jit(solution)/shard_map/ppermute | solution.py:174
  58.8 0.7 reduce_sum.38
  59.5 11.1 %collective-permute-done.1 = f32[1,16,32,128]{3,2,1,0:T(8,128)S(1)} collective-permute-done((f32[1,16,32,128]{3,2,1,0:T(8,128)S(1)}, f32[1,16,32,128]{3,2,1,0:T(8,128)S(1)}, u32[]{:S(2)}, u32[]{:S(2)}) %collective-permute-start.1) | collective-permute-done | bytes 262176 | tf_op jit(solution)/shard_map/ppermute | solution.py:174
  70.8 1.9 collective-permute-start.2
  72.7 1.9 copy_convert_fusion
  74.6 3.9 %collective-permute-done.2 = f32[1,16,32,128]{3,2,1,0:T(8,128)S(1)} collective-permute-done((f32[1,16,32,128]{3,2,1,0:T(8,128)S(1)}, f32[1,16,32,128]{3,2,1,0:T(8,128)S(1)}, u32[]{:S(2)}, u32[]{:S(2)}) %collective-permute-start.2) | collective-permute-done | bytes 262176 | tf_op jit(solution)/shard_map/ppermute | solution.py:174
  79.3 1.9 fusion.34.x_ref
  81.3 34.6 %shard_map.78 = f32[8,128]{1,0:T(8,128)} custom-call(f32[8,128]{1,0:T(8,128)} %fusion.34.x_ref), custom_call_target="tpu_custom_call" | custom-call | tf_op jit(solution)/shard_map/pallas_call | solution.py:74
  115.8 1.3 fusion.43
  118.6 7.7 %fusion.3 = f32[9,9]{1,0:T(8,128)S(1)} fusion(f32[1,1,16,32,128]{4,0,3,2,1:T(1,128)S(1)} %bitcast.85, f32[8,1,16,32,128]{4,0,3,2,1:T(8,128)} %copy_convert_fusion), kind=kOutput, calls=%fused_computation.11 | convolution fusion | flops 64290816 | bytes 2359620 | tf_op jit(solution)/shard_map/dot_general | solution.py:205
  127.0 23.2 %shard_map.79 = f32[8,128]{1,0:T(8,128)} custom-call(f32[8,128]{1,0:T(8,128)} %pad_bitcast_fusion.x_ref), custom_call_target="tpu_custom_call" | custom-call | tf_op jit(solution)/shard_map/pallas_call | solution.py:74
  151.1 0.8 cholesky.16
  154.1 0.8 fusion.44
  156.1 1.3 fusion.5
  158.1 3.0 %collective-permute-start.3 = (f32[3,32,128]{2,1,0:T(8,128)S(1)}, f32[3,32,128]{2,1,0:T(8,128)S(1)}, u32[]{:S(2)}, u32[]{:S(2)}) collective-permute-start(f32[3,32,128]{2,1,0:T(8,128)S(1)} %get-tuple-element.14), channel_id=1, source_target_pairs={{0,128},{8,136},{16,144},{24,152},{32,160},{40,168},{48,176},{56,1... | collective-permute-start | bytes 147464 | tf_op jit(solution)/shard_map/ppermute | solution.py:180
  161.1 2.8 %collective-permute-start.4 = (f32[3,32,128]{2,1,0:T(8,128)S(1)}, f32[3,32,128]{2,1,0:T(8,128)S(1)}, u32[]{:S(2)}, u32[]{:S(2)}) collective-permute-start(f32[3,32,128]{2,1,0:T(8,128)S(1)} %get-tuple-element.15), channel_id=1, source_target_pairs={{128,0},{136,8},{144,16},{152,24},{160,32},{168,40},{176,48},{184,... | collective-permute-start | bytes 147464 | tf_op jit(solution)/shard_map/ppermute | solution.py:180
  164.0 3.0 %collective-permute-done.4 = f32[3,32,128]{2,1,0:T(8,128)S(1)} collective-permute-done((f32[3,32,128]{2,1,0:T(8,128)S(1)}, f32[3,32,128]{2,1,0:T(8,128)S(1)}, u32[]{:S(2)}, u32[]{:S(2)}) %collective-permute-start.4) | collective-permute-done | bytes 49184 | tf_op jit(solution)/shard_map/ppermute | solution.py:180
  167.1 2.9 %collective-permute-start.5 = (f32[22,3,128]{2,1,0:T(4,128)S(1)}, f32[22,3,128]{2,1,0:T(4,128)S(1)}, u32[]{:S(2)}, u32[]{:S(2)}) collective-permute-start(f32[22,3,128]{2,1,0:T(4,128)S(1)} %get-tuple-element.12), channel_id=1, source_target_pairs={{0,32},{8,40},{16,48},{24,56},{32,64},{40,72},{48,80},{56,88},{64,... | collective-permute-start | bytes 101384 | tf_op jit(solution)/shard_map/ppermute | solution.py:180
  170.9 9.6 %collective-permute-start.6 = (f32[22,3,128]{2,1,0:T(4,128)S(1)}, f32[22,3,128]{2,1,0:T(4,128)S(1)}, u32[]{:S(2)}, u32[]{:S(2)}) collective-permute-start(f32[22,3,128]{2,1,0:T(4,128)S(1)} %get-tuple-element.13), channel_id=1, source_target_pairs={{32,0},{40,8},{48,16},{56,24},{64,32},{72,40},{80,48},{88,56},{96,... | collective-permute-start | bytes 101384 | tf_op jit(solution)/shard_map/ppermute | solution.py:180
  180.8 1.3 collective-permute-done.6
  182.4 1.9 collective-permute-start.7
  184.3 1.3 fusion.7
  185.6 11.3 %collective-permute-start.8 = (f32[22,38,3]{2,1,0:T(8,128)S(1)}, f32[22,38,3]{2,1,0:T(8,128)S(1)}, u32[]{:S(2)}, u32[]{:S(2)}) collective-permute-start(f32[22,38,3]{2,1,0:T(8,128)S(1)} %get-tuple-element.11), channel_id=1, source_target_pairs={{8,0},{16,8},{24,16},{32,24},{40,32},{48,40},{56,48},{64,56},{72,6... | collective-permute-start | bytes 30104 | tf_op jit(solution)/shard_map/ppermute | solution.py:180
  196.9 2.9 %collective-permute-done.7 = f32[22,38,3]{2,1,0:T(8,128)S(1)} collective-permute-done((f32[22,38,3]{2,1,0:T(8,128)S(1)}, f32[22,38,3]{2,1,0:T(8,128)S(1)}, u32[]{:S(2)}, u32[]{:S(2)}) %collective-permute-start.7) | collective-permute-done | bytes 10064 | tf_op jit(solution)/shard_map/ppermute | solution.py:180
  199.8 2.8 %collective-permute-done.8 = f32[22,38,3]{2,1,0:T(8,128)S(1)} collective-permute-done((f32[22,38,3]{2,1,0:T(8,128)S(1)}, f32[22,38,3]{2,1,0:T(8,128)S(1)}, u32[]{:S(2)}, u32[]{:S(2)}) %collective-permute-start.8) | collective-permute-done | bytes 10064 | tf_op jit(solution)/shard_map/ppermute | solution.py:180
  202.8 1.1 fusion.16
  205.8 1.9 fusion.29
  (45 shorter events, 9.6 us)
Async XLA Ops:
  0.6 183.7 %copy-start = (bf16[8,1,16,32,128]{4,3,2,1,0:T(8,128)(2,1)S(1)}, bf16[8,1,16,32,128]{4,3,2,1,0:T(8,128)(2,1)}, u32[]{:S(2)}) copy-start(bf16[8,1,16,32,128]{4,3,2,1,0:T(8,128)(2,1)} %param.9) | copy-start | bytes 3145732
  0.6 58.2 %copy-start.2 = (f32[1,16,32,128]{3,2,1,0:T(8,128)S(1)}, f32[1,16,32,128]{3,2,1,0:T(8,128)}, u32[]{:S(2)}) copy-start(f32[1,16,32,128]{3,2,1,0:T(8,128)} %param.8) | copy-start | bytes 786436
  0.7 72.0 %copy-start.1 = (bf16[8,1,16,32,128]{4,3,2,1,0:T(8,128)(2,1)S(1)}, bf16[8,1,16,32,128]{4,3,2,1,0:T(8,128)(2,1)}, u32[]{:S(2)}) copy-start(bf16[8,1,16,32,128]{4,3,2,1,0:T(8,128)(2,1)} %param.10) | copy-start | bytes 3145732
  44.4 8.5 %collective-permute-start = (f32[1,16,32,128]{3,2,1,0:T(8,128)}, f32[1,16,32,128]{3,2,1,0:T(8,128)S(1)}, u32[]{:S(2)}, u32[]{:S(2)}) collective-permute-start(f32[1,16,32,128]{3,2,1,0:T(8,128)} %bitcast.83), channel_id=1, source_target_pairs={{0,384},{8,392},{16,400},{24,408},{32,416},{40,424},{48,432},{56,4... | collective-permute-start | bytes 786440 | tf_op jit(solution)/shard_map/ppermute | solution.py:174
  53.8 16.8 %collective-permute-start.1 = (f32[1,16,32,128]{3,2,1,0:T(8,128)S(1)}, f32[1,16,32,128]{3,2,1,0:T(8,128)S(1)}, u32[]{:S(2)}, u32[]{:S(2)}) collective-permute-start(f32[1,16,32,128]{3,2,1,0:T(8,128)S(1)} %add_multiply_fusion.1), channel_id=1, source_target_pairs={{0,96},{8,104},{16,112},{24,120},{32,64},{40,72},{48,80},{56,88},{... | collective-permute-start | bytes 786440 | tf_op jit(solution)/shard_map/ppermute | solution.py:174
  70.8 7.8 %collective-permute-start.2 = (f32[1,16,32,128]{3,2,1,0:T(8,128)S(1)}, f32[1,16,32,128]{3,2,1,0:T(8,128)S(1)}, u32[]{:S(2)}, u32[]{:S(2)}) collective-permute-start(f32[1,16,32,128]{3,2,1,0:T(8,128)S(1)} %add_multiply_fusion), channel_id=1, source_target_pairs={{0,24},{8,16},{16,8},{24,0},{32,56},{40,48},{48,40},{56,32},{64,88... | collective-permute-start | bytes 786440 | tf_op jit(solution)/shard_map/ppermute | solution.py:174
  118.6 38.8 %copy-start.3 = (f32[1,16,32,128]{3,2,1,0:T(8,128)}, f32[1,16,32,128]{3,2,1,0:T(8,128)S(1)}, u32[]{:S(2)}) copy-start(f32[1,16,32,128]{3,2,1,0:T(8,128)S(1)} %multiply_subtract_fusion) | copy-start | bytes 786436
  158.1 6.0 %collective-permute-start.3 = (f32[3,32,128]{2,1,0:T(8,128)S(1)}, f32[3,32,128]{2,1,0:T(8,128)S(1)}, u32[]{:S(2)}, u32[]{:S(2)}) collective-permute-start(f32[3,32,128]{2,1,0:T(8,128)S(1)} %get-tuple-element.14), channel_id=1, source_target_pairs={{0,128},{8,136},{16,144},{24,152},{32,160},{40,168},{48,176},{56,1... | collective-permute-start | bytes 147464 | tf_op jit(solution)/shard_map/ppermute | solution.py:180
  161.1 6.0 %collective-permute-start.4 = (f32[3,32,128]{2,1,0:T(8,128)S(1)}, f32[3,32,128]{2,1,0:T(8,128)S(1)}, u32[]{:S(2)}, u32[]{:S(2)}) collective-permute-start(f32[3,32,128]{2,1,0:T(8,128)S(1)} %get-tuple-element.15), channel_id=1, source_target_pairs={{128,0},{136,8},{144,16},{152,24},{160,32},{168,40},{176,48},{184,... | collective-permute-start | bytes 147464 | tf_op jit(solution)/shard_map/ppermute | solution.py:180
  167.1 13.7 %collective-permute-start.5 = (f32[22,3,128]{2,1,0:T(4,128)S(1)}, f32[22,3,128]{2,1,0:T(4,128)S(1)}, u32[]{:S(2)}, u32[]{:S(2)}) collective-permute-start(f32[22,3,128]{2,1,0:T(4,128)S(1)} %get-tuple-element.12), channel_id=1, source_target_pairs={{0,32},{8,40},{16,48},{24,56},{32,64},{40,72},{48,80},{56,88},{64,... | collective-permute-start | bytes 101384 | tf_op jit(solution)/shard_map/ppermute | solution.py:180
  170.9 11.3 %collective-permute-start.6 = (f32[22,3,128]{2,1,0:T(4,128)S(1)}, f32[22,3,128]{2,1,0:T(4,128)S(1)}, u32[]{:S(2)}, u32[]{:S(2)}) collective-permute-start(f32[22,3,128]{2,1,0:T(4,128)S(1)} %get-tuple-element.13), channel_id=1, source_target_pairs={{32,0},{40,8},{48,16},{56,24},{64,32},{72,40},{80,48},{88,56},{96,... | collective-permute-start | bytes 101384 | tf_op jit(solution)/shard_map/ppermute | solution.py:180
  182.4 17.4 %collective-permute-start.7 = (f32[22,38,3]{2,1,0:T(8,128)S(1)}, f32[22,38,3]{2,1,0:T(8,128)S(1)}, u32[]{:S(2)}, u32[]{:S(2)}) collective-permute-start(f32[22,38,3]{2,1,0:T(8,128)S(1)} %get-tuple-element.10), channel_id=1, source_target_pairs={{0,8},{8,16},{16,24},{24,32},{32,40},{40,48},{48,56},{56,64},{64,7... | collective-permute-start | bytes 30104 | tf_op jit(solution)/shard_map/ppermute | solution.py:180
  185.6 17.0 %collective-permute-start.8 = (f32[22,38,3]{2,1,0:T(8,128)S(1)}, f32[22,38,3]{2,1,0:T(8,128)S(1)}, u32[]{:S(2)}, u32[]{:S(2)}) collective-permute-start(f32[22,38,3]{2,1,0:T(8,128)S(1)} %get-tuple-element.11), channel_id=1, source_target_pairs={{8,0},{16,8},{24,16},{32,24},{40,32},{48,40},{56,48},{64,56},{72,6... | collective-permute-start | bytes 30104 | tf_op jit(solution)/shard_map/ppermute | solution.py:180

commit v4 on v3

--- a/solution.py
+++ b/solution.py
@@ -195,15 +195,23 @@
     waves = orbitals.astype(jnp.float32)
     partial_value = jnp.sum(occupations[:, None, None, None, None] * waves * waves, 0)
     rho_out = band_sum(partial_value[0])[None]
+    charges = grid_sum(pack([jnp.sum(rho_out), jnp.sum(density_in)]), 1)
     rho_sym = symmetrize(rho_out)
     depth = history_res.shape[0]
     res_hist = history_res.astype(jnp.float32)
-    charges = grid_sum(pack([jnp.sum(rho_sym), jnp.sum(density_in)]), 1)
+    hist_flat = res_hist.reshape(depth, -1)
+    hist_gram = jnp.sum(hist_flat[:, None, :] * hist_flat[None, :, :], axis=-1)
     scale = charges[0, 1] / charges[0, 0]
     residual = scale * rho_sym - density_in
-    vectors = jnp.concatenate([res_hist, residual[None]], 0).reshape(depth + 1, -1)
-    local_gram = jnp.dot(vectors, vectors.T, precision=lax.Precision.HIGHEST)
-    gram = grid_sum(pack([local_gram]), 2).reshape(-1)[: (depth + 1) ** 2].reshape(depth + 1, depth + 1)
+    res_flat = residual.reshape(-1)
+    last_row = jnp.sum(hist_flat * res_flat[None, :], axis=-1)
+    last = jnp.sum(res_flat * res_flat)
+    total = grid_sum(pack([hist_gram, last_row, last]), 2).reshape(-1)
+    gram = jnp.zeros((depth + 1, depth + 1), jnp.float32)
+    gram = gram.at[:depth, :depth].set(total[: depth * depth].reshape(depth, depth))
+    row = total[depth * depth : depth * depth + depth]
+    gram = gram.at[depth, :depth].set(row).at[:depth, depth].set(row)
+    gram = gram.at[depth, depth].set(total[depth * depth + depth])
     lower = jnp.linalg.cholesky(gram)
     solved = jax.scipy.linalg.cho_solve((lower, True), jnp.ones((depth + 1,), jnp.float32))
     coefficients = solved / jnp.sum(solved)

time: 208 us -> 199 us (0.957)
  waiting for transfers between devices: 30.5 us -> 15.3 us
  matrix products: 11.1 us -> 3.44 us
  local copies, waits for them, and re-layouts: 3.95 us -> 10.4 us
  other arithmetic: 17.9 us -> 22.5 us
    ppermute x3, waiting for transfers between devices: 20 us -> 5.15 us  [partner(): return lax.ppermute(value, axis, pairs)]
    dot_general x1 -> x0, matrix products: 7.7 us -> none  [local(): local_gram = jnp.dot(vectors, vectors.T, precision=lax.Precision.HIGHEST)]
    another operation x0 -> x3, other arithmetic: none -> 3.28 us
    reduce_sum x2 -> x5, other arithmetic: 1.4 us -> 4.18 us  [the longest x1 1.68 us: local(): hist_gram = jnp.sum(hist_flat[:, None, :] * hist_flat[None, :, :], axis=-1)]
    scatter x0 -> x5, local copies, waits for them, and re-layouts: none -> 2.49 us  [the longest x2 1.6 us: local(): gram = gram.at[depth, :depth].set(row).at[:depth, depth].set(row)]
  transfers between devices with their start and end apart: 9 -> 9, of which waited for: 9 -> 7; matrix products, arithmetic and copies ran while one was open for 2% -> 6% of each run, Pallas kernels for 0% -> 18%
where the time goes in v4:
time: 199 us; the launch traced here: 198 us
  Pallas kernels  101 us (51%)
  starting transfers between devices  42.2 us (21%)
  other arithmetic  22.5 us (11%)
  waiting for transfers between devices  15.3 us (8%)
  local copies, waits for them, and re-layouts  10.4 us (5%)
  matrix products  3.44 us (2%)
  between operations  3.05 us (2%)
    pallas_call x2, Pallas kernels, grid_sum(): pl.pallas_call(functools.partial(_grid_sum_kernel, n), out_shape=jax.Shap...  59.3 us
    pallas_call x1, Pallas kernels, band_sum(): pl.pallas_call(_band_sum_kernel, out_shape=jax.ShapeDtypeStruct(part.shap...  41.5 us
    ppermute x6, starting transfers between devices, shifted(): return lax.ppermute(block, axis, route)  31.5 us
    ppermute x3, starting transfers between devices, partner(): return lax.ppermute(value, axis, pairs)  10.7 us
    ppermute x6, waiting for transfers between devices, shifted(): return lax.ppermute(block, axis, route)  10.2 us
    ppermute x3, waiting for transfers between devices, partner(): return lax.ppermute(value, axis, pairs)  5.15 us
  transfers between devices with their start and end apart: 9, of which 7 were waited for; matrix products, arithmetic and copies ran while one was open for 6% of the time, Pallas kernels for 18%

profile of v4, /device:TPU:8, one launch (start us, length us, event | category | flops | bytes accessed | tf_op | source)
XLA Modules:
  0.0 197.8 jit_solution(2446993765647355278)
XLA Ops:
  0.6 2.1 %fusion.x_ref = f32[16,32,128]{2,1,0:T(8,128)} fusion(bf16[4,1,16,32,128]{4,3,2,1,0:T(8,128)(2,1)} %param.14, f32[4]{0:T(128)} %param.15), kind=kLoop, calls=%fused_computation.12 | loop fusion | flops 983040 | bytes 786448 | tf_op jit(solution)/shard_map/reduce_sum | solution.py:196
  2.7 41.5 %shard_map.77 = f32[16,32,128]{2,1,0:T(8,128)} custom-call(f32[16,32,128]{2,1,0:T(8,128)} %fusion.x_ref), custom_call_target="tpu_custom_call" | custom-call | tf_op jit(solution)/shard_map/pallas_call | solution.py:150
  44.3 3.5 %collective-permute-start = (f32[1,16,32,128]{3,2,1,0:T(8,128)}, f32[1,16,32,128]{3,2,1,0:T(8,128)S(1)}, u32[]{:S(2)}, u32[]{:S(2)}) collective-permute-start(f32[1,16,32,128]{3,2,1,0:T(8,128)} %bitcast.88), channel_id=1, source_target_pairs={{0,384},{8,392},{16,400},{24,408},{32,416},{40,424},{48,432},{56,4... | collective-permute-start | bytes 786440 | tf_op jit(solution)/shard_map/ppermute | solution.py:174
  47.8 1.8 copy.32
  49.6 1.7 multiply_reduce_fusion
  52.7 1.9 fusion.31.x_ref
  54.7 4.9 %collective-permute-start.1 = (f32[1,16,32,128]{3,2,1,0:T(8,128)S(1)}, f32[1,16,32,128]{3,2,1,0:T(8,128)S(1)}, u32[]{:S(2)}, u32[]{:S(2)}) collective-permute-start(f32[1,16,32,128]{3,2,1,0:T(8,128)S(1)} %add_multiply_fusion.1), channel_id=1, source_target_pairs={{0,96},{8,104},{16,112},{24,120},{32,64},{40,72},{48,80},{56,88},{... | collective-permute-start | bytes 786440 | tf_op jit(solution)/shard_map/ppermute | solution.py:174
  59.7 34.9 %shard_map.78 = f32[8,128]{1,0:T(8,128)} custom-call(f32[8,128]{1,0:T(8,128)} %fusion.31.x_ref), custom_call_target="tpu_custom_call" | custom-call | tf_op jit(solution)/shard_map/pallas_call | solution.py:74
  94.6 1.3 fusion.39
  96.0 2.3 %collective-permute-start.2 = (f32[1,16,32,128]{3,2,1,0:T(8,128)S(1)}, f32[1,16,32,128]{3,2,1,0:T(8,128)S(1)}, u32[]{:S(2)}, u32[]{:S(2)}) collective-permute-start(f32[1,16,32,128]{3,2,1,0:T(8,128)S(1)} %add_multiply_fusion), channel_id=1, source_target_pairs={{0,24},{8,16},{16,8},{24,0},{32,56},{40,48},{48,40},{56,32},{64,88... | collective-permute-start | bytes 786440 | tf_op jit(solution)/shard_map/ppermute | solution.py:174
  101.0 5.1 %collective-permute-done.2 = f32[1,16,32,128]{3,2,1,0:T(8,128)S(1)} collective-permute-done((f32[1,16,32,128]{3,2,1,0:T(8,128)S(1)}, f32[1,16,32,128]{3,2,1,0:T(8,128)S(1)}, u32[]{:S(2)}, u32[]{:S(2)}) %collective-permute-start.2) | collective-permute-done | bytes 262176 | tf_op jit(solution)/shard_map/ppermute | solution.py:174
  107.4 1.4 fusion.30.x_ref
  108.8 24.4 %shard_map.79 = f32[8,128]{1,0:T(8,128)} custom-call(f32[8,128]{1,0:T(8,128)} %fusion.30.x_ref), custom_call_target="tpu_custom_call" | custom-call | tf_op jit(solution)/shard_map/pallas_call | solution.py:74
  134.8 1.3 slice.228
  136.4 2.6 %broadcast_select_fusion = f32[8,1]{0,1:T(1,128)S(1)} fusion(pred[]{:T(512)} %and_reduce_fusion, f32[9,9]{0,1:T(8,128)S(1)} %scatter.15, s32[]{:T(128)} %bitcast.11, s32[]{:T(128)} %bitcast.12, f32[1024]{0:T(1024)} %bitcast.93), kind=kLoop, calls=%fused_computation.95 | loop fusion | flops 8 | bytes 105 | tf_op jit(solution)/shard_map/select.18
  139.0 1.4 scatter.16
  140.4 0.8 scatter.19
  141.3 0.8 cholesky.15
  146.3 1.3 fusion.1
  148.4 2.7 %collective-permute-start.3 = (f32[3,32,128]{2,1,0:T(8,128)S(1)}, f32[3,32,128]{2,1,0:T(8,128)S(1)}, u32[]{:S(2)}, u32[]{:S(2)}) collective-permute-start(f32[3,32,128]{2,1,0:T(8,128)S(1)} %get-tuple-element.62), channel_id=1, source_target_pairs={{0,128},{8,136},{16,144},{24,152},{32,160},{40,168},{48,176},{56,1... | collective-permute-start | bytes 147464 | tf_op jit(solution)/shard_map/ppermute | solution.py:180
  151.1 3.1 %collective-permute-start.4 = (f32[3,32,128]{2,1,0:T(8,128)S(1)}, f32[3,32,128]{2,1,0:T(8,128)S(1)}, u32[]{:S(2)}, u32[]{:S(2)}) collective-permute-start(f32[3,32,128]{2,1,0:T(8,128)S(1)} %get-tuple-element.63), channel_id=1, source_target_pairs={{128,0},{136,8},{144,16},{152,24},{160,32},{168,40},{176,48},{184,... | collective-permute-start | bytes 147464 | tf_op jit(solution)/shard_map/ppermute | solution.py:180
  154.3 2.7 %collective-permute-done.4 = f32[3,32,128]{2,1,0:T(8,128)S(1)} collective-permute-done((f32[3,32,128]{2,1,0:T(8,128)S(1)}, f32[3,32,128]{2,1,0:T(8,128)S(1)}, u32[]{:S(2)}, u32[]{:S(2)}) %collective-permute-start.4) | collective-permute-done | bytes 49184 | tf_op jit(solution)/shard_map/ppermute | solution.py:180
  157.1 2.7 %collective-permute-start.5 = (f32[22,3,128]{2,1,0:T(4,128)S(1)}, f32[22,3,128]{2,1,0:T(4,128)S(1)}, u32[]{:S(2)}, u32[]{:S(2)}) collective-permute-start(f32[22,3,128]{2,1,0:T(4,128)S(1)} %get-tuple-element.60), channel_id=1, source_target_pairs={{0,32},{8,40},{16,48},{24,56},{32,64},{40,72},{48,80},{56,88},{64,... | collective-permute-start | bytes 101384 | tf_op jit(solution)/shard_map/ppermute | solution.py:180
  160.7 9.8 %collective-permute-start.6 = (f32[22,3,128]{2,1,0:T(4,128)S(1)}, f32[22,3,128]{2,1,0:T(4,128)S(1)}, u32[]{:S(2)}, u32[]{:S(2)}) collective-permute-start(f32[22,3,128]{2,1,0:T(4,128)S(1)} %get-tuple-element.61), channel_id=1, source_target_pairs={{32,0},{40,8},{48,16},{56,24},{64,32},{72,40},{80,48},{88,56},{96,... | collective-permute-start | bytes 101384 | tf_op jit(solution)/shard_map/ppermute | solution.py:180
  170.9 1.2 collective-permute-done.6
  172.4 1.9 collective-permute-start.7
  174.3 1.3 fusion.3
  175.6 11.3 %collective-permute-start.8 = (f32[22,38,3]{2,1,0:T(8,128)S(1)}, f32[22,38,3]{2,1,0:T(8,128)S(1)}, u32[]{:S(2)}, u32[]{:S(2)}) collective-permute-start(f32[22,38,3]{2,1,0:T(8,128)S(1)} %get-tuple-element.59), channel_id=1, source_target_pairs={{8,0},{16,8},{24,16},{32,24},{40,32},{48,40},{56,48},{64,56},{72,6... | collective-permute-start | bytes 30104 | tf_op jit(solution)/shard_map/ppermute | solution.py:180
  187.0 2.9 %collective-permute-done.7 = f32[22,38,3]{2,1,0:T(8,128)S(1)} collective-permute-done((f32[22,38,3]{2,1,0:T(8,128)S(1)}, f32[22,38,3]{2,1,0:T(8,128)S(1)}, u32[]{:S(2)}, u32[]{:S(2)}) %collective-permute-start.7) | collective-permute-done | bytes 10064 | tf_op jit(solution)/shard_map/ppermute | solution.py:180
  189.9 2.8 %collective-permute-done.8 = f32[22,38,3]{2,1,0:T(8,128)S(1)} collective-permute-done((f32[22,38,3]{2,1,0:T(8,128)S(1)}, f32[22,38,3]{2,1,0:T(8,128)S(1)}, u32[]{:S(2)}, u32[]{:S(2)}) %collective-permute-start.8) | collective-permute-done | bytes 10064 | tf_op jit(solution)/shard_map/ppermute | solution.py:180
  192.8 1.0 fusion.12
  195.8 2.0 fusion.25
  (62 shorter events, 14.3 us)
Async XLA Ops:
  0.6 173.7 %copy-start = (bf16[8,1,16,32,128]{4,3,2,1,0:T(8,128)(2,1)S(1)}, bf16[8,1,16,32,128]{4,3,2,1,0:T(8,128)(2,1)}, u32[]{:S(2)}) copy-start(bf16[8,1,16,32,128]{4,3,2,1,0:T(8,128)(2,1)} %param.17) | copy-start | bytes 3145732
  44.3 10.4 %collective-permute-start = (f32[1,16,32,128]{3,2,1,0:T(8,128)}, f32[1,16,32,128]{3,2,1,0:T(8,128)S(1)}, u32[]{:S(2)}, u32[]{:S(2)}) collective-permute-start(f32[1,16,32,128]{3,2,1,0:T(8,128)} %bitcast.88), channel_id=1, source_target_pairs={{0,384},{8,392},{16,400},{24,408},{32,416},{40,424},{48,432},{56,4... | collective-permute-start | bytes 786440 | tf_op jit(solution)/shard_map/ppermute | solution.py:174
  49.6 1.7 copy-start.4
  49.6 2.4 %copy-start.2 = (f32[1,16,32,128]{3,2,1,0:T(8,128)S(1)}, f32[1,16,32,128]{3,2,1,0:T(8,128)}, u32[]{:S(2)}) copy-start(f32[1,16,32,128]{3,2,1,0:T(8,128)} %param.16) | copy-start | bytes 786436
  51.3 49.0 %copy-start.5 = (s32[2]{0:T(128)S(1)}, s32[2]{0:T(128)}, u32[]{:S(2)}) copy-start(s32[2]{0:T(128)} %constant.211.clone.1) | copy-start | bytes 28
  52.0 55.0 %copy-start.1 = (bf16[8,1,16,32,128]{4,3,2,1,0:T(8,128)(2,1)S(1)}, bf16[8,1,16,32,128]{4,3,2,1,0:T(8,128)(2,1)}, u32[]{:S(2)}) copy-start(bf16[8,1,16,32,128]{4,3,2,1,0:T(8,128)(2,1)} %param.18) | copy-start | bytes 3145732
  54.7 41.2 %collective-permute-start.1 = (f32[1,16,32,128]{3,2,1,0:T(8,128)S(1)}, f32[1,16,32,128]{3,2,1,0:T(8,128)S(1)}, u32[]{:S(2)}, u32[]{:S(2)}) collective-permute-start(f32[1,16,32,128]{3,2,1,0:T(8,128)S(1)} %add_multiply_fusion.1), channel_id=1, source_target_pairs={{0,96},{8,104},{16,112},{24,120},{32,64},{40,72},{48,80},{56,88},{... | collective-permute-start | bytes 786440 | tf_op jit(solution)/shard_map/ppermute | solution.py:174
  96.0 10.2 %collective-permute-start.2 = (f32[1,16,32,128]{3,2,1,0:T(8,128)S(1)}, f32[1,16,32,128]{3,2,1,0:T(8,128)S(1)}, u32[]{:S(2)}, u32[]{:S(2)}) collective-permute-start(f32[1,16,32,128]{3,2,1,0:T(8,128)S(1)} %add_multiply_fusion), channel_id=1, source_target_pairs={{0,24},{8,16},{16,8},{24,0},{32,56},{40,48},{48,40},{56,32},{64,88... | collective-permute-start | bytes 786440 | tf_op jit(solution)/shard_map/ppermute | solution.py:174
  107.1 50.0 %copy-start.3 = (f32[1,16,32,128]{3,2,1,0:T(8,128)}, f32[1,16,32,128]{3,2,1,0:T(8,128)S(1)}, u32[]{:S(2)}) copy-start(f32[1,16,32,128]{3,2,1,0:T(8,128)S(1)} %get-tuple-element.53) | copy-start | bytes 786436
  148.4 6.0 %collective-permute-start.3 = (f32[3,32,128]{2,1,0:T(8,128)S(1)}, f32[3,32,128]{2,1,0:T(8,128)S(1)}, u32[]{:S(2)}, u32[]{:S(2)}) collective-permute-start(f32[3,32,128]{2,1,0:T(8,128)S(1)} %get-tuple-element.62), channel_id=1, source_target_pairs={{0,128},{8,136},{16,144},{24,152},{32,160},{40,168},{48,176},{56,1... | collective-permute-start | bytes 147464 | tf_op jit(solution)/shard_map/ppermute | solution.py:180
  151.1 6.0 %collective-permute-start.4 = (f32[3,32,128]{2,1,0:T(8,128)S(1)}, f32[3,32,128]{2,1,0:T(8,128)S(1)}, u32[]{:S(2)}, u32[]{:S(2)}) collective-permute-start(f32[3,32,128]{2,1,0:T(8,128)S(1)} %get-tuple-element.63), channel_id=1, source_target_pairs={{128,0},{136,8},{144,16},{152,24},{160,32},{168,40},{176,48},{184,... | collective-permute-start | bytes 147464 | tf_op jit(solution)/shard_map/ppermute | solution.py:180
  157.1 13.8 %collective-permute-start.5 = (f32[22,3,128]{2,1,0:T(4,128)S(1)}, f32[22,3,128]{2,1,0:T(4,128)S(1)}, u32[]{:S(2)}, u32[]{:S(2)}) collective-permute-start(f32[22,3,128]{2,1,0:T(4,128)S(1)} %get-tuple-element.60), channel_id=1, source_target_pairs={{0,32},{8,40},{16,48},{24,56},{32,64},{40,72},{48,80},{56,88},{64,... | collective-permute-start | bytes 101384 | tf_op jit(solution)/shard_map/ppermute | solution.py:180
  160.7 11.5 %collective-permute-start.6 = (f32[22,3,128]{2,1,0:T(4,128)S(1)}, f32[22,3,128]{2,1,0:T(4,128)S(1)}, u32[]{:S(2)}, u32[]{:S(2)}) collective-permute-start(f32[22,3,128]{2,1,0:T(4,128)S(1)} %get-tuple-element.61), channel_id=1, source_target_pairs={{32,0},{40,8},{48,16},{56,24},{64,32},{72,40},{80,48},{88,56},{96,... | collective-permute-start | bytes 101384 | tf_op jit(solution)/shard_map/ppermute | solution.py:180
  172.4 17.4 %collective-permute-start.7 = (f32[22,38,3]{2,1,0:T(8,128)S(1)}, f32[22,38,3]{2,1,0:T(8,128)S(1)}, u32[]{:S(2)}, u32[]{:S(2)}) collective-permute-start(f32[22,38,3]{2,1,0:T(8,128)S(1)} %get-tuple-element.58), channel_id=1, source_target_pairs={{0,8},{8,16},{16,24},{24,32},{32,40},{40,48},{48,56},{56,64},{64,7... | collective-permute-start | bytes 30104 | tf_op jit(solution)/shard_map/ppermute | solution.py:180
  175.6 17.0 %collective-permute-start.8 = (f32[22,38,3]{2,1,0:T(8,128)S(1)}, f32[22,38,3]{2,1,0:T(8,128)S(1)}, u32[]{:S(2)}, u32[]{:S(2)}) collective-permute-start(f32[22,38,3]{2,1,0:T(8,128)S(1)} %get-tuple-element.59), channel_id=1, source_target_pairs={{8,0},{16,8},{24,16},{32,24},{40,32},{48,40},{56,48},{64,56},{72,6... | collective-permute-start | bytes 30104 | tf_op jit(solution)/shard_map/ppermute | solution.py:180

commit v5 on v4

--- a/solution.py
+++ b/solution.py
@@ -13,73 +13,87 @@
 mixing_weight = 0.5
 
 
-def _grid_sum_kernel(n, x_ref, o_ref, buf, send_sem, recv_sem):
+def _grid_sum_kernel(n, x_ref, o_ref, buf_a, sum_a, buf_b, sa, ra, sb, rb):
     me = lax.axis_index("grid")
     band = lax.axis_index("band")
+    na = buf_a.shape[0]
+    nb = n // na
+    row = me // na
+    j = me % na
     barrier = pltpu.get_barrier_semaphore()
 
-    def greet(k, c):
-        peer = lax.rem(me + k, n)
-        pl.semaphore_signal(barrier, inc=1, device_id=(peer, band), device_id_type=MESH)
+    def greet_a(k, c):
+        pl.semaphore_signal(barrier, inc=1, device_id=(row * na + lax.rem(j + k, na), band), device_id_type=MESH)
         return c
 
-    lax.fori_loop(1, n, greet, 0)
-    pl.semaphore_wait(barrier, n - 1)
-
-    def send(k, c):
-        peer = lax.rem(me + k, n)
-        pltpu.make_async_remote_copy(
+    lax.fori_loop(1, na, greet_a, 0)
+    for k in range(1, nb):
+        pl.semaphore_signal(barrier, inc=1, device_id=(lax.rem(row + k, nb) * na + j, band), device_id_type=MESH)
+    pl.semaphore_wait(barrier, na - 1 + nb - 1)
+
+    def copy_a(src_slot, peer_j):
+        return pltpu.make_async_remote_copy(
             src_ref=x_ref,
-            dst_ref=buf.at[me],
-            send_sem=send_sem.at[peer],
-            recv_sem=recv_sem.at[me],
-            device_id=(peer, band),
+            dst_ref=buf_a.at[src_slot],
+            send_sem=sa.at[peer_j],
+            recv_sem=ra.at[src_slot],
+            device_id=(row * na + peer_j, band),
             device_id_type=MESH,
-        ).start()
+        )
+
+    def send_a(k, c):
+        copy_a(j, lax.rem(j + k, na)).start()
         return c
 
-    lax.fori_loop(1, n, send, 0)
-    buf[me] = x_ref[...]
-
-    def wait(k, c):
-        peer = lax.rem(me + k, n)
-        pltpu.make_async_remote_copy(
-            src_ref=x_ref,
-            dst_ref=buf.at[me],
-            send_sem=send_sem.at[peer],
-            recv_sem=recv_sem.at[me],
-            device_id=(peer, band),
+    lax.fori_loop(1, na, send_a, 0)
+    buf_a[j] = x_ref[...]
+
+    def wait_a(k, c):
+        peer = lax.rem(j + k, na)
+        copy_a(j, peer).wait_send()
+        copy_a(peer, peer).wait_recv()
+        return c
+
+    lax.fori_loop(1, na, wait_a, 0)
+    sum_a[...] = lax.fori_loop(1, na, lambda p, acc: acc + buf_a[p], buf_a[0])
+
+    def copy_b(src_slot, peer_row):
+        return pltpu.make_async_remote_copy(
+            src_ref=sum_a,
+            dst_ref=buf_b.at[src_slot],
+            send_sem=sb.at[peer_row],
+            recv_sem=rb.at[src_slot],
+            device_id=(peer_row * na + j, band),
             device_id_type=MESH,
-        ).wait_send()
-        pltpu.make_async_remote_copy(
-            src_ref=x_ref,
-            dst_ref=buf.at[peer],
-            send_sem=send_sem.at[peer],
-            recv_sem=recv_sem.at[peer],
-            device_id=(peer, band),
-            device_id_type=MESH,
-        ).wait_recv()
-        return c
-
-    lax.fori_loop(1, n, wait, 0)
-
-    def add(p, acc):
-        return acc + buf[p]
-
-    o_ref[...] = lax.fori_loop(1, n, add, buf[0])
+        )
+
+    for k in range(1, nb):
+        copy_b(row, lax.rem(row + k, nb)).start()
+    buf_b[row] = sum_a[...]
+    for k in range(1, nb):
+        peer = lax.rem(row + k, nb)
+        copy_b(row, peer).wait_send()
+        copy_b(peer, peer).wait_recv()
+    acc = buf_b[0]
+    for p in range(1, nb):
+        acc = acc + buf_b[p]
+    o_ref[...] = acc
 
 
 def grid_sum(vec, collective_id):
     n = lax.axis_size("grid")
+    na = 16
+    dma = pltpu.SemaphoreType.DMA
     return pl.pallas_call(
         functools.partial(_grid_sum_kernel, n),
         out_shape=jax.ShapeDtypeStruct(vec.shape, jnp.float32),
         in_specs=[pl.BlockSpec(memory_space=pltpu.VMEM)],
         out_specs=pl.BlockSpec(memory_space=pltpu.VMEM),
         scratch_shapes=[
-            pltpu.VMEM((n,) + vec.shape, jnp.float32),
-            pltpu.SemaphoreType.DMA((n,)),
-            pltpu.SemaphoreType.DMA((n,)),
+            pltpu.VMEM((na,) + vec.shape, jnp.float32),
+            pltpu.VMEM(vec.shape, jnp.float32),
+            pltpu.VMEM((n // na,) + vec.shape, jnp.float32),
+            dma((na,)), dma((na,)), dma((n // na,)), dma((n // na,)),
         ],
         compiler_params=pltpu.CompilerParams(collective_id=collective_id, has_side_effects=True),
     )(vec)
@@ -207,11 +221,10 @@
     last_row = jnp.sum(hist_flat * res_flat[None, :], axis=-1)
     last = jnp.sum(res_flat * res_flat)
     total = grid_sum(pack([hist_gram, last_row, last]), 2).reshape(-1)
-    gram = jnp.zeros((depth + 1, depth + 1), jnp.float32)
-    gram = gram.at[:depth, :depth].set(total[: depth * depth].reshape(depth, depth))
     row = total[depth * depth : depth * depth + depth]
-    gram = gram.at[depth, :depth].set(row).at[:depth, depth].set(row)
-    gram = gram.at[depth, depth].set(total[depth * depth + depth])
+    top = jnp.concatenate([total[: depth * depth].reshape(depth, depth), row[:, None]], 1)
+    bottom = jnp.concatenate([row, total[depth * depth + depth :][:1]])[None]
+    gram = jnp.concatenate([top, bottom], 0)
     lower = jnp.linalg.cholesky(gram)
     solved = jax.scipy.linalg.cho_solve((lower, True), jnp.ones((depth + 1,), jnp.float32))
     coefficients = solved / jnp.sum(solved)

time: 199 us -> 186 us (0.935)
  Pallas kernels: 101 us -> 80.4 us
  waiting for transfers between devices: 15.3 us -> 29.5 us
  local copies, waits for them, and re-layouts: 10.4 us -> 5.66 us
    pallas_call x2, Pallas kernels: 59.3 us -> 38.8 us  [grid_sum(): pl.pallas_call(functools.partial(_grid_sum_kernel, n), out_shape=jax.Shap...]
    ppermute x3, waiting for transfers between devices: 5.15 us -> 19.5 us  [partner(): return lax.ppermute(value, axis, pairs)]
    another operation x3 -> x0, other arithmetic: 3.28 us -> none
    scatter x5 -> x0, local copies, waits for them, and re-layouts: 2.49 us -> none  [the longest x2 1.6 us: local(): gram = gram.at[depth, :depth].set(row).at[:depth, depth].set(row)]
  transfers between devices with their start and end apart: 9 -> 9, of which waited for: 7 -> 8; matrix products, arithmetic and copies ran while one was open for 6% -> 6% of each run, Pallas kernels for 18% -> 9%
where the time goes in v5:
time: 186 us
  Pallas kernels  80.4 us (43%)
  starting transfers between devices  42.3 us (23%)
  waiting for transfers between devices  29.5 us (16%)
  other arithmetic  21.3 us (11%)
  local copies, waits for them, and re-layouts  5.66 us (3%)
  matrix products  3.44 us (2%)
  between operations  3.02 us (2%)
    pallas_call x1, Pallas kernels, band_sum(): pl.pallas_call(_band_sum_kernel, out_shape=jax.ShapeDtypeStruct(part.shap...  41.5 us
    pallas_call x2, Pallas kernels, grid_sum(): pl.pallas_call(functools.partial(_grid_sum_kernel, n), out_shape=jax.Shap...  38.8 us
    ppermute x6, starting transfers between devices, shifted(): return lax.ppermute(block, axis, route)  31.5 us
    ppermute x3, waiting for transfers between devices, partner(): return lax.ppermute(value, axis, pairs)  19.5 us
    ppermute x3, starting transfers between devices, partner(): return lax.ppermute(value, axis, pairs)  10.8 us
    ppermute x6, waiting for transfers between devices, shifted(): return lax.ppermute(block, axis, route)  9.99 us
  transfers between devices with their start and end apart: 9, of which 8 were waited for; matrix products, arithmetic and copies ran while one was open for 6% of the time, Pallas kernels for 9%

profile of v5, /device:TPU:8, one launch (start us, length us, event | category | flops | bytes accessed | tf_op | source)
XLA Modules:
  0.0 185.6 jit_solution(3797913045395990804)
XLA Ops:
  0.7 2.1 %fusion.x_ref = f32[16,32,128]{2,1,0:T(8,128)} fusion(bf16[4,1,16,32,128]{4,3,2,1,0:T(8,128)(2,1)} %param.6, f32[4]{0:T(128)} %param.7), kind=kLoop, calls=%fused_computation.12 | loop fusion | flops 983040 | bytes 786448 | tf_op jit(solution)/shard_map/reduce_sum | solution.py:210
  2.8 41.5 %shard_map.77 = f32[16,32,128]{2,1,0:T(8,128)} custom-call(f32[16,32,128]{2,1,0:T(8,128)} %fusion.x_ref), custom_call_target="tpu_custom_call" | custom-call | tf_op jit(solution)/shard_map/pallas_call | solution.py:164
  44.4 3.6 %collective-permute-start = (f32[1,16,32,128]{3,2,1,0:T(8,128)}, f32[1,16,32,128]{3,2,1,0:T(8,128)S(1)}, u32[]{:S(2)}, u32[]{:S(2)}) collective-permute-start(f32[1,16,32,128]{3,2,1,0:T(8,128)} %bitcast.85), channel_id=1, source_target_pairs={{0,384},{8,392},{16,400},{24,408},{32,416},{40,424},{48,432},{56,4... | collective-permute-start | bytes 786440 | tf_op jit(solution)/shard_map/ppermute | solution.py:188
  48.0 1.7 reduce_sum.65
  49.7 1.6 reduce_sum.66
  51.3 1.9 %fusion.31.x_ref = f32[8,128]{1,0:T(8,128)} fusion(f32[1]{0:T(128)} %bitcast.2, f32[1]{0:T(128)} %bitcast.1), kind=kLoop, calls=%fused_computation.89 | loop fusion | flops 4096 | bytes 4104 | tf_op jit(solution)/shard_map/reshape | solution.py:183
  53.2 16.2 %shard_map.78 = f32[8,128]{1,0:T(8,128)} custom-call(f32[8,128]{1,0:T(8,128)} %fusion.31.x_ref), custom_call_target="tpu_custom_call" | custom-call | tf_op jit(solution)/shard_map/pallas_call | solution.py:87
  70.1 5.3 %collective-permute-start.1 = (f32[1,16,32,128]{3,2,1,0:T(8,128)S(1)}, f32[1,16,32,128]{3,2,1,0:T(8,128)S(1)}, u32[]{:S(2)}, u32[]{:S(2)}) collective-permute-start(f32[1,16,32,128]{3,2,1,0:T(8,128)S(1)} %add_multiply_fusion.1), channel_id=1, source_target_pairs={{0,96},{8,104},{16,112},{24,120},{32,64},{40,72},{48,80},{56,88},{... | collective-permute-start | bytes 786440 | tf_op jit(solution)/shard_map/ppermute | solution.py:188
  75.4 1.7 multiply_reduce_fusion
  77.1 13.8 %collective-permute-done.1 = f32[1,16,32,128]{3,2,1,0:T(8,128)S(1)} collective-permute-done((f32[1,16,32,128]{3,2,1,0:T(8,128)S(1)}, f32[1,16,32,128]{3,2,1,0:T(8,128)S(1)}, u32[]{:S(2)}, u32[]{:S(2)}) %collective-permute-start.1) | collective-permute-done | bytes 262176 | tf_op jit(solution)/shard_map/ppermute | solution.py:188
  91.0 1.9 %collective-permute-start.2 = (f32[1,16,32,128]{3,2,1,0:T(8,128)S(1)}, f32[1,16,32,128]{3,2,1,0:T(8,128)S(1)}, u32[]{:S(2)}, u32[]{:S(2)}) collective-permute-start(f32[1,16,32,128]{3,2,1,0:T(8,128)S(1)} %add_multiply_fusion), channel_id=1, source_target_pairs={{0,24},{8,16},{16,8},{24,0},{32,56},{40,48},{48,40},{56,32},{64,88... | collective-permute-start | bytes 786440 | tf_op jit(solution)/shard_map/ppermute | solution.py:188
  92.9 1.3 fusion.39
  95.7 5.7 %collective-permute-done.2 = f32[1,16,32,128]{3,2,1,0:T(8,128)S(1)} collective-permute-done((f32[1,16,32,128]{3,2,1,0:T(8,128)S(1)}, f32[1,16,32,128]{3,2,1,0:T(8,128)S(1)}, u32[]{:S(2)}, u32[]{:S(2)}) %collective-permute-start.2) | collective-permute-done | bytes 262176 | tf_op jit(solution)/shard_map/ppermute | solution.py:188
  101.6 0.8 multiply_reduce_fusion.2
  102.7 1.4 fusion.30.x_ref
  104.0 22.6 %shard_map.79 = f32[8,128]{1,0:T(8,128)} custom-call(f32[8,128]{1,0:T(8,128)} %fusion.30.x_ref), custom_call_target="tpu_custom_call" | custom-call | tf_op jit(solution)/shard_map/pallas_call | solution.py:87
  128.2 0.8 slice.146
  129.3 0.8 cholesky.16
  134.4 1.3 fusion.1
  136.4 2.5 %collective-permute-start.3 = (f32[3,32,128]{2,1,0:T(8,128)S(1)}, f32[3,32,128]{2,1,0:T(8,128)S(1)}, u32[]{:S(2)}, u32[]{:S(2)}) collective-permute-start(f32[3,32,128]{2,1,0:T(8,128)S(1)} %get-tuple-element.14), channel_id=1, source_target_pairs={{0,128},{8,136},{16,144},{24,152},{32,160},{40,168},{48,176},{56,1... | collective-permute-start | bytes 147464 | tf_op jit(solution)/shard_map/ppermute | solution.py:194
  139.0 3.3 %collective-permute-start.4 = (f32[3,32,128]{2,1,0:T(8,128)S(1)}, f32[3,32,128]{2,1,0:T(8,128)S(1)}, u32[]{:S(2)}, u32[]{:S(2)}) collective-permute-start(f32[3,32,128]{2,1,0:T(8,128)S(1)} %get-tuple-element.15), channel_id=1, source_target_pairs={{128,0},{136,8},{144,16},{152,24},{160,32},{168,40},{176,48},{184,... | collective-permute-start | bytes 147464 | tf_op jit(solution)/shard_map/ppermute | solution.py:194
  142.4 2.5 %collective-permute-done.4 = f32[3,32,128]{2,1,0:T(8,128)S(1)} collective-permute-done((f32[3,32,128]{2,1,0:T(8,128)S(1)}, f32[3,32,128]{2,1,0:T(8,128)S(1)}, u32[]{:S(2)}, u32[]{:S(2)}) %collective-permute-start.4) | collective-permute-done | bytes 49184 | tf_op jit(solution)/shard_map/ppermute | solution.py:194
  145.0 2.7 %collective-permute-start.5 = (f32[22,3,128]{2,1,0:T(4,128)S(1)}, f32[22,3,128]{2,1,0:T(4,128)S(1)}, u32[]{:S(2)}, u32[]{:S(2)}) collective-permute-start(f32[22,3,128]{2,1,0:T(4,128)S(1)} %get-tuple-element.12), channel_id=1, source_target_pairs={{0,32},{8,40},{16,48},{24,56},{32,64},{40,72},{48,80},{56,88},{64,... | collective-permute-start | bytes 101384 | tf_op jit(solution)/shard_map/ppermute | solution.py:194
  148.5 9.8 %collective-permute-start.6 = (f32[22,3,128]{2,1,0:T(4,128)S(1)}, f32[22,3,128]{2,1,0:T(4,128)S(1)}, u32[]{:S(2)}, u32[]{:S(2)}) collective-permute-start(f32[22,3,128]{2,1,0:T(4,128)S(1)} %get-tuple-element.13), channel_id=1, source_target_pairs={{32,0},{40,8},{48,16},{56,24},{64,32},{72,40},{80,48},{88,56},{96,... | collective-permute-start | bytes 101384 | tf_op jit(solution)/shard_map/ppermute | solution.py:194
  158.7 1.3 collective-permute-done.6
  160.3 1.9 %collective-permute-start.7 = (f32[22,38,3]{2,1,0:T(8,128)S(1)}, f32[22,38,3]{2,1,0:T(8,128)S(1)}, u32[]{:S(2)}, u32[]{:S(2)}) collective-permute-start(f32[22,38,3]{2,1,0:T(8,128)S(1)} %get-tuple-element.10), channel_id=1, source_target_pairs={{0,8},{8,16},{16,24},{24,32},{32,40},{40,48},{48,56},{56,64},{64,7... | collective-permute-start | bytes 30104 | tf_op jit(solution)/shard_map/ppermute | solution.py:194
  162.2 1.3 fusion.3
  163.5 11.3 %collective-permute-start.8 = (f32[22,38,3]{2,1,0:T(8,128)S(1)}, f32[22,38,3]{2,1,0:T(8,128)S(1)}, u32[]{:S(2)}, u32[]{:S(2)}) collective-permute-start(f32[22,38,3]{2,1,0:T(8,128)S(1)} %get-tuple-element.11), channel_id=1, source_target_pairs={{8,0},{16,8},{24,16},{32,24},{40,32},{48,40},{56,48},{64,56},{72,6... | collective-permute-start | bytes 30104 | tf_op jit(solution)/shard_map/ppermute | solution.py:194
  174.8 2.9 %collective-permute-done.7 = f32[22,38,3]{2,1,0:T(8,128)S(1)} collective-permute-done((f32[22,38,3]{2,1,0:T(8,128)S(1)}, f32[22,38,3]{2,1,0:T(8,128)S(1)}, u32[]{:S(2)}, u32[]{:S(2)}) %collective-permute-start.7) | collective-permute-done | bytes 10064 | tf_op jit(solution)/shard_map/ppermute | solution.py:194
  177.8 2.7 %collective-permute-done.8 = f32[22,38,3]{2,1,0:T(8,128)S(1)} collective-permute-done((f32[22,38,3]{2,1,0:T(8,128)S(1)}, f32[22,38,3]{2,1,0:T(8,128)S(1)}, u32[]{:S(2)}, u32[]{:S(2)}) %collective-permute-start.8) | collective-permute-done | bytes 10064 | tf_op jit(solution)/shard_map/ppermute | solution.py:194
  180.6 1.0 fusion.12
  183.6 2.0 %fusion.25 = f32[1,16,32,128]{3,2,1,0:T(8,128)} fusion(f32[1,16,32,128]{3,2,1,0:T(8,128)S(1)} %multiply_add_fusion, f32[22,38,134]{2,1,0:T(8,128)S(1)} %get-tuple-element.3, f32[22,38,134]{2,1,0:T(8,128)S(1)} %get-tuple-element.9, f32[22,38,134]{2,1,0:T(8,128)S(1)} %get-tuple-element.8, f32[22,38,134]{2,1,0:T(8,128)S(1)} %get-tuple-element.7, ...), kind=kLoop, calls=%fused_computation.56 | loop fusion | flops 786432 | bytes 2424844 | tf_op jit(solution)/shard_map/add | solution.py:279
  (53 shorter events, 11.3 us)
Async XLA Ops:
  0.6 161.6 %copy-start = (bf16[8,1,16,32,128]{4,3,2,1,0:T(8,128)(2,1)S(1)}, bf16[8,1,16,32,128]{4,3,2,1,0:T(8,128)(2,1)}, u32[]{:S(2)}) copy-start(bf16[8,1,16,32,128]{4,3,2,1,0:T(8,128)(2,1)} %param.9) | copy-start | bytes 3145732
  0.6 68.8 %copy-start.1 = (bf16[8,1,16,32,128]{4,3,2,1,0:T(8,128)(2,1)S(1)}, bf16[8,1,16,32,128]{4,3,2,1,0:T(8,128)(2,1)}, u32[]{:S(2)}) copy-start(bf16[8,1,16,32,128]{4,3,2,1,0:T(8,128)(2,1)} %param.10) | copy-start | bytes 3145732
  44.3 25.7 %copy-start.4 = (f32[16,32,128]{2,1,0:T(8,128)S(1)}, f32[16,32,128]{2,1,0:T(8,128)}, u32[]{:S(2)}) copy-start(f32[16,32,128]{2,1,0:T(8,128)} %shard_map.77) | copy-start | bytes 786436
  44.4 25.7 %collective-permute-start = (f32[1,16,32,128]{3,2,1,0:T(8,128)}, f32[1,16,32,128]{3,2,1,0:T(8,128)S(1)}, u32[]{:S(2)}, u32[]{:S(2)}) collective-permute-start(f32[1,16,32,128]{3,2,1,0:T(8,128)} %bitcast.85), channel_id=1, source_target_pairs={{0,384},{8,392},{16,400},{24,408},{32,416},{40,424},{48,432},{56,4... | collective-permute-start | bytes 786440 | tf_op jit(solution)/shard_map/ppermute | solution.py:188
  70.1 20.8 %collective-permute-start.1 = (f32[1,16,32,128]{3,2,1,0:T(8,128)S(1)}, f32[1,16,32,128]{3,2,1,0:T(8,128)S(1)}, u32[]{:S(2)}, u32[]{:S(2)}) collective-permute-start(f32[1,16,32,128]{3,2,1,0:T(8,128)S(1)} %add_multiply_fusion.1), channel_id=1, source_target_pairs={{0,96},{8,104},{16,112},{24,120},{32,64},{40,72},{48,80},{56,88},{... | collective-permute-start | bytes 786440 | tf_op jit(solution)/shard_map/ppermute | solution.py:188
  75.4 26.1 %copy-start.2 = (f32[1,16,32,128]{3,2,1,0:T(8,128)S(1)}, f32[1,16,32,128]{3,2,1,0:T(8,128)}, u32[]{:S(2)}) copy-start(f32[1,16,32,128]{3,2,1,0:T(8,128)} %param.8) | copy-start | bytes 786436
  91.0 10.4 %collective-permute-start.2 = (f32[1,16,32,128]{3,2,1,0:T(8,128)S(1)}, f32[1,16,32,128]{3,2,1,0:T(8,128)S(1)}, u32[]{:S(2)}, u32[]{:S(2)}) collective-permute-start(f32[1,16,32,128]{3,2,1,0:T(8,128)S(1)} %add_multiply_fusion), channel_id=1, source_target_pairs={{0,24},{8,16},{16,8},{24,0},{32,56},{40,48},{48,40},{56,32},{64,88... | collective-permute-start | bytes 786440 | tf_op jit(solution)/shard_map/ppermute | solution.py:188
  102.3 42.6 %copy-start.3 = (f32[1,16,32,128]{3,2,1,0:T(8,128)}, f32[1,16,32,128]{3,2,1,0:T(8,128)S(1)}, u32[]{:S(2)}) copy-start(f32[1,16,32,128]{3,2,1,0:T(8,128)S(1)} %get-tuple-element.5) | copy-start | bytes 786436
  136.4 6.0 %collective-permute-start.3 = (f32[3,32,128]{2,1,0:T(8,128)S(1)}, f32[3,32,128]{2,1,0:T(8,128)S(1)}, u32[]{:S(2)}, u32[]{:S(2)}) collective-permute-start(f32[3,32,128]{2,1,0:T(8,128)S(1)} %get-tuple-element.14), channel_id=1, source_target_pairs={{0,128},{8,136},{16,144},{24,152},{32,160},{40,168},{48,176},{56,1... | collective-permute-start | bytes 147464 | tf_op jit(solution)/shard_map/ppermute | solution.py:194
  139.0 6.0 %collective-permute-start.4 = (f32[3,32,128]{2,1,0:T(8,128)S(1)}, f32[3,32,128]{2,1,0:T(8,128)S(1)}, u32[]{:S(2)}, u32[]{:S(2)}) collective-permute-start(f32[3,32,128]{2,1,0:T(8,128)S(1)} %get-tuple-element.15), channel_id=1, source_target_pairs={{128,0},{136,8},{144,16},{152,24},{160,32},{168,40},{176,48},{184,... | collective-permute-start | bytes 147464 | tf_op jit(solution)/shard_map/ppermute | solution.py:194
  145.0 13.7 %collective-permute-start.5 = (f32[22,3,128]{2,1,0:T(4,128)S(1)}, f32[22,3,128]{2,1,0:T(4,128)S(1)}, u32[]{:S(2)}, u32[]{:S(2)}) collective-permute-start(f32[22,3,128]{2,1,0:T(4,128)S(1)} %get-tuple-element.12), channel_id=1, source_target_pairs={{0,32},{8,40},{16,48},{24,56},{32,64},{40,72},{48,80},{56,88},{64,... | collective-permute-start | bytes 101384 | tf_op jit(solution)/shard_map/ppermute | solution.py:194
  148.5 11.5 %collective-permute-start.6 = (f32[22,3,128]{2,1,0:T(4,128)S(1)}, f32[22,3,128]{2,1,0:T(4,128)S(1)}, u32[]{:S(2)}, u32[]{:S(2)}) collective-permute-start(f32[22,3,128]{2,1,0:T(4,128)S(1)} %get-tuple-element.13), channel_id=1, source_target_pairs={{32,0},{40,8},{48,16},{56,24},{64,32},{72,40},{80,48},{88,56},{96,... | collective-permute-start | bytes 101384 | tf_op jit(solution)/shard_map/ppermute | solution.py:194
  160.3 17.5 %collective-permute-start.7 = (f32[22,38,3]{2,1,0:T(8,128)S(1)}, f32[22,38,3]{2,1,0:T(8,128)S(1)}, u32[]{:S(2)}, u32[]{:S(2)}) collective-permute-start(f32[22,38,3]{2,1,0:T(8,128)S(1)} %get-tuple-element.10), channel_id=1, source_target_pairs={{0,8},{8,16},{16,24},{24,32},{32,40},{40,48},{48,56},{56,64},{64,7... | collective-permute-start | bytes 30104 | tf_op jit(solution)/shard_map/ppermute | solution.py:194
  163.5 17.0 %collective-permute-start.8 = (f32[22,38,3]{2,1,0:T(8,128)S(1)}, f32[22,38,3]{2,1,0:T(8,128)S(1)}, u32[]{:S(2)}, u32[]{:S(2)}) collective-permute-start(f32[22,38,3]{2,1,0:T(8,128)S(1)} %get-tuple-element.11), channel_id=1, source_target_pairs={{8,0},{16,8},{24,16},{32,24},{40,32},{48,40},{56,48},{64,56},{72,6... | collective-permute-start | bytes 30104 | tf_op jit(solution)/shard_map/ppermute | solution.py:194

commit v6 on v5

--- a/solution.py
+++ b/solution.py
@@ -99,80 +99,136 @@
     )(vec)
 
 
-def _band_sum_kernel(x_ref, o_ref, q_in, q_sum, e_in, t_quarter, full, s1, r1, s2, r2, s3, r3, s4, r4):
+def reverse(x, axis):
+    n = x.shape[axis]
+    idx = lax.broadcasted_iota(jnp.int32, x.shape, axis)
+    k = 1
+    while k < n:
+        bit = (idx // k) % 2
+        want = idx + k * (1 - 2 * bit)
+        came = pltpu.roll(idx, k, axis)
+        x = jnp.where(came == want, pltpu.roll(x, k, axis), pltpu.roll(x, n - k, axis))
+        k *= 2
+    return x
+
+
+def _density_kernel(p_ref, o_ref, q_in, q_sum, e_in, e_buf, ax_in, a_buf, ay_in, b_buf, bz_in, s_buf, tq, full,
+                    s1, r1, s2, r2, sx, rx, sy, ry, sz, rz, s6, r6, s7, r7):
     g = lax.axis_index("grid")
     b = lax.axis_index("band")
     zhi = b // 4
     x = b % 4
     other = (1 - zhi) * 4 + x
+    bx = g // 16
+    by = g // 4 % 4
+    bz = g % 4
+    gx = g + (3 - 2 * bx) * 16
+    gy = g + (3 - 2 * by) * 4
+    gz = g + (3 - 2 * bz)
+    rows = p_ref.shape[0]
     barrier = pltpu.get_barrier_semaphore()
     for k in range(1, 4):
         pl.semaphore_signal(barrier, inc=1, device_id=(g, zhi * 4 + lax.rem(x + k, 4)), device_id_type=MESH)
     pl.semaphore_signal(barrier, inc=1, device_id=(g, other), device_id_type=MESH)
-    pl.semaphore_wait(barrier, 4)
-
-    def remote(src, dst, ssem, rsem, peer):
+    pl.semaphore_signal(barrier, inc=1, device_id=(gx, b), device_id_type=MESH)
+    pl.semaphore_signal(barrier, inc=1, device_id=(gy, b), device_id_type=MESH)
+    pl.semaphore_signal(barrier, inc=1, device_id=(gz, b), device_id_type=MESH)
+    pl.semaphore_wait(barrier, 7)
+
+    def remote(src, dst, ssem, rsem, dev):
         return pltpu.make_async_remote_copy(
-            src_ref=src, dst_ref=dst, send_sem=ssem, recv_sem=rsem, device_id=(g, peer), device_id_type=MESH
+            src_ref=src, dst_ref=dst, send_sem=ssem, recv_sem=rsem, device_id=dev, device_id_type=MESH
         )
 
-    q = x_ref.shape[0] // 4
-    e = q // 2
-    out1 = []
+    def low(q):
+        return pl.ds(2 * q, 2)
+
+    def high(q):
+        return pl.ds(rows - 2 - 2 * q, 2)
+
     for k in range(1, 4):
         px = lax.rem(x + k, 4)
-        c = remote(x_ref.at[pl.ds(px * q, q)], q_in.at[x], s1.at[k], r1.at[x], zhi * 4 + px)
-        c.start()
-        out1.append(c)
-    q_in[x] = x_ref[pl.ds(x * q, q)]
-    for c in out1:
-        c.wait_send()
-    for k in range(1, 4):
-        sx = lax.rem(x + k, 4)
-        remote(x_ref.at[pl.ds(0, q)], q_in.at[sx], s1.at[k], r1.at[sx], zhi * 4 + sx).wait_recv()
+        dev = (g, zhi * 4 + px)
+        remote(p_ref.at[low(px)], q_in.at[x, pl.ds(0, 2)], s1.at[k, 0], r1.at[x, 0], dev).start()
+        remote(p_ref.at[high(px)], q_in.at[x, pl.ds(2, 2)], s1.at[k, 1], r1.at[x, 1], dev).start()
+    q_in[x, pl.ds(0, 2)] = p_ref[low(x)]
+    q_in[x, pl.ds(2, 2)] = p_ref[high(x)]
+    for k in range(1, 4):
+        px = lax.rem(x + k, 4)
+        dev = (g, zhi * 4 + px)
+        remote(p_ref.at[low(px)], q_in.at[x, pl.ds(0, 2)], s1.at[k, 0], r1.at[x, 0], dev).wait_send()
+        remote(p_ref.at[high(px)], q_in.at[x, pl.ds(2, 2)], s1.at[k, 1], r1.at[x, 1], dev).wait_send()
+        remote(p_ref.at[low(px)], q_in.at[px, pl.ds(0, 2)], s1.at[k, 0], r1.at[px, 0], dev).wait_recv()
+        remote(p_ref.at[high(px)], q_in.at[px, pl.ds(2, 2)], s1.at[k, 1], r1.at[px, 1], dev).wait_recv()
     q_sum[...] = ((q_in[0] + q_in[1]) + q_in[2]) + q_in[3]
-    c2 = remote(q_sum.at[pl.ds((1 - zhi) * e, e)], e_in.at[zhi], s2, r2, other)
-    c2.start()
-    e_in[zhi] = q_sum[pl.ds(zhi * e, e)]
-    c2.wait_send()
-    remote(q_sum.at[pl.ds(0, e)], e_in.at[1 - zhi], s2, r2, other).wait_recv()
-    t_quarter[pl.ds(zhi * e, e)] = e_in[0] + e_in[1]
-    c3 = remote(t_quarter.at[pl.ds(zhi * e, e)], t_quarter.at[pl.ds(zhi * e, e)], s3, r3, other)
-    c3.start()
-    c3.wait_send()
-    remote(t_quarter.at[pl.ds(0, e)], t_quarter.at[pl.ds((1 - zhi) * e, e)], s3, r3, other).wait_recv()
-    out4 = []
+    dev = (g, other)
+    c_a = remote(q_sum.at[pl.ds(1 - zhi, 1)], e_in.at[zhi, pl.ds(0, 1)], s2.at[0], r2.at[zhi, 0], dev)
+    c_b = remote(q_sum.at[pl.ds(2 + zhi, 1)], e_in.at[zhi, pl.ds(1, 1)], s2.at[1], r2.at[zhi, 1], dev)
+    c_a.start()
+    c_b.start()
+    e_in[zhi, pl.ds(0, 1)] = q_sum[pl.ds(zhi, 1)]
+    e_in[zhi, pl.ds(1, 1)] = q_sum[pl.ds(3 - zhi, 1)]
+    c_a.wait_send()
+    c_b.wait_send()
+    remote(q_sum.at[pl.ds(0, 1)], e_in.at[1 - zhi, pl.ds(0, 1)], s2.at[0], r2.at[1 - zhi, 0], dev).wait_recv()
+    remote(q_sum.at[pl.ds(0, 1)], e_in.at[1 - zhi, pl.ds(1, 1)], s2.at[1], r2.at[1 - zhi, 1], dev).wait_recv()
+    e_buf[...] = e_in[0] + e_in[1]
+    c_x = remote(e_buf, ax_in, sx, rx, (gx, b))
+    c_x.start()
+    c_x.wait_send()
+    c_x.wait_recv()
+    a_buf[0] = 0.5 * (e_buf[0] + ax_in[1])
+    a_buf[1] = 0.5 * (e_buf[1] + ax_in[0])
+    c_y = remote(a_buf, ay_in, sy, ry, (gy, b))
+    c_y.start()
+    c_y.wait_send()
+    c_y.wait_recv()
+    b_buf[...] = 0.5 * (a_buf[...] + reverse(ay_in[...], 1))
+    c_z = remote(b_buf, bz_in, sz, rz, (gz, b))
+    c_z.start()
+    c_z.wait_send()
+    c_z.wait_recv()
+    s_buf[...] = 0.5 * (b_buf[...] + reverse(bz_in[...], 2))
+    c_a = remote(s_buf.at[pl.ds(0, 1)], tq.at[pl.ds(zhi, 1)], s6.at[0], r6.at[0], dev)
+    c_b = remote(s_buf.at[pl.ds(1, 1)], tq.at[pl.ds(3 - zhi, 1)], s6.at[1], r6.at[1], dev)
+    c_a.start()
+    c_b.start()
+    tq[pl.ds(zhi, 1)] = s_buf[pl.ds(0, 1)]
+    tq[pl.ds(3 - zhi, 1)] = s_buf[pl.ds(1, 1)]
+    c_a.wait_send()
+    c_b.wait_send()
+    remote(s_buf.at[pl.ds(0, 1)], tq.at[pl.ds(1 - zhi, 1)], s6.at[0], r6.at[0], dev).wait_recv()
+    remote(s_buf.at[pl.ds(1, 1)], tq.at[pl.ds(2 + zhi, 1)], s6.at[1], r6.at[1], dev).wait_recv()
     for k in range(1, 4):
         px = lax.rem(x + k, 4)
-        c = remote(t_quarter, full.at[pl.ds(x * q, q)], s4.at[k], r4.at[x], zhi * 4 + px)
-        c.start()
-        out4.append(c)
-    full[pl.ds(x * q, q)] = t_quarter[...]
-    for c in out4:
-        c.wait_send()
-    for k in range(1, 4):
-        sx = lax.rem(x + k, 4)
-        remote(t_quarter, full.at[pl.ds(sx * q, q)], s4.at[k], r4.at[sx], zhi * 4 + sx).wait_recv()
+        dev = (g, zhi * 4 + px)
+        remote(tq.at[pl.ds(0, 2)], full.at[low(x)], s7.at[k, 0], r7.at[x, 0], dev).start()
+        remote(tq.at[pl.ds(2, 2)], full.at[high(x)], s7.at[k, 1], r7.at[x, 1], dev).start()
+    full[low(x)] = tq[pl.ds(0, 2)]
+    full[high(x)] = tq[pl.ds(2, 2)]
+    for k in range(1, 4):
+        px = lax.rem(x + k, 4)
+        dev = (g, zhi * 4 + px)
+        remote(tq.at[pl.ds(0, 2)], full.at[low(x)], s7.at[k, 0], r7.at[x, 0], dev).wait_send()
+        remote(tq.at[pl.ds(2, 2)], full.at[high(x)], s7.at[k, 1], r7.at[x, 1], dev).wait_send()
+        remote(tq.at[pl.ds(0, 2)], full.at[low(px)], s7.at[k, 0], r7.at[px, 0], dev).wait_recv()
+        remote(tq.at[pl.ds(2, 2)], full.at[high(px)], s7.at[k, 1], r7.at[px, 1], dev).wait_recv()
     o_ref[...] = full[...]
 
 
-def band_sum(part):
-    rows = part.shape[0]
-    q, e = rows // 4, rows // 8
+def symmetric_density(part):
     rest = part.shape[1:]
     dma = pltpu.SemaphoreType.DMA
+    vm = lambda *s: pltpu.VMEM(s + rest, jnp.float32)
     return pl.pallas_call(
-        _band_sum_kernel,
+        _density_kernel,
         out_shape=jax.ShapeDtypeStruct(part.shape, jnp.float32),
         in_specs=[pl.BlockSpec(memory_space=pltpu.VMEM)],
         out_specs=pl.BlockSpec(memory_space=pltpu.VMEM),
         scratch_shapes=[
-            pltpu.VMEM((4, q) + rest, jnp.float32),
-            pltpu.VMEM((q,) + rest, jnp.float32),
-            pltpu.VMEM((2, e) + rest, jnp.float32),
-            pltpu.VMEM((q,) + rest, jnp.float32),
-            pltpu.VMEM(part.shape, jnp.float32),
-            dma((4,)), dma((4,)), dma(()), dma(()), dma(()), dma(()), dma((4,)), dma((4,)),
+            vm(4, 4), vm(4), vm(2, 2), vm(2), vm(2), vm(2), vm(2), vm(2), vm(2), vm(2), vm(4), vm(part.shape[0]),
+            dma((4, 2)), dma((4, 2)), dma((2,)), dma((2, 2)), dma(()), dma(()), dma(()), dma(()), dma(()), dma(()),
+            dma((2,)), dma((2,)), dma((4, 2)), dma((4, 2)),
         ],
         compiler_params=pltpu.CompilerParams(collective_id=3, has_side_effects=True),
     )(part)
@@ -208,9 +264,8 @@
 def local(orbitals, occupations, density_in, history_in, history_res, screening):
     waves = orbitals.astype(jnp.float32)
     partial_value = jnp.sum(occupations[:, None, None, None, None] * waves * waves, 0)
-    rho_out = band_sum(partial_value[0])[None]
-    charges = grid_sum(pack([jnp.sum(rho_out), jnp.sum(density_in)]), 1)
-    rho_sym = symmetrize(rho_out)
+    rho_sym = symmetric_density(partial_value[0])[None]
+    charges = grid_sum(pack([jnp.sum(rho_sym), jnp.sum(density_in)]), 1)
     depth = history_res.shape[0]
     res_hist = history_res.astype(jnp.float32)
     hist_flat = res_hist.reshape(depth, -1)

time: 186 us -> 162 us (0.87)
  waiting for transfers between devices: 29.5 us -> 8.62 us
  starting transfers between devices: 42.3 us -> 31.5 us
  Pallas kernels: 80.4 us -> 87 us
    ppermute x3 -> x0, waiting for transfers between devices: 19.5 us -> none  [partner(): return lax.ppermute(value, axis, pairs)]
    pallas_call x1, Pallas kernels: 41.5 us -> 54.3 us  [symmetric_density(): pl.pallas_call(_density_kernel, out_shape=jax.ShapeDtypeStruct(part.shape...]
    ppermute x3 -> x0, starting transfers between devices: 10.8 us -> none  [partner(): return lax.ppermute(value, axis, pairs)]
    pallas_call x2, Pallas kernels: 38.8 us -> 32.6 us  [grid_sum(): pl.pallas_call(functools.partial(_grid_sum_kernel, n), out_shape=jax.Shap...]
  transfers between devices with their start and end apart: 9 -> 6, of which waited for: 8 -> 5; matrix products, arithmetic and copies ran while one was open for 6% -> 1% of each run, Pallas kernels for 9% -> 0%
where the time goes in v6:
time: 162 us; the launch traced here: 161 us
  Pallas kernels  87 us (54%)
  starting transfers between devices  31.5 us (19%)
  other arithmetic  22.2 us (14%)
  waiting for transfers between devices  8.62 us (5%)
  local copies, waits for them, and re-layouts  5.78 us (4%)
  matrix products  3.43 us (2%)
  between operations  2.97 us (2%)
    pallas_call x1, Pallas kernels, symmetric_density(): pl.pallas_call(_density_kernel, out_shape=jax.ShapeDtypeStruct(part.shape...  54.3 us
    pallas_call x2, Pallas kernels, grid_sum(): pl.pallas_call(functools.partial(_grid_sum_kernel, n), out_shape=jax.Shap...  32.6 us
    ppermute x6, starting transfers between devices, shifted(): return lax.ppermute(block, axis, route)  31.5 us
    ppermute x6, waiting for transfers between devices, shifted(): return lax.ppermute(block, axis, route)  8.62 us
    reduce_sum x2, other arithmetic, local(): charges = grid_sum(pack([jnp.sum(rho_sym), jnp.sum(density_in)]), 1)  3.3 us
  transfers between devices with their start and end apart: 6, of which 5 were waited for; matrix products, arithmetic and copies ran while one was open for 1% of the time, Pallas kernels for 0%

profile of v6, /device:TPU:8, one launch (start us, length us, event | category | flops | bytes accessed | tf_op | source)
XLA Modules:
  0.0 161.5 jit_solution(6156856390287368457)
XLA Ops:
  0.7 2.1 %fusion.p_ref = f32[16,32,128]{2,1,0:T(8,128)} fusion(bf16[4,1,16,32,128]{4,3,2,1,0:T(8,128)(2,1)} %param.6, f32[4]{0:T(128)} %param.7), kind=kLoop, calls=%fused_computation.12 | loop fusion | flops 983040 | bytes 786448 | tf_op jit(solution)/shard_map/reduce_sum | solution.py:266
  2.8 54.3 %shard_map.77 = f32[16,32,128]{2,1,0:T(8,128)} custom-call(f32[16,32,128]{2,1,0:T(8,128)} %fusion.p_ref), custom_call_target="tpu_custom_call" | custom-call | tf_op jit(solution)/shard_map/pallas_call | solution.py:223
  57.1 1.7 %reduce_sum.65 = f32[]{:T(128)} reduce(f32[16,32,128]{2,1,0:T(8,128)} %shard_map.77, f32[]{:T(128)} %constant.104.clone.1), dimensions={0,1,2}, to_apply=%region_2.0 | reduce | flops 65535 | bytes 262152 | tf_op jit(solution)/shard_map/reduce_sum | solution.py:268
  58.8 1.6 %reduce_sum.66 = f32[]{:T(128)} reduce(f32[1,16,32,128]{3,2,1,0:T(8,128)} %param.8, f32[]{:T(128)} %constant.104.clone.1), dimensions={0,1,2,3}, to_apply=%region_3.4 | reduce | flops 65535 | bytes 262152 | tf_op jit(solution)/shard_map/reduce_sum | solution.py:268
  60.4 1.9 %fusion.31.x_ref = f32[8,128]{1,0:T(8,128)} fusion(f32[1]{0:T(128)} %bitcast.1, f32[1]{0:T(128)} %bitcast), kind=kLoop, calls=%fused_computation.87 | loop fusion | flops 4096 | bytes 4104 | tf_op jit(solution)/shard_map/reshape | solution.py:239
  62.4 16.3 %shard_map.78 = f32[8,128]{1,0:T(8,128)} custom-call(f32[8,128]{1,0:T(8,128)} %fusion.31.x_ref), custom_call_target="tpu_custom_call" | custom-call | tf_op jit(solution)/shard_map/pallas_call | solution.py:87
  78.6 1.3 fusion.39
  81.3 1.8 %multiply_reduce_fusion.2 = (f32[]{:T(128)}, f32[1,16,32,128]{3,2,1,0:T(8,128)S(1)}) fusion(f32[1,16,32,128]{3,2,1,0:T(8,128)} %param.8, f32[16,32,128]{2,1,0:T(8,128)} %shard_map.77, f32[]{:T(128)} %bitcast.3), kind=kLoop, calls=%fused_computation.62 | loop fusion | flops 262143 | bytes 786440 | tf_op jit(solution)/shard_map/reduce_sum | solution.py:277
  84.0 1.7 %multiply_reduce_fusion = f32[8,8]{1,0:T(8,128)S(1)} fusion(f32[8,65536]{1,0:T(8,128)S(1)} %bitcast.79), kind=kLoop, calls=%fused_computation | loop fusion | flops 8388544 | bytes 2097408 | tf_op jit(solution)/shard_map/reduce_sum | solution.py:272
  85.8 1.3 fusion.30.x_ref
  87.1 16.4 %shard_map.79 = f32[8,128]{1,0:T(8,128)} custom-call(f32[8,128]{1,0:T(8,128)} %fusion.30.x_ref), custom_call_target="tpu_custom_call" | custom-call | tf_op jit(solution)/shard_map/pallas_call | solution.py:87
  103.5 0.8 slice_bitcast_fusion.2
  104.2 0.8 slice_bitcast_fusion.3
  105.0 0.8 slice.146
  106.2 0.8 cholesky.16
  109.2 0.8 fusion.40
  111.2 1.3 fusion.1
  112.5 0.7 multiply_add_fusion
  113.3 2.5 %collective-permute-start = (f32[3,32,128]{2,1,0:T(8,128)S(1)}, f32[3,32,128]{2,1,0:T(8,128)S(1)}, u32[]{:S(2)}, u32[]{:S(2)}) collective-permute-start(f32[3,32,128]{2,1,0:T(8,128)S(1)} %get-tuple-element.14), channel_id=1, source_target_pairs={{0,128},{8,136},{16,144},{24,152},{32,160},{40,168},{48,176},{56,1... | collective-permute-start | bytes 147464 | tf_op jit(solution)/shard_map/ppermute | solution.py:250
  115.8 3.3 %collective-permute-start.1 = (f32[3,32,128]{2,1,0:T(8,128)S(1)}, f32[3,32,128]{2,1,0:T(8,128)S(1)}, u32[]{:S(2)}, u32[]{:S(2)}) collective-permute-start(f32[3,32,128]{2,1,0:T(8,128)S(1)} %get-tuple-element.15), channel_id=1, source_target_pairs={{128,0},{136,8},{144,16},{152,24},{160,32},{168,40},{176,48},{184,... | collective-permute-start | bytes 147464 | tf_op jit(solution)/shard_map/ppermute | solution.py:250
  119.2 1.3 fusion.3
  120.5 1.3 collective-permute-done.1
  121.8 2.7 %collective-permute-start.2 = (f32[22,3,128]{2,1,0:T(4,128)S(1)}, f32[22,3,128]{2,1,0:T(4,128)S(1)}, u32[]{:S(2)}, u32[]{:S(2)}) collective-permute-start(f32[22,3,128]{2,1,0:T(4,128)S(1)} %get-tuple-element.12), channel_id=1, source_target_pairs={{0,32},{8,40},{16,48},{24,56},{32,64},{40,72},{48,80},{56,88},{64,... | collective-permute-start | bytes 101384 | tf_op jit(solution)/shard_map/ppermute | solution.py:250
  124.5 9.8 %collective-permute-start.3 = (f32[22,3,128]{2,1,0:T(4,128)S(1)}, f32[22,3,128]{2,1,0:T(4,128)S(1)}, u32[]{:S(2)}, u32[]{:S(2)}) collective-permute-start(f32[22,3,128]{2,1,0:T(4,128)S(1)} %get-tuple-element.13), channel_id=1, source_target_pairs={{32,0},{40,8},{48,16},{56,24},{64,32},{72,40},{80,48},{88,56},{96,... | collective-permute-start | bytes 101384 | tf_op jit(solution)/shard_map/ppermute | solution.py:250
  134.3 1.0 collective-permute-done.2
  135.3 0.7 collective-permute-done.3
  136.3 1.9 %collective-permute-start.4 = (f32[22,38,3]{2,1,0:T(8,128)S(1)}, f32[22,38,3]{2,1,0:T(8,128)S(1)}, u32[]{:S(2)}, u32[]{:S(2)}) collective-permute-start(f32[22,38,3]{2,1,0:T(8,128)S(1)} %get-tuple-element.10), channel_id=1, source_target_pairs={{0,8},{8,16},{16,24},{24,32},{32,40},{40,48},{48,56},{56,64},{64,7... | collective-permute-start | bytes 30104 | tf_op jit(solution)/shard_map/ppermute | solution.py:250
  139.0 11.3 %collective-permute-start.5 = (f32[22,38,3]{2,1,0:T(8,128)S(1)}, f32[22,38,3]{2,1,0:T(8,128)S(1)}, u32[]{:S(2)}, u32[]{:S(2)}) collective-permute-start(f32[22,38,3]{2,1,0:T(8,128)S(1)} %get-tuple-element.11), channel_id=1, source_target_pairs={{8,0},{16,8},{24,16},{32,24},{40,32},{48,40},{56,48},{64,56},{72,6... | collective-permute-start | bytes 30104 | tf_op jit(solution)/shard_map/ppermute | solution.py:250
  150.4 3.4 %collective-permute-done.4 = f32[22,38,3]{2,1,0:T(8,128)S(1)} collective-permute-done((f32[22,38,3]{2,1,0:T(8,128)S(1)}, f32[22,38,3]{2,1,0:T(8,128)S(1)}, u32[]{:S(2)}, u32[]{:S(2)}) %collective-permute-start.4) | collective-permute-done | bytes 10064 | tf_op jit(solution)/shard_map/ppermute | solution.py:250
  153.8 2.3 %collective-permute-done.5 = f32[22,38,3]{2,1,0:T(8,128)S(1)} collective-permute-done((f32[22,38,3]{2,1,0:T(8,128)S(1)}, f32[22,38,3]{2,1,0:T(8,128)S(1)}, u32[]{:S(2)}, u32[]{:S(2)}) %collective-permute-start.5) | collective-permute-done | bytes 10064 | tf_op jit(solution)/shard_map/ppermute | solution.py:250
  156.2 1.1 fusion.12
  159.5 2.0 %fusion.25 = f32[1,16,32,128]{3,2,1,0:T(8,128)} fusion(f32[1,16,32,128]{3,2,1,0:T(8,128)S(1)} %multiply_add_fusion, f32[22,38,134]{2,1,0:T(8,128)S(1)} %get-tuple-element.3, f32[22,38,134]{2,1,0:T(8,128)S(1)} %get-tuple-element.9, f32[22,38,134]{2,1,0:T(8,128)S(1)} %get-tuple-element.8, f32[22,38,134]{2,1,0:T(8,128)S(1)} %get-tuple-element.7, ...), kind=kLoop, calls=%fused_computation.56 | loop fusion | flops 786432 | bytes 2424844 | tf_op jit(solution)/shard_map/add | solution.py:334
  (41 shorter events, 7.8 us)
Async XLA Ops:
  0.6 118.6 %copy-start = (bf16[8,1,16,32,128]{4,3,2,1,0:T(8,128)(2,1)S(1)}, bf16[8,1,16,32,128]{4,3,2,1,0:T(8,128)(2,1)}, u32[]{:S(2)}) copy-start(bf16[8,1,16,32,128]{4,3,2,1,0:T(8,128)(2,1)} %param.9) | copy-start | bytes 3145732
  0.6 82.4 %copy-start.1 = (bf16[8,1,16,32,128]{4,3,2,1,0:T(8,128)(2,1)S(1)}, bf16[8,1,16,32,128]{4,3,2,1,0:T(8,128)(2,1)}, u32[]{:S(2)}) copy-start(bf16[8,1,16,32,128]{4,3,2,1,0:T(8,128)(2,1)} %param.10) | copy-start | bytes 3145732
  83.1 29.4 %copy-start.3 = (f32[1,16,32,128]{3,2,1,0:T(8,128)}, f32[1,16,32,128]{3,2,1,0:T(8,128)S(1)}, u32[]{:S(2)}) copy-start(f32[1,16,32,128]{3,2,1,0:T(8,128)S(1)} %get-tuple-element.5) | copy-start | bytes 786436
  113.3 7.2 %collective-permute-start = (f32[3,32,128]{2,1,0:T(8,128)S(1)}, f32[3,32,128]{2,1,0:T(8,128)S(1)}, u32[]{:S(2)}, u32[]{:S(2)}) collective-permute-start(f32[3,32,128]{2,1,0:T(8,128)S(1)} %get-tuple-element.14), channel_id=1, source_target_pairs={{0,128},{8,136},{16,144},{24,152},{32,160},{40,168},{48,176},{56,1... | collective-permute-start | bytes 147464 | tf_op jit(solution)/shard_map/ppermute | solution.py:250
  115.8 6.0 %collective-permute-start.1 = (f32[3,32,128]{2,1,0:T(8,128)S(1)}, f32[3,32,128]{2,1,0:T(8,128)S(1)}, u32[]{:S(2)}, u32[]{:S(2)}) collective-permute-start(f32[3,32,128]{2,1,0:T(8,128)S(1)} %get-tuple-element.15), channel_id=1, source_target_pairs={{128,0},{136,8},{144,16},{152,24},{160,32},{168,40},{176,48},{184,... | collective-permute-start | bytes 147464 | tf_op jit(solution)/shard_map/ppermute | solution.py:250
  121.8 13.5 %collective-permute-start.2 = (f32[22,3,128]{2,1,0:T(4,128)S(1)}, f32[22,3,128]{2,1,0:T(4,128)S(1)}, u32[]{:S(2)}, u32[]{:S(2)}) collective-permute-start(f32[22,3,128]{2,1,0:T(4,128)S(1)} %get-tuple-element.12), channel_id=1, source_target_pairs={{0,32},{8,40},{16,48},{24,56},{32,64},{40,72},{48,80},{56,88},{64,... | collective-permute-start | bytes 101384 | tf_op jit(solution)/shard_map/ppermute | solution.py:250
  124.5 11.5 %collective-permute-start.3 = (f32[22,3,128]{2,1,0:T(4,128)S(1)}, f32[22,3,128]{2,1,0:T(4,128)S(1)}, u32[]{:S(2)}, u32[]{:S(2)}) collective-permute-start(f32[22,3,128]{2,1,0:T(4,128)S(1)} %get-tuple-element.13), channel_id=1, source_target_pairs={{32,0},{40,8},{48,16},{56,24},{64,32},{72,40},{80,48},{88,56},{96,... | collective-permute-start | bytes 101384 | tf_op jit(solution)/shard_map/ppermute | solution.py:250
  136.3 17.5 %collective-permute-start.4 = (f32[22,38,3]{2,1,0:T(8,128)S(1)}, f32[22,38,3]{2,1,0:T(8,128)S(1)}, u32[]{:S(2)}, u32[]{:S(2)}) collective-permute-start(f32[22,38,3]{2,1,0:T(8,128)S(1)} %get-tuple-element.10), channel_id=1, source_target_pairs={{0,8},{8,16},{16,24},{24,32},{32,40},{40,48},{48,56},{56,64},{64,7... | collective-permute-start | bytes 30104 | tf_op jit(solution)/shard_map/ppermute | solution.py:250
  139.0 17.0 %collective-permute-start.5 = (f32[22,38,3]{2,1,0:T(8,128)S(1)}, f32[22,38,3]{2,1,0:T(8,128)S(1)}, u32[]{:S(2)}, u32[]{:S(2)}) collective-permute-start(f32[22,38,3]{2,1,0:T(8,128)S(1)} %get-tuple-element.11), channel_id=1, source_target_pairs={{8,0},{16,8},{24,16},{32,24},{40,32},{48,40},{56,48},{64,56},{72,6... | collective-permute-start | bytes 30104 | tf_op jit(solution)/shard_map/ppermute | solution.py:250
  158.5 1.0 copy-start.2

commit v7 on v6

--- a/solution.py
+++ b/solution.py
@@ -234,6 +234,82 @@
     )(part)
 
 
+def _swap_kernel(stride, lo_ref, hi_ref, from_lo_ref, from_hi_ref, got_lo, got_hi, s_lo, s_hi, r_lo, r_hi):
+    g = lax.axis_index("grid")
+    b = lax.axis_index("band")
+    c = g // stride % 4
+    has_lo = c > 0
+    has_hi = c < 3
+    lo = (g - stride, b)
+    hi = (g + stride, b)
+    barrier = pltpu.get_barrier_semaphore()
+
+    @pl.when(has_lo)
+    def _():
+        pl.semaphore_signal(barrier, inc=1, device_id=lo, device_id_type=MESH)
+
+    @pl.when(has_hi)
+    def _():
+        pl.semaphore_signal(barrier, inc=1, device_id=hi, device_id_type=MESH)
+
+    pl.semaphore_wait(barrier, has_lo.astype(jnp.int32) + has_hi.astype(jnp.int32))
+
+    def to_lo(dev):
+        return pltpu.make_async_remote_copy(
+            src_ref=lo_ref, dst_ref=got_hi, send_sem=s_lo, recv_sem=r_hi, device_id=dev, device_id_type=MESH
+        )
+
+    def to_hi(dev):
+        return pltpu.make_async_remote_copy(
+            src_ref=hi_ref, dst_ref=got_lo, send_sem=s_hi, recv_sem=r_lo, device_id=dev, device_id_type=MESH
+        )
+
+    @pl.when(has_lo)
+    def _():
+        to_lo(lo).start()
+
+    @pl.when(has_hi)
+    def _():
+        to_hi(hi).start()
+
+    @pl.when(has_lo)
+    def _():
+        to_lo(lo).wait_send()
+        to_hi(lo).wait_recv()
+        from_lo_ref[...] = got_lo[...]
+
+    @pl.when(has_hi)
+    def _():
+        to_hi(hi).wait_send()
+        to_lo(hi).wait_recv()
+        from_hi_ref[...] = got_hi[...]
+
+    @pl.when(jnp.logical_not(has_lo))
+    def _():
+        from_lo_ref[...] = jnp.zeros(from_lo_ref.shape, jnp.float32)
+
+    @pl.when(jnp.logical_not(has_hi))
+    def _():
+        from_hi_ref[...] = jnp.zeros(from_hi_ref.shape, jnp.float32)
+
+
+def swap_faces(to_lo, to_hi, stride, collective_id):
+    dma = pltpu.SemaphoreType.DMA
+    face = jax.ShapeDtypeStruct(to_lo.shape, jnp.float32)
+    return pl.pallas_call(
+        functools.partial(_swap_kernel, stride),
+        out_shape=(face, face),
+        in_specs=[pl.BlockSpec(memory_space=pltpu.VMEM)] * 2,
+        out_specs=(pl.BlockSpec(memory_space=pltpu.VMEM),) * 2,
+        scratch_shapes=[
+            pltpu.VMEM(to_lo.shape, jnp.float32),
+            pltpu.VMEM(to_lo.shape, jnp.float32),
+            dma(()), dma(()), dma(()), dma(()),
+        ],
+        compiler_params=pltpu.CompilerParams(collective_id=collective_id, has_side_effects=True),
+    )(to_lo, to_hi)
+
+
 def pack(values):
     flat = jnp.concatenate([v.reshape(-1) for v in values])
     return jnp.pad(flat, (0, 1024 - flat.shape[0])).reshape(8, 128)
@@ -301,20 +377,15 @@
     block_x = index // 16
     block_y = index // 4 % 4
     block_z = index % 4
-    keep_ylow = (block_y > 0).astype(jnp.float32)
-    keep_yhigh = (block_y < 3).astype(jnp.float32)
-    keep_zlow = (block_z > 0).astype(jnp.float32)
-    keep_zhigh = (block_z < 3).astype(jnp.float32)
     source = res_opt[0]
     h = SWEEPS - 1
     cx, cy, cz = source.shape
-    ext = jnp.concatenate([neighbour(source[-h:], 16), source, neighbour(source[:h], -16)], 0)
-    ext = jnp.concatenate(
-        [neighbour(ext[:, -h:], 4) * keep_ylow, ext, neighbour(ext[:, :h], -4) * keep_yhigh], 1
-    )
-    ext = jnp.concatenate(
-        [neighbour(ext[:, :, -h:], 1) * keep_zlow, ext, neighbour(ext[:, :, :h], -1) * keep_zhigh], 2
-    )
+    lo, hi = swap_faces(source[:h], source[-h:], 16, 4)
+    ext = jnp.concatenate([lo, source, hi], 0)
+    lo, hi = swap_faces(ext[:, :h], ext[:, -h:], 4, 5)
+    ext = jnp.concatenate([lo, ext, hi], 1)
+    lo, hi = swap_faces(jnp.transpose(ext[:, :, :h], (2, 0, 1)), jnp.transpose(ext[:, :, -h:], (2, 0, 1)), 1, 6)
+    ext = jnp.concatenate([jnp.transpose(lo, (1, 2, 0)), ext, jnp.transpose(hi, (1, 2, 0))], 2)
 
     def inside(block, size, n_blocks, axis):
         pos = block * size + lax.broadcasted_iota(jnp.int32, ext.shape, axis) - h

time: 162 us -> 150 us (0.926)
  the two profiles are of different devices: /device:TPU:8 before, /device:TPU:1 now
where the time goes in v7:
time: 150 us; the launch traced here: 149 us
  Pallas kernels  109 us (73%)
  other arithmetic  24.1 us (16%)
  local copies, waits for them, and re-layouts  9.88 us (7%)
  matrix products  3.44 us (2%)
  between operations  2.96 us (2%)
    pallas_call x1, Pallas kernels, symmetric_density(): pl.pallas_call(_density_kernel, out_shape=jax.ShapeDtypeStruct(part.shape...  56.4 us
    pallas_call x2, Pallas kernels, grid_sum(): pl.pallas_call(functools.partial(_grid_sum_kernel, n), out_shape=jax.Shap...  31.8 us
    pallas_call x3, Pallas kernels, swap_faces(): pl.pallas_call(functools.partial(_swap_kernel, stride), out_shape=(face,...  20.4 us
    reduce_sum x2, other arithmetic, local(): charges = grid_sum(pack([jnp.sum(rho_sym), jnp.sum(density_in)]), 1)  3.3 us
    reshape x2, other arithmetic, pack(): return jnp.pad(flat, (0, 1024 - flat.shape[0])).reshape(8, 128)  3.22 us

profile of v7, /device:TPU:1, one launch (start us, length us, event | category | flops | bytes accessed | tf_op | source)
XLA Modules:
  0.0 148.9 jit_solution(730316427092512869)
XLA Ops:
  0.7 2.1 %fusion.p_ref = f32[16,32,128]{2,1,0:T(8,128)} fusion(bf16[4,1,16,32,128]{4,3,2,1,0:T(8,128)(2,1)} %param.6, f32[4]{0:T(128)} %param.7), kind=kLoop, calls=%fused_computation.12 | loop fusion | flops 983040 | bytes 786448 | tf_op jit(solution)/shard_map/reduce_sum | solution.py:342
  2.8 56.4 %shard_map.77 = f32[16,32,128]{2,1,0:T(8,128)} custom-call(f32[16,32,128]{2,1,0:T(8,128)} %fusion.p_ref), custom_call_target="tpu_custom_call" | custom-call | tf_op jit(solution)/shard_map/pallas_call | solution.py:223
  59.2 1.7 %reduce_sum.65 = f32[]{:T(128)} reduce(f32[16,32,128]{2,1,0:T(8,128)} %shard_map.77, f32[]{:T(128)} %constant.103.clone.1), dimensions={0,1,2}, to_apply=%region_2.0 | reduce | flops 65535 | bytes 262152 | tf_op jit(solution)/shard_map/reduce_sum | solution.py:344
  60.9 1.6 %reduce_sum.66 = f32[]{:T(128)} reduce(f32[1,16,32,128]{3,2,1,0:T(8,128)} %param.8, f32[]{:T(128)} %constant.103.clone.1), dimensions={0,1,2,3}, to_apply=%region_3.4 | reduce | flops 65535 | bytes 262152 | tf_op jit(solution)/shard_map/reduce_sum | solution.py:344
  62.5 1.9 %fusion.31.x_ref = f32[8,128]{1,0:T(8,128)} fusion(f32[1]{0:T(128)} %bitcast.1, f32[1]{0:T(128)} %bitcast), kind=kLoop, calls=%fused_computation.83 | loop fusion | flops 4096 | bytes 4104 | tf_op jit(solution)/shard_map/reshape | solution.py:315
  64.5 14.9 %shard_map.78 = f32[8,128]{1,0:T(8,128)} custom-call(f32[8,128]{1,0:T(8,128)} %fusion.31.x_ref), custom_call_target="tpu_custom_call" | custom-call | tf_op jit(solution)/shard_map/pallas_call | solution.py:87
  79.4 1.3 fusion.39
  82.0 1.8 %multiply_reduce_fusion.2 = (f32[]{:T(128)}, f32[1,16,32,128]{3,2,1,0:T(8,128)S(1)}) fusion(f32[1,16,32,128]{3,2,1,0:T(8,128)} %param.8, f32[16,32,128]{2,1,0:T(8,128)} %shard_map.77, f32[]{:T(128)} %bitcast.3), kind=kLoop, calls=%fused_computation.62 | loop fusion | flops 262143 | bytes 786440 | tf_op jit(solution)/shard_map/reduce_sum | solution.py:353
  84.8 1.7 %multiply_reduce_fusion = f32[8,8]{1,0:T(8,128)S(1)} fusion(f32[8,65536]{1,0:T(8,128)S(1)} %bitcast.83), kind=kLoop, calls=%fused_computation | loop fusion | flops 8388544 | bytes 2097408 | tf_op jit(solution)/shard_map/reduce_sum | solution.py:348
  86.5 1.3 fusion.30.x_ref
  87.8 16.9 %shard_map.79 = f32[8,128]{1,0:T(8,128)} custom-call(f32[8,128]{1,0:T(8,128)} %fusion.30.x_ref), custom_call_target="tpu_custom_call" | custom-call | tf_op jit(solution)/shard_map/pallas_call | solution.py:87
  104.7 0.8 slice_bitcast_fusion.2
  105.6 0.8 slice_bitcast_fusion.3
  106.3 0.8 slice.146
  107.4 0.8 cholesky.16
  109.6 0.7 custom-call.10
  110.4 0.8 fusion.40
  111.8 1.3 fusion.1
  114.9 5.1 %shard_map.80 = (f32[3,32,128]{2,1,0:T(8,128)}, f32[3,32,128]{2,1,0:T(8,128)}) custom-call(f32[3,32,128]{2,1,0:T(8,128)} %get-tuple-element.31.lo_ref, f32[3,32,128]{2,1,0:T(8,128)} %get-tuple-element.30.hi_ref), custom_call_target="tpu_custom_call" | custom-call | tf_op jit(solution)/shard_map/pallas_call | solution.py:299
  120.0 1.4 pad_maximum_fusion.2
  121.5 6.8 %shard_map.81 = (f32[22,3,128]{2,1,0:T(4,128)}, f32[22,3,128]{2,1,0:T(4,128)}) custom-call(f32[22,3,128]{2,1,0:T(4,128)} %get-tuple-element.29.lo_ref, f32[22,3,128]{2,1,0:T(4,128)} %get-tuple-element.28.hi_ref), custom_call_target="tpu_custom_call" | custom-call | tf_op jit(solution)/shard_map/pallas_call | solution.py:299
  128.3 0.9 pad_maximum_fusion.1
  129.4 0.9 copy.66
  130.3 0.9 copy.67
  131.2 8.5 %shard_map.82 = (f32[3,22,38]{2,1,0:T(8,128)}, f32[3,22,38]{2,1,0:T(8,128)}) custom-call(f32[3,22,38]{2,1,0:T(8,128)} %bitcast.92, f32[3,22,38]{2,1,0:T(8,128)} %bitcast.93), custom_call_target="tpu_custom_call" | custom-call | tf_op jit(solution)/shard_map/pallas_call | solution.py:299
  139.6 1.0 copy.57
  140.7 1.0 copy.58
  142.6 1.0 fusion.12
  144.2 0.7 divide_select_fusion
  144.9 0.7 slice_add_fusion
  145.6 1.3 fusion.3
  147.1 1.8 %fusion.25 = f32[1,16,32,128]{3,2,1,0:T(8,128)} fusion(f32[1,16,32,128]{3,2,1,0:T(8,128)S(1)} %multiply_add_fusion, f32[22,38,134]{2,1,0:T(8,128)S(1)} %get-tuple-element.19, f32[22,38,134]{2,1,0:T(8,128)S(1)} %get-tuple-element.25, f32[22,38,134]{2,1,0:T(8,128)S(1)} %get-tuple-element.24, f32[22,38,134]{2,1,0:T(8,128)S(1)} %get-tuple-element.23, ...), kind=kLoop, calls=%fused_computation.56 | loop fusion | flops 786432 | bytes 2424844 | tf_op jit(solution)/shard_map/add | solution.py:405
  (40 shorter events, 6.5 us)
Async XLA Ops:
  0.6 144.9 %copy-start = (bf16[8,1,16,32,128]{4,3,2,1,0:T(8,128)(2,1)S(1)}, bf16[8,1,16,32,128]{4,3,2,1,0:T(8,128)(2,1)}, u32[]{:S(2)}) copy-start(bf16[8,1,16,32,128]{4,3,2,1,0:T(8,128)(2,1)} %param.9) | copy-start | bytes 3145732
  0.6 83.2 %copy-start.1 = (bf16[8,1,16,32,128]{4,3,2,1,0:T(8,128)(2,1)S(1)}, bf16[8,1,16,32,128]{4,3,2,1,0:T(8,128)(2,1)}, u32[]{:S(2)}) copy-start(bf16[8,1,16,32,128]{4,3,2,1,0:T(8,128)(2,1)} %param.10) | copy-start | bytes 3145732
  83.8 29.9 %copy-start.3 = (f32[1,16,32,128]{3,2,1,0:T(8,128)}, f32[1,16,32,128]{3,2,1,0:T(8,128)S(1)}, u32[]{:S(2)}) copy-start(f32[1,16,32,128]{3,2,1,0:T(8,128)S(1)} %get-tuple-element.21) | copy-start | bytes 786436
  129.2 13.3 %copy-start.4 = (f32[3,32,128]{2,1,0:T(8,128)S(1)}, f32[3,32,128]{2,1,0:T(8,128)}, u32[]{:S(2)}) copy-start(f32[3,32,128]{2,1,0:T(8,128)} %get-tuple-element.8) | copy-start | bytes 147460
  129.2 13.3 %copy-start.5 = (f32[3,32,128]{2,1,0:T(8,128)S(1)}, f32[3,32,128]{2,1,0:T(8,128)}, u32[]{:S(2)}) copy-start(f32[3,32,128]{2,1,0:T(8,128)} %get-tuple-element.9) | copy-start | bytes 147460
  129.2 13.3 %copy-start.6 = (f32[22,3,128]{2,1,0:T(4,128)S(1)}, f32[22,3,128]{2,1,0:T(4,128)}, u32[]{:S(2)}) copy-start(f32[22,3,128]{2,1,0:T(4,128)} %get-tuple-element.10) | copy-start | bytes 101380
  129.2 13.3 %copy-start.7 = (f32[22,3,128]{2,1,0:T(4,128)S(1)}, f32[22,3,128]{2,1,0:T(4,128)}, u32[]{:S(2)}) copy-start(f32[22,3,128]{2,1,0:T(4,128)} %get-tuple-element.11) | copy-start | bytes 101380
  144.9 2.2 %copy-start.2 = (f32[1,16,32,128]{3,2,1,0:T(8,128)S(1)}, f32[1,16,32,128]{3,2,1,0:T(8,128)}, u32[]{:S(2)}) copy-start(f32[1,16,32,128]{3,2,1,0:T(8,128)} %param.8) | copy-start | bytes 786436

commit v8 on v7

--- a/solution.py
+++ b/solution.py
@@ -112,8 +112,9 @@
     return x
 
 
-def _density_kernel(p_ref, o_ref, q_in, q_sum, e_in, e_buf, ax_in, a_buf, ay_in, b_buf, bz_in, s_buf, tq, full,
-                    s1, r1, s2, r2, sx, rx, sy, ry, sz, rz, s6, r6, s7, r7):
+def _density_kernel(p_ref, d_ref, o_ref, c_ref, q_in, q_sum, e_in, e_buf, ax_in, a_buf, ay_in, b_buf, bz_in, s_buf,
+                    tq, full, ga_in, ga_sum, gb_in, t_buf, tz_in, tp_buf, tx_in,
+                    s1, r1, s2, r2, sx, rx, sy, ry, sz, rz, s6, r6, s7, r7, sga, rga, sgb, rgb, stz, rtz, stx, rtx):
     g = lax.axis_index("grid")
     b = lax.axis_index("band")
     zhi = b // 4
@@ -133,7 +134,38 @@
     pl.semaphore_signal(barrier, inc=1, device_id=(gx, b), device_id_type=MESH)
     pl.semaphore_signal(barrier, inc=1, device_id=(gy, b), device_id_type=MESH)
     pl.semaphore_signal(barrier, inc=1, device_id=(gz, b), device_id_type=MESH)
-    pl.semaphore_wait(barrier, 7)
+    na = ga_in.shape[0]
+    nb = gb_in.shape[0]
+    grow = g // na
+    gj = g % na
+
+    def greet(k, c):
+        pl.semaphore_signal(barrier, inc=1, device_id=(grow * na + lax.rem(gj + k, na), b), device_id_type=MESH)
+        return c
+
+    lax.fori_loop(1, na, greet, 0)
+    for k in range(1, nb):
+        pl.semaphore_signal(barrier, inc=1, device_id=(lax.rem(grow + k, nb) * na + gj, b), device_id_type=MESH)
+    pl.semaphore_wait(barrier, 7 + na - 1 + nb - 1)
+
+    e = 2 * x + zhi
+    lane = lax.broadcasted_iota(jnp.int32, ga_sum.shape, 1)
+    first = lax.broadcasted_iota(jnp.int32, ga_sum.shape, 0) == 0
+    din_pair = jnp.sum(d_ref[pl.ds(e, 1)]) + jnp.sum(d_ref[pl.ds(rows - 1 - e, 1)])
+    own = jnp.where(first & (lane == 0), jnp.sum(p_ref[...]), jnp.where(first & (lane == 1), din_pair, 0.0))
+    ga_in[gj] = own
+
+    def copy_ga(slot, peer_j):
+        return pltpu.make_async_remote_copy(
+            src_ref=ga_in.at[gj], dst_ref=ga_in.at[slot], send_sem=sga.at[peer_j], recv_sem=rga.at[slot],
+            device_id=(grow * na + peer_j, b), device_id_type=MESH,
+        )
+
+    def send_ga(k, c):
+        copy_ga(gj, lax.rem(gj + k, na)).start()
+        return c
+
+    lax.fori_loop(1, na, send_ga, 0)
 
     def remote(src, dst, ssem, rsem, dev):
         return pltpu.make_async_remote_copy(
@@ -173,6 +205,25 @@
     remote(q_sum.at[pl.ds(0, 1)], e_in.at[1 - zhi, pl.ds(0, 1)], s2.at[0], r2.at[1 - zhi, 0], dev).wait_recv()
     remote(q_sum.at[pl.ds(0, 1)], e_in.at[1 - zhi, pl.ds(1, 1)], s2.at[1], r2.at[1 - zhi, 1], dev).wait_recv()
     e_buf[...] = e_in[0] + e_in[1]
+
+    def wait_ga(k, c):
+        peer = lax.rem(gj + k, na)
+        copy_ga(gj, peer).wait_send()
+        copy_ga(peer, peer).wait_recv()
+        return c
+
+    lax.fori_loop(1, na, wait_ga, 0)
+    ga_sum[...] = lax.fori_loop(1, na, lambda p, acc: acc + ga_in[p], ga_in[0])
+
+    def copy_gb(slot, peer_row):
+        return pltpu.make_async_remote_copy(
+            src_ref=ga_sum, dst_ref=gb_in.at[slot], send_sem=sgb.at[peer_row], recv_sem=rgb.at[slot],
+            device_id=(peer_row * na + gj, b), device_id_type=MESH,
+        )
+
+    for k in range(1, nb):
+        copy_gb(grow, lax.rem(grow + k, nb)).start()
+    gb_in[grow] = ga_sum[...]
     c_x = remote(e_buf, ax_in, sx, rx, (gx, b))
     c_x.start()
     c_x.wait_send()
@@ -189,6 +240,17 @@
     c_z.wait_send()
     c_z.wait_recv()
     s_buf[...] = 0.5 * (b_buf[...] + reverse(bz_in[...], 2))
+    for k in range(1, nb):
+        peer = lax.rem(grow + k, nb)
+        copy_gb(grow, peer).wait_send()
+        copy_gb(peer, peer).wait_recv()
+    acc = gb_in[0]
+    for p in range(1, nb):
+        acc = acc + gb_in[p]
+    t_buf[...] = acc
+    c_t = remote(t_buf, tz_in.at[zhi], stz, rtz.at[zhi], dev)
+    c_t.start()
+    tz_in[zhi] = t_buf[...]
     c_a = remote(s_buf.at[pl.ds(0, 1)], tq.at[pl.ds(zhi, 1)], s6.at[0], r6.at[0], dev)
     c_b = remote(s_buf.at[pl.ds(1, 1)], tq.at[pl.ds(3 - zhi, 1)], s6.at[1], r6.at[1], dev)
     c_a.start()
@@ -199,11 +261,16 @@
     c_b.wait_send()
     remote(s_buf.at[pl.ds(0, 1)], tq.at[pl.ds(1 - zhi, 1)], s6.at[0], r6.at[0], dev).wait_recv()
     remote(s_buf.at[pl.ds(1, 1)], tq.at[pl.ds(2 + zhi, 1)], s6.at[1], r6.at[1], dev).wait_recv()
+    c_t.wait_send()
+    remote(t_buf, tz_in.at[1 - zhi], stz, rtz.at[1 - zhi], dev).wait_recv()
+    tp_buf[...] = tz_in[0] + tz_in[1]
     for k in range(1, 4):
         px = lax.rem(x + k, 4)
         dev = (g, zhi * 4 + px)
         remote(tq.at[pl.ds(0, 2)], full.at[low(x)], s7.at[k, 0], r7.at[x, 0], dev).start()
         remote(tq.at[pl.ds(2, 2)], full.at[high(x)], s7.at[k, 1], r7.at[x, 1], dev).start()
+        remote(tp_buf, tx_in.at[x], stx.at[k], rtx.at[x], dev).start()
+    tx_in[x] = tp_buf[...]
     full[low(x)] = tq[pl.ds(0, 2)]
     full[high(x)] = tq[pl.ds(2, 2)]
     for k in range(1, 4):
@@ -213,25 +280,33 @@
         remote(tq.at[pl.ds(2, 2)], full.at[high(x)], s7.at[k, 1], r7.at[x, 1], dev).wait_send()
         remote(tq.at[pl.ds(0, 2)], full.at[low(px)], s7.at[k, 0], r7.at[px, 0], dev).wait_recv()
         remote(tq.at[pl.ds(2, 2)], full.at[high(px)], s7.at[k, 1], r7.at[px, 1], dev).wait_recv()
+        remote(tp_buf, tx_in.at[x], stx.at[k], rtx.at[x], dev).wait_send()
+        remote(tp_buf, tx_in.at[px], stx.at[k], rtx.at[px], dev).wait_recv()
     o_ref[...] = full[...]
-
-
-def symmetric_density(part):
+    c_ref[...] = ((tx_in[0] + tx_in[1]) + tx_in[2]) + tx_in[3]
+
+
+def symmetric_density(part, din):
     rest = part.shape[1:]
     dma = pltpu.SemaphoreType.DMA
     vm = lambda *s: pltpu.VMEM(s + rest, jnp.float32)
+    tile = lambda *s: pltpu.VMEM(s + (8, 128), jnp.float32)
+    n = lax.axis_size("grid")
+    na = 16
     return pl.pallas_call(
         _density_kernel,
-        out_shape=jax.ShapeDtypeStruct(part.shape, jnp.float32),
-        in_specs=[pl.BlockSpec(memory_space=pltpu.VMEM)],
-        out_specs=pl.BlockSpec(memory_space=pltpu.VMEM),
+        out_shape=(jax.ShapeDtypeStruct(part.shape, jnp.float32), jax.ShapeDtypeStruct((8, 128), jnp.float32)),
+        in_specs=[pl.BlockSpec(memory_space=pltpu.VMEM)] * 2,
+        out_specs=(pl.BlockSpec(memory_space=pltpu.VMEM),) * 2,
         scratch_shapes=[
             vm(4, 4), vm(4), vm(2, 2), vm(2), vm(2), vm(2), vm(2), vm(2), vm(2), vm(2), vm(4), vm(part.shape[0]),
+            tile(na), tile(), tile(n // na), tile(), tile(2), tile(), tile(4),
             dma((4, 2)), dma((4, 2)), dma((2,)), dma((2, 2)), dma(()), dma(()), dma(()), dma(()), dma(()), dma(()),
             dma((2,)), dma((2,)), dma((4, 2)), dma((4, 2)),
+            dma((na,)), dma((na,)), dma((n // na,)), dma((n // na,)), dma(()), dma((2,)), dma((4,)), dma((4,)),
         ],
         compiler_params=pltpu.CompilerParams(collective_id=3, has_side_effects=True),
-    )(part)
+    )(part, din)
 
 
 def _swap_kernel(stride, lo_ref, hi_ref, from_lo_ref, from_hi_ref, got_lo, got_hi, s_lo, s_hi, r_lo, r_hi):
@@ -340,8 +415,8 @@
 def local(orbitals, occupations, density_in, history_in, history_res, screening):
     waves = orbitals.astype(jnp.float32)
     partial_value = jnp.sum(occupations[:, None, None, None, None] * waves * waves, 0)
-    rho_sym = symmetric_density(partial_value[0])[None]
-    charges = grid_sum(pack([jnp.sum(rho_sym), jnp.sum(density_in)]), 1)
+    rho_block, charges = symmetric_density(partial_value[0], density_in[0])
+    rho_sym = rho_block[None]
     depth = history_res.shape[0]
     res_hist = history_res.astype(jnp.float32)
     hist_flat = res_hist.reshape(depth, -1)

time: 150 us -> 129 us (0.86)
  Pallas kernels: 109 us -> 93 us
  other arithmetic: 24.1 us -> 18.8 us
    pallas_call x2 -> x1, Pallas kernels: 31.8 us -> 14.4 us  [grid_sum(): pl.pallas_call(functools.partial(_grid_sum_kernel, n), out_shape=jax.Shap...]
    reduce_sum x2 -> x0, other arithmetic: 3.3 us -> none  [local(): charges = grid_sum(pack([jnp.sum(rho_sym), jnp.sum(density_in)]), 1)]
    reshape x2 -> x1, other arithmetic: 3.22 us -> 1.29 us  [pack(): return jnp.pad(flat, (0, 1024 - flat.shape[0])).reshape(8, 128)]
where the time goes in v8:
time: 129 us; the launch traced here: 128 us
  Pallas kernels  93 us (72%)
  other arithmetic  18.8 us (15%)
  local copies, waits for them, and re-layouts  9.88 us (8%)
  matrix products  3.44 us (3%)
  between operations  2.95 us (2%)
    pallas_call x1, Pallas kernels, symmetric_density(): pl.pallas_call(_density_kernel, out_shape=(jax.ShapeDtypeStruct(part.shap...  57.3 us
    pallas_call x3, Pallas kernels, swap_faces(): pl.pallas_call(functools.partial(_swap_kernel, stride), out_shape=(face,...  21.3 us
    pallas_call x1, Pallas kernels, grid_sum(): pl.pallas_call(functools.partial(_grid_sum_kernel, n), out_shape=jax.Shap...  14.4 us

profile of v8, /device:TPU:1, one launch (start us, length us, event | category | flops | bytes accessed | tf_op | source)
XLA Modules:
  0.0 128.1 jit_solution(3914627732442829975)
XLA Ops:
  0.7 2.1 %fusion.p_ref = f32[16,32,128]{2,1,0:T(8,128)} fusion(bf16[4,1,16,32,128]{4,3,2,1,0:T(8,128)(2,1)} %param.6, f32[4]{0:T(128)} %param.7), kind=kLoop, calls=%fused_computation.12 | loop fusion | flops 983040 | bytes 786448 | tf_op jit(solution)/shard_map/reduce_sum | solution.py:417
  2.8 57.3 %shard_map.77 = (f32[16,32,128]{2,1,0:T(8,128)}, f32[8,128]{1,0:T(8,128)}) custom-call(f32[16,32,128]{2,1,0:T(8,128)} %fusion.p_ref, f32[16,32,128]{2,1,0:T(8,128)} %bitcast.86), custom_call_target="tpu_custom_call" | custom-call | tf_op jit(solution)/shard_map/pallas_call | solution.py:296
  60.1 1.3 %fusion.38 = (f32[1,1]{1,0:T(1,128)}, f32[1,1]{1,0:T(1,128)}) fusion(f32[8,128]{1,0:T(8,128)} %get-tuple-element.10), kind=kLoop, calls=%fused_computation.96 | loop fusion | bytes 16 | tf_op jit(solution)/shard_map/slice | solution.py:424
  62.8 1.8 %multiply_reduce_fusion.2 = (f32[]{:T(128)}, f32[1,16,32,128]{3,2,1,0:T(8,128)S(1)}) fusion(f32[1,16,32,128]{3,2,1,0:T(8,128)} %param.8, f32[16,32,128]{2,1,0:T(8,128)} %get-tuple-element.11, f32[]{:T(128)} %bitcast.1), kind=kLoop, calls=%fused_computation.62 | loop fusion | flops 262143 | bytes 786440 | tf_op jit(solution)/shard_map/reduce_sum | solution.py:428
  65.5 1.7 %multiply_reduce_fusion = f32[8,8]{1,0:T(8,128)S(1)} fusion(f32[8,65536]{1,0:T(8,128)S(1)} %bitcast.80), kind=kLoop, calls=%fused_computation | loop fusion | flops 8388544 | bytes 2097408 | tf_op jit(solution)/shard_map/reduce_sum | solution.py:423
  67.3 1.3 %fusion.30.x_ref = f32[8,128]{1,0:T(8,128)} fusion(f32[1]{0:T(128)} %bitcast.4, f32[8]{0:T(128)S(1)} %multiply_reduce_fusion.1, f32[64]{0:T(128)S(1)} %reshape.67), kind=kLoop, calls=%fused_computation.79 | loop fusion | flops 6144 | bytes 4388 | tf_op jit(solution)/shard_map/reshape | solution.py:390
  68.6 14.4 %shard_map.78 = f32[8,128]{1,0:T(8,128)} custom-call(f32[8,128]{1,0:T(8,128)} %fusion.30.x_ref), custom_call_target="tpu_custom_call" | custom-call | tf_op jit(solution)/shard_map/pallas_call | solution.py:87
  83.0 0.8 slice_bitcast_fusion.2
  83.9 0.8 slice_bitcast_fusion.3
  84.6 0.8 slice.146
  85.7 0.8 cholesky.16
  86.6 0.6 compare_reduce_fusion
  87.2 0.6 fusion.26
  87.9 0.7 custom-call.10
  88.7 0.8 fusion.39
  89.5 0.6 broadcast_divide_fusion
  90.1 1.3 fusion.1
  92.6 0.6 slice_bitcast_fusion
  93.2 5.9 %shard_map.79 = (f32[3,32,128]{2,1,0:T(8,128)}, f32[3,32,128]{2,1,0:T(8,128)}) custom-call(f32[3,32,128]{2,1,0:T(8,128)} %get-tuple-element.35.lo_ref, f32[3,32,128]{2,1,0:T(8,128)} %get-tuple-element.34.hi_ref), custom_call_target="tpu_custom_call" | custom-call | tf_op jit(solution)/shard_map/pallas_call | solution.py:374
  99.1 1.4 %pad_maximum_fusion.2 = (f32[22,3,128]{2,1,0:T(4,128)}, f32[22,3,128]{2,1,0:T(4,128)}) fusion(f32[3,32,128]{2,1,0:T(8,128)} %get-tuple-element.13, f32[16,32,128]{2,1,0:T(8,128)S(1)} %bitcast.83, f32[3,32,128]{2,1,0:T(8,128)} %get-tuple-element.12), kind=kLoop, calls=%fused_computation.65 | loop fusion | flops 33792 | bytes 428032 | tf_op jit(solution)/shard_map/concatenate | solution.py:459
  100.5 6.9 %shard_map.80 = (f32[22,3,128]{2,1,0:T(4,128)}, f32[22,3,128]{2,1,0:T(4,128)}) custom-call(f32[22,3,128]{2,1,0:T(4,128)} %get-tuple-element.33.lo_ref, f32[22,3,128]{2,1,0:T(4,128)} %get-tuple-element.32.hi_ref), custom_call_target="tpu_custom_call" | custom-call | tf_op jit(solution)/shard_map/pallas_call | solution.py:374
  107.5 0.9 pad_maximum_fusion.1
  108.6 0.9 copy.66
  109.5 0.9 copy.67
  110.3 8.5 %shard_map.81 = (f32[3,22,38]{2,1,0:T(8,128)}, f32[3,22,38]{2,1,0:T(8,128)}) custom-call(f32[3,22,38]{2,1,0:T(8,128)} %bitcast.90, f32[3,22,38]{2,1,0:T(8,128)} %bitcast.91), custom_call_target="tpu_custom_call" | custom-call | tf_op jit(solution)/shard_map/pallas_call | solution.py:374
  118.8 1.0 copy.57
  119.9 1.0 copy.58
  121.8 1.0 fusion.12
  123.4 0.7 divide_select_fusion
  124.1 0.7 slice_add_fusion
  124.8 1.3 fusion.3
  126.3 1.8 %fusion.25 = f32[1,16,32,128]{3,2,1,0:T(8,128)} fusion(f32[1,16,32,128]{3,2,1,0:T(8,128)S(1)} %multiply_add_fusion, f32[22,38,134]{2,1,0:T(8,128)S(1)} %get-tuple-element.23, f32[22,38,134]{2,1,0:T(8,128)S(1)} %get-tuple-element.29, f32[22,38,134]{2,1,0:T(8,128)S(1)} %get-tuple-element.28, f32[22,38,134]{2,1,0:T(8,128)S(1)} %get-tuple-element.27, ...), kind=kLoop, calls=%fused_computation.56 | loop fusion | flops 786432 | bytes 2424844 | tf_op jit(solution)/shard_map/add | solution.py:480
  (36 shorter events, 4.0 us)
Async XLA Ops:
  0.6 124.1 %copy-start = (bf16[8,1,16,32,128]{4,3,2,1,0:T(8,128)(2,1)S(1)}, bf16[8,1,16,32,128]{4,3,2,1,0:T(8,128)(2,1)}, u32[]{:S(2)}) copy-start(bf16[8,1,16,32,128]{4,3,2,1,0:T(8,128)(2,1)} %param.9) | copy-start | bytes 3145732
  0.6 63.9 %copy-start.1 = (bf16[8,1,16,32,128]{4,3,2,1,0:T(8,128)(2,1)S(1)}, bf16[8,1,16,32,128]{4,3,2,1,0:T(8,128)(2,1)}, u32[]{:S(2)}) copy-start(bf16[8,1,16,32,128]{4,3,2,1,0:T(8,128)(2,1)} %param.10) | copy-start | bytes 3145732
  64.6 27.4 %copy-start.3 = (f32[1,16,32,128]{3,2,1,0:T(8,128)}, f32[1,16,32,128]{3,2,1,0:T(8,128)S(1)}, u32[]{:S(2)}) copy-start(f32[1,16,32,128]{3,2,1,0:T(8,128)S(1)} %get-tuple-element.25) | copy-start | bytes 786436
  108.4 13.3 %copy-start.4 = (f32[3,32,128]{2,1,0:T(8,128)S(1)}, f32[3,32,128]{2,1,0:T(8,128)}, u32[]{:S(2)}) copy-start(f32[3,32,128]{2,1,0:T(8,128)} %get-tuple-element.12) | copy-start | bytes 147460
  108.4 13.3 %copy-start.5 = (f32[3,32,128]{2,1,0:T(8,128)S(1)}, f32[3,32,128]{2,1,0:T(8,128)}, u32[]{:S(2)}) copy-start(f32[3,32,128]{2,1,0:T(8,128)} %get-tuple-element.13) | copy-start | bytes 147460
  108.4 13.3 %copy-start.6 = (f32[22,3,128]{2,1,0:T(4,128)S(1)}, f32[22,3,128]{2,1,0:T(4,128)}, u32[]{:S(2)}) copy-start(f32[22,3,128]{2,1,0:T(4,128)} %get-tuple-element.14) | copy-start | bytes 101380
  108.4 13.3 %copy-start.7 = (f32[22,3,128]{2,1,0:T(4,128)S(1)}, f32[22,3,128]{2,1,0:T(4,128)}, u32[]{:S(2)}) copy-start(f32[22,3,128]{2,1,0:T(4,128)} %get-tuple-element.15) | copy-start | bytes 101380
  124.1 2.2 %copy-start.2 = (f32[1,16,32,128]{3,2,1,0:T(8,128)S(1)}, f32[1,16,32,128]{3,2,1,0:T(8,128)}, u32[]{:S(2)}) copy-start(f32[1,16,32,128]{3,2,1,0:T(8,128)} %param.8) | copy-start | bytes 786436

commit v9 on v8

--- a/solution.py
+++ b/solution.py
@@ -13,7 +13,43 @@
 mixing_weight = 0.5
 
 
-def _grid_sum_kernel(n, x_ref, o_ref, buf_a, sum_a, buf_b, sa, ra, sb, rb):
+def _solve_ones(gram, m):
+    row = lax.broadcasted_iota(jnp.int32, gram.shape, 0)
+    col = lax.broadcasted_iota(jnp.int32, gram.shape, 1)
+    rows = lax.broadcasted_iota(jnp.int32, (gram.shape[0], 1), 0)
+    zero = jnp.zeros_like(gram)
+    a = gram
+    lower = zero
+    upper = zero
+    for j in range(m):
+        col_j = jnp.sum(jnp.where(col == j, a, 0.0), axis=1, keepdims=True)
+        row_j = jnp.sum(jnp.where(row == j, a, 0.0), axis=0, keepdims=True)
+        pivot = jnp.sqrt(jnp.sum(jnp.where((row == j) & (col == j), a, 0.0), axis=(0, 1), keepdims=True))
+        l_col = jnp.where(rows >= j, col_j / pivot, 0.0)
+        l_row = jnp.where(col[:1] >= j, row_j / pivot, 0.0)
+        lower = lower + jnp.where(col == j, l_col, 0.0)
+        upper = upper + jnp.where(row == j, l_row, 0.0)
+        a = a - l_col * l_row
+    b = jnp.where(rows < m, 1.0, 0.0)
+    y = jnp.zeros_like(b)
+    for j in range(m):
+        l_col = jnp.sum(jnp.where(col == j, lower, 0.0), axis=1, keepdims=True)
+        diag = jnp.sum(jnp.where(rows == j, l_col, 0.0), axis=0, keepdims=True)
+        y_j = jnp.sum(jnp.where(rows == j, b, 0.0), axis=0, keepdims=True) / diag
+        y = y + jnp.where(rows == j, y_j, 0.0)
+        b = b - jnp.where(rows > j, l_col * y_j, 0.0)
+    z = jnp.zeros_like(y)
+    c = y
+    for j in reversed(range(m)):
+        u_col = jnp.sum(jnp.where(col == j, upper, 0.0), axis=1, keepdims=True)
+        diag = jnp.sum(jnp.where(rows == j, u_col, 0.0), axis=0, keepdims=True)
+        z_j = jnp.sum(jnp.where(rows == j, c, 0.0), axis=0, keepdims=True) / diag
+        z = z + jnp.where(rows == j, z_j, 0.0)
+        c = c - jnp.where(rows < j, u_col * z_j, 0.0)
+    return z / jnp.sum(z, axis=0, keepdims=True)
+
+
+def _grid_sum_kernel(n, solve, x_ref, o_ref, buf_a, sum_a, buf_b, sa, ra, sb, rb):
     me = lax.axis_index("grid")
     band = lax.axis_index("band")
     na = buf_a.shape[0]
@@ -77,15 +113,17 @@
     acc = buf_b[0]
     for p in range(1, nb):
         acc = acc + buf_b[p]
+    if solve:
+        acc = jnp.broadcast_to(_solve_ones(acc, solve), acc.shape)
     o_ref[...] = acc
 
 
-def grid_sum(vec, collective_id):
+def grid_sum(vec, collective_id, solve=0):
     n = lax.axis_size("grid")
     na = 16
     dma = pltpu.SemaphoreType.DMA
     return pl.pallas_call(
-        functools.partial(_grid_sum_kernel, n),
+        functools.partial(_grid_sum_kernel, n, solve),
         out_shape=jax.ShapeDtypeStruct(vec.shape, jnp.float32),
         in_specs=[pl.BlockSpec(memory_space=pltpu.VMEM)],
         out_specs=pl.BlockSpec(memory_space=pltpu.VMEM),
@@ -426,14 +464,11 @@
     res_flat = residual.reshape(-1)
     last_row = jnp.sum(hist_flat * res_flat[None, :], axis=-1)
     last = jnp.sum(res_flat * res_flat)
-    total = grid_sum(pack([hist_gram, last_row, last]), 2).reshape(-1)
-    row = total[depth * depth : depth * depth + depth]
-    top = jnp.concatenate([total[: depth * depth].reshape(depth, depth), row[:, None]], 1)
-    bottom = jnp.concatenate([row, total[depth * depth + depth :][:1]])[None]
-    gram = jnp.concatenate([top, bottom], 0)
-    lower = jnp.linalg.cholesky(gram)
-    solved = jax.scipy.linalg.cho_solve((lower, True), jnp.ones((depth + 1,), jnp.float32))
-    coefficients = solved / jnp.sum(solved)
+    local_gram = jnp.concatenate(
+        [jnp.concatenate([hist_gram, last_row[:, None]], 1), jnp.concatenate([last_row, last[None]])[None]], 0
+    )
+    local_gram = jnp.pad(local_gram, ((0, 16 - depth - 1), (0, 128 - depth - 1)))
+    coefficients = grid_sum(local_gram, 2, depth + 1)[: depth + 1, 0]
     rho_opt = (
         jnp.einsum(
             "m,mgxyz->gxyz",

time: 129 us -> 127 us (0.984)
  Pallas kernels: 93 us -> 96.4 us
  other arithmetic: 18.8 us -> 15.7 us
    pallas_call x1, Pallas kernels: 14.4 us -> 17.6 us  [grid_sum(): pl.pallas_call(functools.partial(_grid_sum_kernel, n, solve), out_shape=j...]
    another operation x5 -> x0, other arithmetic: 2.83 us -> none  [the longest x3 1.49 us: local(): lower = jnp.linalg.cholesky(gram)]
    broadcast_in_dim x3 -> x1, local copies, waits for them, and re-layouts: 1.6 us -> 0.08 us  [local(): last_row[:, None]]
    reshape x1 -> x0, other arithmetic: 1.29 us -> none  [pack(): return jnp.pad(flat, (0, 1024 - flat.shape[0])).reshape(8, 128)]
where the time goes in v9:
time: 127 us; the launch traced here: 126 us
  Pallas kernels  96.4 us (76%)
  other arithmetic  15.7 us (12%)
  local copies, waits for them, and re-layouts  8.85 us (7%)
  between operations  2.91 us (2%)
  matrix products  2.54 us (2%)
    pallas_call x1, Pallas kernels, symmetric_density(): pl.pallas_call(_density_kernel, out_shape=(jax.ShapeDtypeStruct(part.shap...  57.3 us
    pallas_call x3, Pallas kernels, swap_faces(): pl.pallas_call(functools.partial(_swap_kernel, stride), out_shape=(face,...  21.4 us
    pallas_call x1, Pallas kernels, grid_sum(): pl.pallas_call(functools.partial(_grid_sum_kernel, n, solve), out_shape=j...  17.6 us

profile of v9, /device:TPU:1, one launch (start us, length us, event | category | flops | bytes accessed | tf_op | source)
XLA Modules:
  0.0 126.4 jit_solution(12427479362488252270)
XLA Ops:
  0.7 2.1 %fusion.p_ref = f32[16,32,128]{2,1,0:T(8,128)} fusion(bf16[4,1,16,32,128]{4,3,2,1,0:T(8,128)(2,1)} %param.6, f32[4]{0:T(128)} %param.7), kind=kLoop, calls=%fused_computation.10 | loop fusion | flops 983040 | bytes 786448 | tf_op jit(solution)/shard_map/reduce_sum | solution.py:455
  2.8 57.3 %shard_map.77 = (f32[16,32,128]{2,1,0:T(8,128)}, f32[8,128]{1,0:T(8,128)}) custom-call(f32[16,32,128]{2,1,0:T(8,128)} %fusion.p_ref, f32[16,32,128]{2,1,0:T(8,128)} %bitcast.60), custom_call_target="tpu_custom_call" | custom-call | tf_op jit(solution)/shard_map/pallas_call | solution.py:334
  60.1 1.3 %fusion.29 = (f32[1,1]{1,0:T(1,128)}, f32[1,1]{1,0:T(1,128)}) fusion(f32[8,128]{1,0:T(8,128)} %get-tuple-element.10), kind=kLoop, calls=%fused_computation.78 | loop fusion | bytes 16 | tf_op jit(solution)/shard_map/slice | solution.py:462
  62.8 1.7 %multiply_reduce_fusion.2 = (f32[]{:T(128)}, f32[1,16,32,128]{3,2,1,0:T(8,128)S(1)}) fusion(f32[1,16,32,128]{3,2,1,0:T(8,128)} %param.8, f32[16,32,128]{2,1,0:T(8,128)} %get-tuple-element.11, f32[]{:T(128)} %bitcast.1), kind=kLoop, calls=%fused_computation.60 | loop fusion | flops 262143 | bytes 786440 | tf_op jit(solution)/shard_map/reduce_sum | solution.py:466
  64.5 0.3 multiply_reduce_fusion.1
  64.9 0.6 maximum_bitcast_fusion
  65.6 0.6 copy.62
  66.2 1.9 %multiply_reduce_fusion = f32[8,8]{1,0:T(8,128)S(1)} fusion(f32[8,65536]{1,0:T(8,128)S(1)} %bitcast.54), kind=kLoop, calls=%fused_computation | loop fusion | flops 8388544 | bytes 2097408 | tf_op jit(solution)/shard_map/reduce_sum | solution.py:461
  68.0 0.7 select_maximum_fusion.x_ref
  68.7 17.6 %shard_map.78 = f32[16,128]{1,0:T(8,128)} custom-call(f32[16,128]{1,0:T(8,128)} %select_maximum_fusion.x_ref), custom_call_target="tpu_custom_call" | custom-call | tf_op jit(solution)/shard_map/pallas_call | solution.py:125
  86.4 0.8 slice_reduce_fusion
  87.2 1.3 %fusion.1 = f32[1,16,32,128]{3,0,2,1:T(1,128)S(1)} fusion(bf16[8,16,32,128]{3,2,1,0:T(8,128)(2,1)S(1)} %bitcast.56, f32[8]{0:T(128)S(1)} %slice_reduce_fusion), kind=kOutput, calls=%fused_computation.11 | convolution fusion | flops 6291456 | bytes 1310752 | tf_op jit(solution)/shard_map/m,mgxyz->gxyz/dot_general | solution.py:482
  88.4 1.3 %slice.124 = f32[1,1]{1,0:T(1,128)} slice(f32[16,128]{1,0:T(8,128)} %shard_map.78), slice={[8:9], [0:1]} | slice | bytes 8 | tf_op jit(solution)/shard_map/slice | solution.py:479
  89.7 0.7 multiply_add_fusion
  90.4 0.6 slice_bitcast_fusion
  91.1 5.1 %shard_map.79 = (f32[3,32,128]{2,1,0:T(8,128)}, f32[3,32,128]{2,1,0:T(8,128)}) custom-call(f32[3,32,128]{2,1,0:T(8,128)} %get-tuple-element.35.lo_ref, f32[3,32,128]{2,1,0:T(8,128)} %get-tuple-element.34.hi_ref), custom_call_target="tpu_custom_call" | custom-call | tf_op jit(solution)/shard_map/pallas_call | solution.py:412
  96.2 1.4 %pad_maximum_fusion.2 = (f32[22,3,128]{2,1,0:T(4,128)}, f32[22,3,128]{2,1,0:T(4,128)}) fusion(f32[3,32,128]{2,1,0:T(8,128)} %get-tuple-element.13, f32[16,32,128]{2,1,0:T(8,128)S(1)} %bitcast.57, f32[3,32,128]{2,1,0:T(8,128)} %get-tuple-element.12), kind=kLoop, calls=%fused_computation.63 | loop fusion | flops 33792 | bytes 428032 | tf_op jit(solution)/shard_map/concatenate | solution.py:494
  97.6 7.6 %shard_map.80 = (f32[22,3,128]{2,1,0:T(4,128)}, f32[22,3,128]{2,1,0:T(4,128)}) custom-call(f32[22,3,128]{2,1,0:T(4,128)} %get-tuple-element.33.lo_ref, f32[22,3,128]{2,1,0:T(4,128)} %get-tuple-element.32.hi_ref), custom_call_target="tpu_custom_call" | custom-call | tf_op jit(solution)/shard_map/pallas_call | solution.py:412
  105.2 0.9 pad_maximum_fusion.1
  106.2 0.2 fusion.28
  106.4 0.9 copy.54
  107.3 0.9 copy.55
  108.1 8.7 %shard_map.81 = (f32[3,22,38]{2,1,0:T(8,128)}, f32[3,22,38]{2,1,0:T(8,128)}) custom-call(f32[3,22,38]{2,1,0:T(8,128)} %bitcast.64, f32[3,22,38]{2,1,0:T(8,128)} %bitcast.65), custom_call_target="tpu_custom_call" | custom-call | tf_op jit(solution)/shard_map/pallas_call | solution.py:412
  116.8 1.0 copy.46
  117.9 1.0 copy.47
  119.8 1.1 fusion.12
  120.8 0.7 divide_select_fusion.1
  121.5 0.6 divide_select_fusion
  122.2 0.6 slice_add_fusion
  122.8 0.2 and_and_fusion
  123.1 1.3 %fusion.3 = f32[1,16,32,128]{3,0,2,1:T(1,128)S(1)} fusion(bf16[8,16,32,128]{3,2,1,0:T(8,128)(2,1)S(1)} %bitcast.53, f32[8]{0:T(128)S(1)} %slice_reduce_fusion), kind=kOutput, calls=%fused_computation.13 | convolution fusion | flops 6291456 | bytes 1310752 | tf_op jit(solution)/shard_map/m,mgxyz->gxyz/dot_general | solution.py:473
  124.3 2.0 %fusion.25 = f32[1,16,32,128]{3,2,1,0:T(8,128)} fusion(f32[1,16,32,128]{3,2,1,0:T(8,128)S(1)} %multiply_add_fusion, f32[22,38,134]{2,1,0:T(8,128)S(1)} %get-tuple-element.23, f32[22,38,134]{2,1,0:T(8,128)S(1)} %get-tuple-element.29, f32[22,38,134]{2,1,0:T(8,128)S(1)} %get-tuple-element.28, f32[22,38,134]{2,1,0:T(8,128)S(1)} %get-tuple-element.27, ...), kind=kLoop, calls=%fused_computation.54 | loop fusion | flops 786432 | bytes 2424844 | tf_op jit(solution)/shard_map/add | solution.py:515
  (21 shorter events, 0.2 us)
Async XLA Ops:
  0.6 122.4 %copy-start = (bf16[8,1,16,32,128]{4,3,2,1,0:T(8,128)(2,1)S(1)}, bf16[8,1,16,32,128]{4,3,2,1,0:T(8,128)(2,1)}, u32[]{:S(2)}) copy-start(bf16[8,1,16,32,128]{4,3,2,1,0:T(8,128)(2,1)} %param.9) | copy-start | bytes 3145732
  0.6 63.9 %copy-start.1 = (bf16[8,1,16,32,128]{4,3,2,1,0:T(8,128)(2,1)S(1)}, bf16[8,1,16,32,128]{4,3,2,1,0:T(8,128)(2,1)}, u32[]{:S(2)}) copy-start(bf16[8,1,16,32,128]{4,3,2,1,0:T(8,128)(2,1)} %param.10) | copy-start | bytes 3145732
  64.5 25.2 %copy-start.3 = (f32[1,16,32,128]{3,2,1,0:T(8,128)}, f32[1,16,32,128]{3,2,1,0:T(8,128)S(1)}, u32[]{:S(2)}) copy-start(f32[1,16,32,128]{3,2,1,0:T(8,128)S(1)} %get-tuple-element.25) | copy-start | bytes 786436
  106.2 13.6 %copy-start.4 = (f32[3,32,128]{2,1,0:T(8,128)S(1)}, f32[3,32,128]{2,1,0:T(8,128)}, u32[]{:S(2)}) copy-start(f32[3,32,128]{2,1,0:T(8,128)} %get-tuple-element.12) | copy-start | bytes 147460
  106.2 13.6 %copy-start.5 = (f32[3,32,128]{2,1,0:T(8,128)S(1)}, f32[3,32,128]{2,1,0:T(8,128)}, u32[]{:S(2)}) copy-start(f32[3,32,128]{2,1,0:T(8,128)} %get-tuple-element.13) | copy-start | bytes 147460
  106.2 13.6 %copy-start.6 = (f32[22,3,128]{2,1,0:T(4,128)S(1)}, f32[22,3,128]{2,1,0:T(4,128)}, u32[]{:S(2)}) copy-start(f32[22,3,128]{2,1,0:T(4,128)} %get-tuple-element.14) | copy-start | bytes 101380
  106.2 13.6 %copy-start.7 = (f32[22,3,128]{2,1,0:T(4,128)S(1)}, f32[22,3,128]{2,1,0:T(4,128)}, u32[]{:S(2)}) copy-start(f32[22,3,128]{2,1,0:T(4,128)} %get-tuple-element.15) | copy-start | bytes 101380
  122.2 2.2 %copy-start.2 = (f32[1,16,32,128]{3,2,1,0:T(8,128)S(1)}, f32[1,16,32,128]{3,2,1,0:T(8,128)}, u32[]{:S(2)}) copy-start(f32[1,16,32,128]{3,2,1,0:T(8,128)} %param.8) | copy-start | bytes 786436

commit v10 on v9

--- a/solution.py
+++ b/solution.py
@@ -49,6 +49,112 @@
     return z / jnp.sum(z, axis=0, keepdims=True)
 
 
+def _mix_kernel(n, hres_ref, hin_ref, rho_ref, din_ref, ch_ref, hg_ref, res_ref, ropt_ref, sopt_ref,
+                mine, buf_a, sum_a, buf_b, sa, ra, sb, rb):
+    depth = hres_ref.shape[0]
+    me = lax.axis_index("grid")
+    band = lax.axis_index("band")
+    na = buf_a.shape[0]
+    nb = n // na
+    row = me // na
+    j = me % na
+    barrier = pltpu.get_barrier_semaphore()
+
+    def greet_a(k, c):
+        pl.semaphore_signal(barrier, inc=1, device_id=(row * na + lax.rem(j + k, na), band), device_id_type=MESH)
+        return c
+
+    lax.fori_loop(1, na, greet_a, 0)
+    for k in range(1, nb):
+        pl.semaphore_signal(barrier, inc=1, device_id=(lax.rem(row + k, nb) * na + j, band), device_id_type=MESH)
+
+    first = lax.broadcasted_iota(jnp.int32, ch_ref.shape, 0) == 0
+    lane = lax.broadcasted_iota(jnp.int32, ch_ref.shape, 1)
+    charges = ch_ref[...]
+    scale = jnp.sum(jnp.where(first & (lane == 1), charges, 0.0)) / jnp.sum(jnp.where(first & (lane == 0), charges, 0.0))
+    residual = scale * rho_ref[...] - din_ref[...]
+    res_ref[...] = residual
+    t_row = lax.broadcasted_iota(jnp.int32, hg_ref.shape, 0)
+    t_col = lax.broadcasted_iota(jnp.int32, hg_ref.shape, 1)
+    gram = hg_ref[...]
+    for i in range(depth):
+        dot = jnp.sum(hres_ref[i].astype(jnp.float32) * residual)
+        gram = gram + jnp.where(((t_row == i) & (t_col == depth)) | ((t_row == depth) & (t_col == i)), dot, 0.0)
+    gram = gram + jnp.where((t_row == depth) & (t_col == depth), jnp.sum(residual * residual), 0.0)
+    mine[...] = gram
+    pl.semaphore_wait(barrier, na - 1 + nb - 1)
+
+    def copy_a(src_slot, peer_j):
+        return pltpu.make_async_remote_copy(
+            src_ref=mine, dst_ref=buf_a.at[src_slot], send_sem=sa.at[peer_j], recv_sem=ra.at[src_slot],
+            device_id=(row * na + peer_j, band), device_id_type=MESH,
+        )
+
+    def send_a(k, c):
+        copy_a(j, lax.rem(j + k, na)).start()
+        return c
+
+    lax.fori_loop(1, na, send_a, 0)
+    buf_a[j] = mine[...]
+
+    def wait_a(k, c):
+        peer = lax.rem(j + k, na)
+        copy_a(j, peer).wait_send()
+        copy_a(peer, peer).wait_recv()
+        return c
+
+    lax.fori_loop(1, na, wait_a, 0)
+    sum_a[...] = lax.fori_loop(1, na, lambda p, acc: acc + buf_a[p], buf_a[0])
+
+    def copy_b(src_slot, peer_row):
+        return pltpu.make_async_remote_copy(
+            src_ref=sum_a, dst_ref=buf_b.at[src_slot], send_sem=sb.at[peer_row], recv_sem=rb.at[src_slot],
+            device_id=(peer_row * na + j, band), device_id_type=MESH,
+        )
+
+    for k in range(1, nb):
+        copy_b(row, lax.rem(row + k, nb)).start()
+    buf_b[row] = sum_a[...]
+    for k in range(1, nb):
+        peer = lax.rem(row + k, nb)
+        copy_b(row, peer).wait_send()
+        copy_b(peer, peer).wait_recv()
+    acc = buf_b[0]
+    for p in range(1, nb):
+        acc = acc + buf_b[p]
+    coeff = _solve_ones(acc, depth + 1)
+    rows = lax.broadcasted_iota(jnp.int32, coeff.shape, 0)
+    c = [jnp.sum(jnp.where(rows == m, coeff, 0.0)) for m in range(depth + 1)]
+    rho_opt = c[0] * hin_ref[0].astype(jnp.float32)
+    res_opt = c[0] * hres_ref[0].astype(jnp.float32)
+    for m in range(1, depth):
+        rho_opt = rho_opt + c[m] * hin_ref[m].astype(jnp.float32)
+        res_opt = res_opt + c[m] * hres_ref[m].astype(jnp.float32)
+    ropt_ref[...] = rho_opt + c[depth] * din_ref[...]
+    sopt_ref[...] = res_opt + c[depth] * residual
+
+
+def mix(hres, hin, rho, din, charges, hist):
+    n = lax.axis_size("grid")
+    na = 16
+    dma = pltpu.SemaphoreType.DMA
+    field = jax.ShapeDtypeStruct(rho.shape, jnp.float32)
+    return pl.pallas_call(
+        functools.partial(_mix_kernel, n),
+        out_shape=(field, field, field),
+        in_specs=[pl.BlockSpec(memory_space=pltpu.VMEM)] * 6,
+        out_specs=(pl.BlockSpec(memory_space=pltpu.VMEM),) * 3,
+        scratch_shapes=[
+            pltpu.VMEM(hist.shape, jnp.float32),
+            pltpu.VMEM((na,) + hist.shape, jnp.float32),
+            pltpu.VMEM(hist.shape, jnp.float32),
+            pltpu.VMEM((n // na,) + hist.shape, jnp.float32),
+            dma((na,)), dma((na,)), dma((n // na,)), dma((n // na,)),
+        ],
+        compiler_params=pltpu.CompilerParams(collective_id=2, has_side_effects=True),
+    )(hres, hin, rho, din, charges, hist)
+
+
 def _grid_sum_kernel(n, solve, x_ref, o_ref, buf_a, sum_a, buf_b, sa, ra, sb, rb):
     me = lax.axis_index("grid")
     band = lax.axis_index("band")
@@ -150,7 +256,7 @@
     return x
 
 
-def _density_kernel(p_ref, d_ref, o_ref, c_ref, q_in, q_sum, e_in, e_buf, ax_in, a_buf, ay_in, b_buf, bz_in, s_buf,
+def _density_kernel(p_ref, d_ref, h_ref, o_ref, c_ref, hg_ref, q_in, q_sum, e_in, e_buf, ax_in, a_buf, ay_in, b_buf, bz_in, s_buf,
                     tq, full, ga_in, ga_sum, gb_in, t_buf, tz_in, tp_buf, tx_in,
                     s1, r1, s2, r2, sx, rx, sy, ry, sz, rz, s6, r6, s7, r7, sga, rga, sgb, rgb, stz, rtz, stx, rtx):
     g = lax.axis_index("grid")
@@ -238,6 +344,14 @@
     c_b.start()
     e_in[zhi, pl.ds(0, 1)] = q_sum[pl.ds(zhi, 1)]
     e_in[zhi, pl.ds(1, 1)] = q_sum[pl.ds(3 - zhi, 1)]
+    t_row = lax.broadcasted_iota(jnp.int32, hg_ref.shape, 0)
+    t_col = lax.broadcasted_iota(jnp.int32, hg_ref.shape, 1)
+    hist = jnp.zeros(hg_ref.shape, jnp.float32)
+    for i in range(h_ref.shape[0]):
+        for k in range(i, h_ref.shape[0]):
+            dot = jnp.sum(h_ref[i].astype(jnp.float32) * h_ref[k].astype(jnp.float32))
+            hist = hist + jnp.where(((t_row == i) & (t_col == k)) | ((t_row == k) & (t_col == i)), dot, 0.0)
+    hg_ref[...] = hist
     c_a.wait_send()
     c_b.wait_send()
     remote(q_sum.at[pl.ds(0, 1)], e_in.at[1 - zhi, pl.ds(0, 1)], s2.at[0], r2.at[1 - zhi, 0], dev).wait_recv()
@@ -324,7 +438,7 @@
     c_ref[...] = ((tx_in[0] + tx_in[1]) + tx_in[2]) + tx_in[3]
 
 
-def symmetric_density(part, din):
+def symmetric_density(part, din, hist):
     rest = part.shape[1:]
     dma = pltpu.SemaphoreType.DMA
     vm = lambda *s: pltpu.VMEM(s + rest, jnp.float32)
@@ -333,9 +447,13 @@
     na = 16
     return pl.pallas_call(
         _density_kernel,
-        out_shape=(jax.ShapeDtypeStruct(part.shape, jnp.float32), jax.ShapeDtypeStruct((8, 128), jnp.float32)),
-        in_specs=[pl.BlockSpec(memory_space=pltpu.VMEM)] * 2,
-        out_specs=(pl.BlockSpec(memory_space=pltpu.VMEM),) * 2,
+        out_shape=(
+            jax.ShapeDtypeStruct(part.shape, jnp.float32),
+            jax.ShapeDtypeStruct((8, 128), jnp.float32),
+            jax.ShapeDtypeStruct((16, 128), jnp.float32),
+        ),
+        in_specs=[pl.BlockSpec(memory_space=pltpu.VMEM)] * 3,
+        out_specs=(pl.BlockSpec(memory_space=pltpu.VMEM),) * 3,
         scratch_shapes=[
             vm(4, 4), vm(4), vm(2, 2), vm(2), vm(2), vm(2), vm(2), vm(2), vm(2), vm(2), vm(4), vm(part.shape[0]),
             tile(na), tile(), tile(n // na), tile(), tile(2), tile(), tile(4),
@@ -344,7 +462,7 @@
             dma((na,)), dma((na,)), dma((n // na,)), dma((n // na,)), dma(()), dma((2,)), dma((4,)), dma((4,)),
         ],
         compiler_params=pltpu.CompilerParams(collective_id=3, has_side_effects=True),
-    )(part, din)
+    )(part, din, hist)
 
 
 def _swap_kernel(stride, lo_ref, hi_ref, from_lo_ref, from_hi_ref, got_lo, got_hi, s_lo, s_hi, r_lo, r_hi):
@@ -453,35 +571,11 @@
 def local(orbitals, occupations, density_in, history_in, history_res, screening):
     waves = orbitals.astype(jnp.float32)
     partial_value = jnp.sum(occupations[:, None, None, None, None] * waves * waves, 0)
-    rho_block, charges = symmetric_density(partial_value[0], density_in[0])
-    rho_sym = rho_block[None]
-    depth = history_res.shape[0]
-    res_hist = history_res.astype(jnp.float32)
-    hist_flat = res_hist.reshape(depth, -1)
-    hist_gram = jnp.sum(hist_flat[:, None, :] * hist_flat[None, :, :], axis=-1)
-    scale = charges[0, 1] / charges[0, 0]
-    residual = scale * rho_sym - density_in
-    res_flat = residual.reshape(-1)
-    last_row = jnp.sum(hist_flat * res_flat[None, :], axis=-1)
-    last = jnp.sum(res_flat * res_flat)
-    local_gram = jnp.concatenate(
-        [jnp.concatenate([hist_gram, last_row[:, None]], 1), jnp.concatenate([last_row, last[None]])[None]], 0
-    )
-    local_gram = jnp.pad(local_gram, ((0, 16 - depth - 1), (0, 128 - depth - 1)))
-    coefficients = grid_sum(local_gram, 2, depth + 1)[: depth + 1, 0]
-    rho_opt = (
-        jnp.einsum(
-            "m,mgxyz->gxyz",
-            coefficients[:depth],
-            history_in.astype(jnp.float32),
-            precision=lax.Precision.HIGHEST,
-        )
-        + coefficients[depth] * density_in
-    )
-    res_opt = (
-        jnp.einsum("m,mgxyz->gxyz", coefficients[:depth], res_hist, precision=lax.Precision.HIGHEST)
-        + coefficients[depth] * residual
-    )
+    rho_block, charges, hist = symmetric_density(partial_value[0], density_in[0], history_res[:, 0])
+    residual, rho_opt, res_opt = mix(history_res[:, 0], history_in[:, 0], rho_block, density_in[0], charges, hist)
+    residual = residual[None]
+    rho_opt = rho_opt[None]
+    res_opt = res_opt[None]
     kappa = screening[0]
     index = lax.axis_index("grid")
     block_x = index // 16

time: 127 us -> 118 us (0.929)
  other arithmetic: 15.7 us -> 7.34 us
  matrix products: 2.54 us -> 0 us
  Pallas kernels: 96.4 us -> 98.6 us
  between operations: 2.91 us -> 1.5 us
    reduce_sum x3 -> x0, other arithmetic: 3.9 us -> none  [the longest x1 1.85 us: local(): hist_gram = jnp.sum(hist_flat[:, None, :] * hist_flat[None, :, :], axis=-1)]
    unnamed x19 -> x21, local copies, waits for them, and re-layouts: 2.39 us -> 5.51 us
    slice x3 -> x1, local copies, waits for them, and re-layouts: 3.41 us -> 0.65 us  [local(): lo, hi = swap_faces(ext[:, :h], ext[:, -h:], 4, 5)]
    dot_general x2 -> x0, matrix products: 2.54 us -> none  [the longest x1 1.27 us: local(): jnp.einsum('m,mgxyz->gxyz', coefficients[:depth], res_hist, precision=lax...]
    concatenate x2 -> x0, other arithmetic: 2.09 us -> none  [the longest x1 1.41 us: local(): ext = jnp.concatenate([lo, source, hi], 0)]
    pallas_call x1, Pallas kernels: 17.6 us -> 19.4 us  [mix(): pl.pallas_call(functools.partial(_mix_kernel, n), out_shape=(field, field...]
where the time goes in v10:
time: 118 us; the launch traced here: 117 us
  Pallas kernels  98.6 us (84%)
  local copies, waits for them, and re-layouts  9.25 us (8%)
  other arithmetic  7.34 us (6%)
  between operations  1.5 us (1%)
    pallas_call x1, Pallas kernels, symmetric_density(): pl.pallas_call(_density_kernel, out_shape=(jax.ShapeDtypeStruct(part.shap...  57.7 us
    pallas_call x3, Pallas kernels, swap_faces(): pl.pallas_call(functools.partial(_swap_kernel, stride), out_shape=(face,...  21.4 us
    pallas_call x1, Pallas kernels, mix(): pl.pallas_call(functools.partial(_mix_kernel, n), out_shape=(field, field...  19.4 us
    unnamed x21, local copies, waits for them, and re-layouts  5.51 us
    mul x3, other arithmetic, local(): field_u = (ext + beside) / (6.0 + kappa) * mask  2.4 us

profile of v10, /device:TPU:1, one launch (start us, length us, event | category | flops | bytes accessed | tf_op | source)
XLA Modules:
  0.0 116.7 jit_solution(2803989059785298858)
XLA Ops:
  0.6 0.0 copy-start.7
  0.6 0.6 copy-done.7
  1.3 2.0 %fusion.p_ref = f32[16,32,128]{2,1,0:T(8,128)} fusion(bf16[4,1,16,32,128]{4,3,2,1,0:T(8,128)(2,1)} %param.6, f32[4]{0:T(128)S(1)} %copy-done.7), kind=kLoop, calls=%fused_computation.7 | loop fusion | flops 983040 | bytes 786448 | tf_op jit(solution)/shard_map/reduce_sum | solution.py:573
  3.3 57.7 %shard_map.77 = (f32[16,32,128]{2,1,0:T(8,128)}, f32[8,128]{1,0:T(8,128)}, f32[16,128]{1,0:T(8,128)}) custom-call(f32[16,32,128]{2,1,0:T(8,128)} %fusion.p_ref, f32[16,32,128]{2,1,0:T(8,128)} %bitcast.16, bf16[8,16,32,128]{3,2,1,0:T(8,128)(2,1)} %bitcast.13), custom_call_target="tpu_custom_call" | custom-call | tf_op jit(solution)/shard_map/pallas_call | solution.py:448
  61.0 19.4 %shard_map.78 = (f32[16,32,128]{2,1,0:T(8,128)}, f32[16,32,128]{2,1,0:T(8,128)}, f32[16,32,128]{2,1,0:T(8,128)}) custom-call(bf16[8,16,32,128]{3,2,1,0:T(8,128)(2,1)} %bitcast.14, bf16[8,16,32,128]{3,2,1,0:T(8,128)(2,1)} %bitcast.15, f32[16,32,128]{2,1,0:T(8,128)} %get-tuple-element.14.rho_ref, f32[16,32,128]{2,1,0:T(8,128)} %bitcast.17, ...), custom_call_target="tpu_custom_call" | custom-call | tf_op jit(solution)/shard_map/pallas_call | solution.py:142
  80.5 0.0 copy-start
  80.5 1.5 %fusion.24 = (f32[3,32,128]{2,1,0:T(8,128)}, f32[3,32,128]{2,1,0:T(8,128)}) fusion(f32[16,32,128]{2,1,0:T(8,128)} %get-tuple-element.18), kind=kLoop, calls=%fused_computation.59 | loop fusion | bytes 196608 | tf_op jit(solution)/shard_map/slice | solution.py:587
  82.0 5.1 %shard_map.79 = (f32[3,32,128]{2,1,0:T(8,128)}, f32[3,32,128]{2,1,0:T(8,128)}) custom-call(f32[3,32,128]{2,1,0:T(8,128)} %get-tuple-element.39.lo_ref, f32[3,32,128]{2,1,0:T(8,128)} %get-tuple-element.38.hi_ref), custom_call_target="tpu_custom_call" | custom-call | tf_op jit(solution)/shard_map/pallas_call | solution.py:530
  87.1 0.8 constant_dynamic-update-slice_fusion.2
  87.9 0.0 copy-done
  88.0 0.8 copy-done.5
  88.7 0.7 fusion.23
  89.4 7.6 %shard_map.80 = (f32[22,3,128]{2,1,0:T(4,128)}, f32[22,3,128]{2,1,0:T(4,128)}) custom-call(f32[22,3,128]{2,1,0:T(4,128)} %get-tuple-element.37.lo_ref, f32[22,3,128]{2,1,0:T(4,128)} %get-tuple-element.36.hi_ref), custom_call_target="tpu_custom_call" | custom-call | tf_op jit(solution)/shard_map/pallas_call | solution.py:530
  97.0 0.9 pad_maximum_fusion.1
  97.9 0.2 fusion.22
  98.0 0.9 copy.22
  98.9 0.9 copy.23
  99.8 8.7 %shard_map.81 = (f32[3,22,38]{2,1,0:T(8,128)}, f32[3,22,38]{2,1,0:T(8,128)}) custom-call(f32[3,22,38]{2,1,0:T(8,128)} %bitcast.19, f32[3,22,38]{2,1,0:T(8,128)} %bitcast.20), custom_call_target="tpu_custom_call" | custom-call | tf_op jit(solution)/shard_map/pallas_call | solution.py:530
  108.5 0.0 copy-start.6
  108.5 1.0 copy.20
  109.6 0.3 copy.21
  110.6 0.1 broadcast_in_dim.4
  110.7 0.7 copy-done.3
  111.4 0.0 copy-done.4
  111.4 1.1 fusion.8
  112.5 0.7 divide_select_fusion.1
  113.2 0.7 divide_select_fusion
  113.8 0.7 slice_add_fusion
  114.5 0.2 and_and_fusion
  114.7 0.1 copy-done.2
  114.8 1.2 %fusion.21 = f32[1,16,32,128]{3,2,1,0:T(8,128)} fusion(f32[16,32,128]{2,1,0:T(8,128)S(1)} %copy-done.2, f32[16,32,128]{2,1,0:T(8,128)S(1)} %copy-done, f32[22,38,134]{2,1,0:T(8,128)S(1)} %get-tuple-element.33, f32[22,38,134]{2,1,0:T(8,128)S(1)} %get-tuple-element.32, f32[22,38,134]{2,1,0:T(8,128)S(1)} %get-tuple-element.31, ...), kind=kLoop, calls=%fused_computation.50 | loop fusion | flops 655360 | bytes 2162696 | tf_op jit(solution)/shard_map/add | solution.py:609
  116.0 0.7 copy.28
  (12 shorter events, 0.1 us)
Async XLA Ops:
  0.6 0.7 copy-start.7
  80.5 7.5 %copy-start = (f32[16,32,128]{2,1,0:T(8,128)S(1)}, f32[16,32,128]{2,1,0:T(8,128)}, u32[]{:S(2)}) copy-start(f32[16,32,128]{2,1,0:T(8,128)} %get-tuple-element.18) | copy-start | bytes 786436
  87.9 0.8 copy-start.5
  108.5 1.1 copy-start.6
  110.6 0.8 copy-start.3
  110.6 0.8 copy-start.4
  113.8 1.0 copy-start.2
  114.8 1.2 %copy-start.1 = (f32[16,32,128]{2,1,0:T(8,128)S(1)}, f32[16,32,128]{2,1,0:T(8,128)}, u32[]{:S(2)}) copy-start(f32[16,32,128]{2,1,0:T(8,128)} %get-tuple-element.25) | copy-start | bytes 786436

commit v11 on v10

--- a/solution.py
+++ b/solution.py
@@ -50,7 +50,8 @@
 
 
 def _mix_kernel(n, hres_ref, hin_ref, rho_ref, din_ref, ch_ref, hg_ref, res_ref, ropt_ref, sopt_ref,
-                mine, buf_a, sum_a, buf_b, sa, ra, sb, rb):
+                xlo_ref, xhi_ref, ylo_ref, yhi_ref,
+                mine, buf_a, sum_a, buf_b, xlo_s, xhi_s, xext, ylo_s, yhi_s, sa, ra, sb, rb, hx, hy):
     depth = hres_ref.shape[0]
     me = lax.axis_index("grid")
     band = lax.axis_index("band")
@@ -132,6 +133,60 @@
         res_opt = res_opt + c[m] * hres_ref[m].astype(jnp.float32)
     ropt_ref[...] = rho_opt + c[depth] * din_ref[...]
     sopt_ref[...] = res_opt + c[depth] * residual
+    h = xlo_s.shape[0]
+    cx = sopt_ref.shape[0]
+    cy = sopt_ref.shape[1]
+    wy = ylo_s.shape[1]
+
+    def exchange(lo_src, hi_src, lo_dst, hi_dst, sems, has_lo, has_hi, lo_dev, hi_dev, lo_out, hi_out):
+        def to_lo(dev):
+            return pltpu.make_async_remote_copy(
+                src_ref=lo_src, dst_ref=hi_dst, send_sem=sems.at[0], recv_sem=sems.at[3], device_id=dev,
+                device_id_type=MESH,
+            )
+
+        def to_hi(dev):
+            return pltpu.make_async_remote_copy(
+                src_ref=hi_src, dst_ref=lo_dst, send_sem=sems.at[1], recv_sem=sems.at[2], device_id=dev,
+                device_id_type=MESH,
+            )
+
+        @pl.when(has_lo)
+        def _():
+            to_lo(lo_dev).start()
+
+        @pl.when(has_hi)
+        def _():
+            to_hi(hi_dev).start()
+
+        @pl.when(has_lo)
+        def _():
+            to_lo(lo_dev).wait_send()
+            to_hi(lo_dev).wait_recv()
+            lo_out[...] = lo_dst[...]
+
+        @pl.when(has_hi)
+        def _():
+            to_hi(hi_dev).wait_send()
+            to_lo(hi_dev).wait_recv()
+            hi_out[...] = hi_dst[...]
+
+        @pl.when(jnp.logical_not(has_lo))
+        def _():
+            lo_out[...] = jnp.zeros(lo_out.shape, jnp.float32)
+
+        @pl.when(jnp.logical_not(has_hi))
+        def _():
+            hi_out[...] = jnp.zeros(hi_out.shape, jnp.float32)
+
+    exchange(sopt_ref.at[pl.ds(0, h)], sopt_ref.at[pl.ds(cx - h, h)], xlo_s, xhi_s, hx,
+             row > 0, row < nb - 1, ((row - 1) * na + j, band), ((row + 1) * na + j, band), xlo_ref, xhi_ref)
+    xext[pl.ds(0, h)] = xlo_ref[...]
+    xext[pl.ds(h, cx)] = sopt_ref[...]
+    xext[pl.ds(h + cx, h)] = xhi_ref[...]
+    by = j // 4
+    exchange(xext.at[:, pl.ds(0, wy)], xext.at[:, pl.ds(cy - wy, wy)], ylo_s, yhi_s, hy,
+             by > 0, by < 3, (me - 4, band), (me + 4, band), ylo_ref, yhi_ref)
 
 
 def mix(hres, hin, rho, din, charges, hist):
@@ -139,17 +194,26 @@
     na = 16
     dma = pltpu.SemaphoreType.DMA
     field = jax.ShapeDtypeStruct(rho.shape, jnp.float32)
+    cx, cy, cz = rho.shape
+    h, wy = SWEEPS - 1, 8
+    xface = (h, cy, cz)
+    yface = (cx + 2 * h, wy, cz)
     return pl.pallas_call(
         functools.partial(_mix_kernel, n),
-        out_shape=(field, field, field),
+        out_shape=(field, field, field) + tuple(jax.ShapeDtypeStruct(s, jnp.float32) for s in (xface, xface, yface, yface)),
         in_specs=[pl.BlockSpec(memory_space=pltpu.VMEM)] * 6,
-        out_specs=(pl.BlockSpec(memory_space=pltpu.VMEM),) * 3,
+        out_specs=(pl.BlockSpec(memory_space=pltpu.VMEM),) * 7,
         scratch_shapes=[
             pltpu.VMEM(hist.shape, jnp.float32),
             pltpu.VMEM((na,) + hist.shape, jnp.float32),
             pltpu.VMEM(hist.shape, jnp.float32),
             pltpu.VMEM((n // na,) + hist.shape, jnp.float32),
-            dma((na,)), dma((na,)), dma((n // na,)), dma((n // na,)),
+            pltpu.VMEM(xface, jnp.float32),
+            pltpu.VMEM(xface, jnp.float32),
+            pltpu.VMEM((cx + 2 * h, cy, cz), jnp.float32),
+            pltpu.VMEM(yface, jnp.float32),
+            pltpu.VMEM(yface, jnp.float32),
+            dma((na,)), dma((na,)), dma((n // na,)), dma((n // na,)), dma((4,)), dma((4,)),
         ],
         compiler_params=pltpu.CompilerParams(collective_id=2, has_side_effects=True),
     )(hres, hin, rho, din, charges, hist)
@@ -572,7 +636,9 @@
     waves = orbitals.astype(jnp.float32)
     partial_value = jnp.sum(occupations[:, None, None, None, None] * waves * waves, 0)
     rho_block, charges, hist = symmetric_density(partial_value[0], density_in[0], history_res[:, 0])
-    residual, rho_opt, res_opt = mix(history_res[:, 0], history_in[:, 0], rho_block, density_in[0], charges, hist)
+    residual, rho_opt, res_opt, x_lo, x_hi, y_lo, y_hi = mix(
+        history_res[:, 0], history_in[:, 0], rho_block, density_in[0], charges, hist
+    )
     residual = residual[None]
     rho_opt = rho_opt[None]
     res_opt = res_opt[None]
@@ -584,10 +650,8 @@
     source = res_opt[0]
     h = SWEEPS - 1
     cx, cy, cz = source.shape
-    lo, hi = swap_faces(source[:h], source[-h:], 16, 4)
-    ext = jnp.concatenate([lo, source, hi], 0)
-    lo, hi = swap_faces(ext[:, :h], ext[:, -h:], 4, 5)
-    ext = jnp.concatenate([lo, ext, hi], 1)
+    ext = jnp.concatenate([x_lo, source, x_hi], 0)
+    ext = jnp.concatenate([y_lo[:, -h:], ext, y_hi[:, :h]], 1)
     lo, hi = swap_faces(jnp.transpose(ext[:, :, :h], (2, 0, 1)), jnp.transpose(ext[:, :, -h:], (2, 0, 1)), 1, 6)
     ext = jnp.concatenate([jnp.transpose(lo, (1, 2, 0)), ext, jnp.transpose(hi, (1, 2, 0))], 2)
 

time: 118 us -> 108 us (0.915)
  Pallas kernels: 98.6 us -> 90.7 us
  local copies, waits for them, and re-layouts: 9.25 us -> 7.33 us
    pallas_call x3 -> x1, Pallas kernels: 21.4 us -> 6.91 us  [swap_faces(): pl.pallas_call(functools.partial(_swap_kernel, stride), out_shape=(face,...]
    pallas_call x1, Pallas kernels: 19.4 us -> 26.1 us  [mix(): pl.pallas_call(functools.partial(_mix_kernel, n), out_shape=(field, field...]
    slice x2, local copies, waits for them, and re-layouts: 2.16 us -> 0.94 us  [local(): ext = jnp.concatenate([y_lo[:, -h:], ext, y_hi[:, :h]], 1)]
    unnamed x21 -> x19, local copies, waits for them, and re-layouts: 5.51 us -> 4.81 us
where the time goes in v11:
time: 108 us; the launch traced here: 107 us
  Pallas kernels  90.7 us (84%)
  other arithmetic  7.46 us (7%)
  local copies, waits for them, and re-layouts  7.33 us (7%)
  between operations  1.51 us (1%)
    pallas_call x1, Pallas kernels, symmetric_density(): pl.pallas_call(_density_kernel, out_shape=(jax.ShapeDtypeStruct(part.shap...  57.7 us
    pallas_call x1, Pallas kernels, mix(): pl.pallas_call(functools.partial(_mix_kernel, n), out_shape=(field, field...  26.1 us
    pallas_call x1, Pallas kernels, swap_faces(): pl.pallas_call(functools.partial(_swap_kernel, stride), out_shape=(face,...  6.91 us
    unnamed x19, local copies, waits for them, and re-layouts  4.81 us
    mul x3, other arithmetic, local(): field_u = (ext + beside) / (6.0 + kappa) * mask  2.32 us

profile of v11, /device:TPU:1, one launch (start us, length us, event | category | flops | bytes accessed | tf_op | source)
XLA Modules:
  0.0 107.0 jit_solution(15602857155151787431)
XLA Ops:
  0.6 0.0 copy-start.7
  0.6 0.6 copy-done.7
  1.3 2.0 %fusion.p_ref = f32[16,32,128]{2,1,0:T(8,128)} fusion(bf16[4,1,16,32,128]{4,3,2,1,0:T(8,128)(2,1)} %param.6, f32[4]{0:T(128)S(1)} %copy-done.7), kind=kLoop, calls=%fused_computation.7 | loop fusion | flops 983040 | bytes 786448 | tf_op jit(solution)/shard_map/reduce_sum | solution.py:637
  3.3 57.7 %shard_map.77 = (f32[16,32,128]{2,1,0:T(8,128)}, f32[8,128]{1,0:T(8,128)}, f32[16,128]{1,0:T(8,128)}) custom-call(f32[16,32,128]{2,1,0:T(8,128)} %fusion.p_ref, f32[16,32,128]{2,1,0:T(8,128)} %bitcast.16, bf16[8,16,32,128]{3,2,1,0:T(8,128)(2,1)} %bitcast.13), custom_call_target="tpu_custom_call" | custom-call | tf_op jit(solution)/shard_map/pallas_call | solution.py:512
  61.0 26.1 %shard_map.78 = (f32[16,32,128]{2,1,0:T(8,128)}, f32[16,32,128]{2,1,0:T(8,128)}, f32[16,32,128]{2,1,0:T(8,128)}, f32[3,32,128]{2,1,0:T(8,128)}, f32[3,32,128]{2,...) custom-call(bf16[8,16,32,128]{3,2,1,0:T(8,128)(2,1)} %bitcast.14, bf16[8,16,32,128]{3,2,1,0:T(8,128)(2,1)} %bitcast.15, ...), custom_call_target="tpu_custom_call" | custom-call | tf_op jit(solution)/shard_map/pallas_call | solution.py:201
  87.1 0.0 copy-start.6
  87.1 0.0 copy-start.4
  87.1 0.9 slice.87
  88.0 0.0 copy-start.3
  88.0 0.0 copy-done.6
  88.1 0.0 copy-done.4
  88.1 0.8 copy-done.3
  88.8 1.0 pad_maximum_fusion.1
  89.8 0.2 fusion.22
  90.0 0.9 copy.20
  90.9 0.9 copy.21
  91.8 6.9 %shard_map.79 = (f32[3,22,38]{2,1,0:T(8,128)}, f32[3,22,38]{2,1,0:T(8,128)}) custom-call(f32[3,22,38]{2,1,0:T(8,128)} %bitcast.19, f32[3,22,38]{2,1,0:T(8,128)} %bitcast.20), custom_call_target="tpu_custom_call" | custom-call | tf_op jit(solution)/shard_map/pallas_call | solution.py:594
  98.7 0.0 copy-start.5
  98.7 1.0 copy.18
  99.7 0.0 copy-done.5
  99.7 0.3 copy.19
  100.8 0.0 copy-start
  100.8 0.1 broadcast_in_dim.4
  100.8 0.9 copy-done
  101.7 1.0 fusion.8
  102.8 0.6 divide_select_fusion.1
  103.4 0.7 divide_select_fusion
  104.1 0.7 slice_add_fusion
  104.7 0.2 and_and_fusion
  104.9 0.1 copy-done.2
  105.0 1.3 %fusion.21 = f32[1,16,32,128]{3,2,1,0:T(8,128)} fusion(f32[16,32,128]{2,1,0:T(8,128)S(1)} %copy-done.2, f32[16,32,128]{2,1,0:T(8,128)S(1)} %copy-done, f32[22,38,134]{2,1,0:T(8,128)S(1)} %get-tuple-element.33, f32[22,38,134]{2,1,0:T(8,128)S(1)} %get-tuple-element.32, f32[22,38,134]{2,1,0:T(8,128)S(1)} %get-tuple-element.31, ...), kind=kLoop, calls=%fused_computation.50 | loop fusion | flops 655360 | bytes 2162696 | tf_op jit(solution)/shard_map/add | solution.py:673
  106.3 0.7 copy.24
  (7 shorter events, 0.0 us)
Async XLA Ops:
  0.6 0.7 copy-start.7
  87.1 1.0 copy-start.6
  87.1 1.0 copy-start.4
  88.0 0.8 copy-start.3
  98.7 1.1 copy-start.5
  100.8 1.0 copy-start
  104.1 1.0 copy-start.2
  105.0 1.3 %copy-start.1 = (f32[16,32,128]{2,1,0:T(8,128)S(1)}, f32[16,32,128]{2,1,0:T(8,128)}, u32[]{:S(2)}) copy-start(f32[16,32,128]{2,1,0:T(8,128)} %get-tuple-element.25) | copy-start | bytes 786436

commit v12 on v11

--- a/solution.py
+++ b/solution.py
@@ -320,7 +320,7 @@
     return x
 
 
-def _density_kernel(p_ref, d_ref, h_ref, o_ref, c_ref, hg_ref, q_in, q_sum, e_in, e_buf, ax_in, a_buf, ay_in, b_buf, bz_in, s_buf,
+def _density_kernel(occ_ref, w_ref, d_ref, h_ref, o_ref, c_ref, hg_ref, p_ref, q_in, q_sum, e_in, e_buf, ax_in, a_buf, ay_in, b_buf, bz_in, s_buf,
                     tq, full, ga_in, ga_sum, gb_in, t_buf, tz_in, tp_buf, tx_in,
                     s1, r1, s2, r2, sx, rx, sy, ry, sz, rz, s6, r6, s7, r7, sga, rga, sgb, rgb, stz, rtz, stx, rtx):
     g = lax.axis_index("grid")
@@ -354,6 +354,10 @@
     lax.fori_loop(1, na, greet, 0)
     for k in range(1, nb):
         pl.semaphore_signal(barrier, inc=1, device_id=(lax.rem(grow + k, nb) * na + gj, b), device_id_type=MESH)
+    part = occ_ref[0] * jnp.square(w_ref[0].astype(jnp.float32))
+    for k in range(1, w_ref.shape[0]):
+        part = part + occ_ref[k] * jnp.square(w_ref[k].astype(jnp.float32))
+    p_ref[...] = part
     pl.semaphore_wait(barrier, 7 + na - 1 + nb - 1)
 
     e = 2 * x + zhi
@@ -502,7 +506,8 @@
     c_ref[...] = ((tx_in[0] + tx_in[1]) + tx_in[2]) + tx_in[3]
 
 
-def symmetric_density(part, din, hist):
+def symmetric_density(occ, waves, din, hist):
+    part = din
     rest = part.shape[1:]
     dma = pltpu.SemaphoreType.DMA
     vm = lambda *s: pltpu.VMEM(s + rest, jnp.float32)
@@ -516,9 +521,10 @@
             jax.ShapeDtypeStruct((8, 128), jnp.float32),
             jax.ShapeDtypeStruct((16, 128), jnp.float32),
         ),
-        in_specs=[pl.BlockSpec(memory_space=pltpu.VMEM)] * 3,
+        in_specs=[pl.BlockSpec(memory_space=pltpu.SMEM)] + [pl.BlockSpec(memory_space=pltpu.VMEM)] * 3,
         out_specs=(pl.BlockSpec(memory_space=pltpu.VMEM),) * 3,
         scratch_shapes=[
+            vm(part.shape[0]),
             vm(4, 4), vm(4), vm(2, 2), vm(2), vm(2), vm(2), vm(2), vm(2), vm(2), vm(2), vm(4), vm(part.shape[0]),
             tile(na), tile(), tile(n // na), tile(), tile(2), tile(), tile(4),
             dma((4, 2)), dma((4, 2)), dma((2,)), dma((2, 2)), dma(()), dma(()), dma(()), dma(()), dma(()), dma(()),
@@ -526,7 +532,7 @@
             dma((na,)), dma((na,)), dma((n // na,)), dma((n // na,)), dma(()), dma((2,)), dma((4,)), dma((4,)),
         ],
         compiler_params=pltpu.CompilerParams(collective_id=3, has_side_effects=True),
-    )(part, din, hist)
+    )(occ, waves, din, hist)
 
 
 def _swap_kernel(stride, lo_ref, hi_ref, from_lo_ref, from_hi_ref, got_lo, got_hi, s_lo, s_hi, r_lo, r_hi):
@@ -633,9 +639,7 @@
 
 
 def local(orbitals, occupations, density_in, history_in, history_res, screening):
-    waves = orbitals.astype(jnp.float32)
-    partial_value = jnp.sum(occupations[:, None, None, None, None] * waves * waves, 0)
-    rho_block, charges, hist = symmetric_density(partial_value[0], density_in[0], history_res[:, 0])
+    rho_block, charges, hist = symmetric_density(occupations, orbitals[:, 0], density_in[0], history_res[:, 0])
     residual, rho_opt, res_opt, x_lo, x_hi, y_lo, y_hi = mix(
         history_res[:, 0], history_in[:, 0], rho_block, density_in[0], charges, hist
     )

time: 108 us -> 105 us (0.972)
  other arithmetic: 7.46 us -> 5.46 us
    reduce_sum x1 -> x0, other arithmetic: 2 us -> none  [local(): jnp.sum(occupations[:, None, None, None, None] * waves * waves, 0)]
    unnamed x19 -> x17, local copies, waits for them, and re-layouts: 4.81 us -> 4.17 us
where the time goes in v12:
time: 105 us
  Pallas kernels  91.2 us (87%)
  local copies, waits for them, and re-layouts  6.68 us (6%)
  other arithmetic  5.46 us (5%)
  between operations  1.5 us (1%)
    pallas_call x1, Pallas kernels, symmetric_density(): pl.pallas_call(_density_kernel, out_shape=(jax.ShapeDtypeStruct(part.shap...  58 us
    pallas_call x1, Pallas kernels, mix(): pl.pallas_call(functools.partial(_mix_kernel, n), out_shape=(field, field...  26.7 us
    pallas_call x1, Pallas kernels, swap_faces(): pl.pallas_call(functools.partial(_swap_kernel, stride), out_shape=(face,...  6.46 us
    unnamed x17, local copies, waits for them, and re-layouts  4.17 us
    mul x3, other arithmetic, local(): field_u = (ext + beside) / (6.0 + kappa) * mask  2.32 us

profile of v12, /device:TPU:1, one launch (start us, length us, event | category | flops | bytes accessed | tf_op | source)
XLA Modules:
  0.0 104.8 jit_solution(788376053449172630)
XLA Ops:
  0.6 58.0 %shard_map.77 = (f32[16,32,128]{2,1,0:T(8,128)}, f32[8,128]{1,0:T(8,128)}, f32[16,128]{1,0:T(8,128)}) custom-call(f32[4]{0:T(128)} %occ_ref.1, bf16[4,16,32,128]{3,2,1,0:T(8,128)(2,1)} %bitcast.19, f32[16,32,128]{2,1,0:T(8,128)} %bitcast.17, bf16[8,16,32,128]{3,2,1,0:T(8,128)(2,1)} %bitcast.14), custom_call_target="tpu_custom_call" | custom-call | tf_op jit(solution)/shard_map/pallas_call | solution.py:517
  58.7 26.7 %shard_map.78 = (f32[16,32,128]{2,1,0:T(8,128)}, f32[16,32,128]{2,1,0:T(8,128)}, f32[16,32,128]{2,1,0:T(8,128)}, f32[3,32,128]{2,1,0:T(8,128)}, f32[3,32,128]{2,...) custom-call(bf16[8,16,32,128]{3,2,1,0:T(8,128)(2,1)} %bitcast.15, bf16[8,16,32,128]{3,2,1,0:T(8,128)(2,1)} %bitcast.16, ...), custom_call_target="tpu_custom_call" | custom-call | tf_op jit(solution)/shard_map/pallas_call | solution.py:201
  85.3 0.0 copy-start.6
  85.4 0.0 copy-start.4
  85.4 0.9 slice.87
  86.3 0.0 copy-start.3
  86.3 0.0 copy-done.6
  86.3 0.0 copy-done.4
  86.3 0.8 copy-done.3
  87.1 1.0 pad_maximum_fusion.1
  88.1 0.2 fusion.21
  88.3 0.9 copy.20
  89.2 0.9 copy.21
  90.0 6.5 %shard_map.79 = (f32[3,22,38]{2,1,0:T(8,128)}, f32[3,22,38]{2,1,0:T(8,128)}) custom-call(f32[3,22,38]{2,1,0:T(8,128)} %bitcast.21, f32[3,22,38]{2,1,0:T(8,128)} %bitcast.22), custom_call_target="tpu_custom_call" | custom-call | tf_op jit(solution)/shard_map/pallas_call | solution.py:600
  96.5 0.0 copy-start.5
  96.5 1.0 copy.18
  97.6 0.0 copy-done.5
  97.6 0.3 copy.19
  98.6 0.0 copy-start
  98.6 0.1 broadcast_in_dim.4
  98.7 0.9 copy-done
  99.5 1.0 fusion.7
  100.6 0.6 divide_select_fusion.1
  101.2 0.7 divide_select_fusion
  101.9 0.0 copy-start.2
  101.9 0.7 slice_add_fusion
  102.6 0.2 and_and_fusion
  102.8 0.1 copy-done.2
  102.8 0.0 copy-start.1
  102.8 1.3 %fusion.20 = f32[1,16,32,128]{3,2,1,0:T(8,128)} fusion(f32[16,32,128]{2,1,0:T(8,128)S(1)} %copy-done.2, f32[16,32,128]{2,1,0:T(8,128)S(1)} %copy-done, f32[22,38,134]{2,1,0:T(8,128)S(1)} %get-tuple-element.33, f32[22,38,134]{2,1,0:T(8,128)S(1)} %get-tuple-element.32, f32[22,38,134]{2,1,0:T(8,128)S(1)} %get-tuple-element.31, ...), kind=kLoop, calls=%fused_computation.48 | loop fusion | flops 655360 | bytes 2162696 | tf_op jit(solution)/shard_map/add | solution.py:677
  104.1 0.0 copy-done.1
  104.1 0.7 copy.24
  (4 shorter events, 0.0 us)
Async XLA Ops:
  85.3 1.0 copy-start.6
  85.4 1.0 copy-start.4
  86.3 0.8 copy-start.3
  96.5 1.1 %copy-start.5 = (f32[3,22,38]{2,1,0:T(8,128)S(1)}, f32[3,22,38]{2,1,0:T(8,128)}, u32[]{:S(2)}) copy-start(f32[3,22,38]{2,1,0:T(8,128)} %get-tuple-element.24) | copy-start | bytes 30100
  98.6 1.0 copy-start
  101.9 1.0 copy-start.2
  102.8 1.3 %copy-start.1 = (f32[16,32,128]{2,1,0:T(8,128)S(1)}, f32[16,32,128]{2,1,0:T(8,128)}, u32[]{:S(2)}) copy-start(f32[16,32,128]{2,1,0:T(8,128)} %get-tuple-element.25) | copy-start | bytes 786436

commit v13 on v10

--- a/solution.py
+++ b/solution.py
@@ -50,7 +50,8 @@
 
 
 def _mix_kernel(n, hres_ref, hin_ref, rho_ref, din_ref, ch_ref, hg_ref, res_ref, ropt_ref, sopt_ref,
-                mine, buf_a, sum_a, buf_b, sa, ra, sb, rb):
+                xlo_ref, xhi_ref, ylo_ref, yhi_ref,
+                mine, buf_a, sum_a, buf_b, xext, ylo_s, yhi_s, sa, ra, sb, rb, hx, hy):
     depth = hres_ref.shape[0]
     me = lax.axis_index("grid")
     band = lax.axis_index("band")
@@ -97,6 +98,60 @@
     lax.fori_loop(1, na, send_a, 0)
     buf_a[j] = mine[...]
 
+    h = SWEEPS - 1
+    cx = rho_ref.shape[0]
+    cy = rho_ref.shape[1]
+    wy = ylo_s.shape[2]
+    for m in range(depth):
+        xext[m, pl.ds(h, cx)] = hres_ref[m].astype(jnp.float32)
+    xext[depth, pl.ds(h, cx)] = residual
+
+    def pair(lo_src, hi_src, lo_dst, hi_dst, sems, has_lo, has_hi, lo_dev, hi_dev):
+        def to_lo(dev):
+            return pltpu.make_async_remote_copy(
+                src_ref=lo_src, dst_ref=hi_dst, send_sem=sems.at[0], recv_sem=sems.at[3], device_id=dev,
+                device_id_type=MESH,
+            )
+
+        def to_hi(dev):
+            return pltpu.make_async_remote_copy(
+                src_ref=hi_src, dst_ref=lo_dst, send_sem=sems.at[1], recv_sem=sems.at[2], device_id=dev,
+                device_id_type=MESH,
+            )
+
+        @pl.when(has_lo)
+        def _():
+            to_lo(lo_dev).start()
+
+        @pl.when(has_hi)
+        def _():
+            to_hi(hi_dev).start()
+
+        def finish():
+            @pl.when(has_lo)
+            def _():
+                to_lo(lo_dev).wait_send()
+                to_hi(lo_dev).wait_recv()
+
+            @pl.when(has_hi)
+            def _():
+                to_hi(hi_dev).wait_send()
+                to_lo(hi_dev).wait_recv()
+
+            @pl.when(jnp.logical_not(has_lo))
+            def _():
+                lo_dst[...] = jnp.zeros(lo_dst.shape, jnp.float32)
+
+            @pl.when(jnp.logical_not(has_hi))
+            def _():
+                hi_dst[...] = jnp.zeros(hi_dst.shape, jnp.float32)
+
+        return finish
+
+    wait_x = pair(xext.at[:, pl.ds(h, h)], xext.at[:, pl.ds(cx, h)], xext.at[:, pl.ds(0, h)],
+                  xext.at[:, pl.ds(h + cx, h)], hx, row > 0, row < nb - 1,
+                  ((row - 1) * na + j, band), ((row + 1) * na + j, band))
+
     def wait_a(k, c):
         peer = lax.rem(j + k, na)
         copy_a(j, peer).wait_send()
@@ -115,6 +170,10 @@
     for k in range(1, nb):
         copy_b(row, lax.rem(row + k, nb)).start()
     buf_b[row] = sum_a[...]
+    wait_x()
+    by = j // 4
+    wait_y = pair(xext.at[:, :, pl.ds(0, wy)], xext.at[:, :, pl.ds(cy - wy, wy)], ylo_s, yhi_s, hy,
+                  by > 0, by < 3, (me - 4, band), (me + 4, band))
     for k in range(1, nb):
         peer = lax.rem(row + k, nb)
         copy_b(row, peer).wait_send()
@@ -132,6 +191,17 @@
         res_opt = res_opt + c[m] * hres_ref[m].astype(jnp.float32)
     ropt_ref[...] = rho_opt + c[depth] * din_ref[...]
     sopt_ref[...] = res_opt + c[depth] * residual
+    def combine(f):
+        out = c[0] * f[0]
+        for m in range(1, depth):
+            out = out + c[m] * f[m]
+        return out + c[depth] * f[depth]
+
+    xlo_ref[...] = combine(xext[:, pl.ds(0, h)])
+    xhi_ref[...] = combine(xext[:, pl.ds(h + cx, h)])
+    wait_y()
+    ylo_ref[...] = combine(ylo_s[...])
+    yhi_ref[...] = combine(yhi_s[...])
 
 
 def mix(hres, hin, rho, din, charges, hist):
@@ -139,17 +209,25 @@
     na = 16
     dma = pltpu.SemaphoreType.DMA
     field = jax.ShapeDtypeStruct(rho.shape, jnp.float32)
+    depth = hres.shape[0]
+    cx, cy, cz = rho.shape
+    h, wy = SWEEPS - 1, 8
+    xface = (h, cy, cz)
+    yface = (cx + 2 * h, wy, cz)
     return pl.pallas_call(
         functools.partial(_mix_kernel, n),
-        out_shape=(field, field, field),
+        out_shape=(field, field, field) + tuple(jax.ShapeDtypeStruct(s, jnp.float32) for s in (xface, xface, yface, yface)),
         in_specs=[pl.BlockSpec(memory_space=pltpu.VMEM)] * 6,
-        out_specs=(pl.BlockSpec(memory_space=pltpu.VMEM),) * 3,
+        out_specs=(pl.BlockSpec(memory_space=pltpu.VMEM),) * 7,
         scratch_shapes=[
             pltpu.VMEM(hist.shape, jnp.float32),
             pltpu.VMEM((na,) + hist.shape, jnp.float32),
             pltpu.VMEM(hist.shape, jnp.float32),
             pltpu.VMEM((n // na,) + hist.shape, jnp.float32),
-            dma((na,)), dma((na,)), dma((n // na,)), dma((n // na,)),
+            pltpu.VMEM((depth + 1, cx + 2 * h, cy, cz), jnp.float32),
+            pltpu.VMEM((depth + 1,) + yface, jnp.float32),
+            pltpu.VMEM((depth + 1,) + yface, jnp.float32),
+            dma((na,)), dma((na,)), dma((n // na,)), dma((n // na,)), dma((4,)), dma((4,)),
         ],
         compiler_params=pltpu.CompilerParams(collective_id=2, has_side_effects=True),
     )(hres, hin, rho, din, charges, hist)
@@ -256,7 +334,7 @@
     return x
 
 
-def _density_kernel(p_ref, d_ref, h_ref, o_ref, c_ref, hg_ref, q_in, q_sum, e_in, e_buf, ax_in, a_buf, ay_in, b_buf, bz_in, s_buf,
+def _density_kernel(occ_ref, w_ref, d_ref, h_ref, o_ref, c_ref, hg_ref, p_ref, q_in, q_sum, e_in, e_buf, ax_in, a_buf, ay_in, b_buf, bz_in, s_buf,
                     tq, full, ga_in, ga_sum, gb_in, t_buf, tz_in, tp_buf, tx_in,
                     s1, r1, s2, r2, sx, rx, sy, ry, sz, rz, s6, r6, s7, r7, sga, rga, sgb, rgb, stz, rtz, stx, rtx):
     g = lax.axis_index("grid")
@@ -290,6 +368,10 @@
     lax.fori_loop(1, na, greet, 0)
     for k in range(1, nb):
         pl.semaphore_signal(barrier, inc=1, device_id=(lax.rem(grow + k, nb) * na + gj, b), device_id_type=MESH)
+    part = occ_ref[0] * jnp.square(w_ref[0].astype(jnp.float32))
+    for k in range(1, w_ref.shape[0]):
+        part = part + occ_ref[k] * jnp.square(w_ref[k].astype(jnp.float32))
+    p_ref[...] = part
     pl.semaphore_wait(barrier, 7 + na - 1 + nb - 1)
 
     e = 2 * x + zhi
@@ -438,7 +520,8 @@
     c_ref[...] = ((tx_in[0] + tx_in[1]) + tx_in[2]) + tx_in[3]
 
 
-def symmetric_density(part, din, hist):
+def symmetric_density(occ, waves, din, hist):
+    part = din
     rest = part.shape[1:]
     dma = pltpu.SemaphoreType.DMA
     vm = lambda *s: pltpu.VMEM(s + rest, jnp.float32)
@@ -452,9 +535,10 @@
             jax.ShapeDtypeStruct((8, 128), jnp.float32),
             jax.ShapeDtypeStruct((16, 128), jnp.float32),
         ),
-        in_specs=[pl.BlockSpec(memory_space=pltpu.VMEM)] * 3,
+        in_specs=[pl.BlockSpec(memory_space=pltpu.SMEM)] + [pl.BlockSpec(memory_space=pltpu.VMEM)] * 3,
         out_specs=(pl.BlockSpec(memory_space=pltpu.VMEM),) * 3,
         scratch_shapes=[
+            vm(part.shape[0]),
             vm(4, 4), vm(4), vm(2, 2), vm(2), vm(2), vm(2), vm(2), vm(2), vm(2), vm(2), vm(4), vm(part.shape[0]),
             tile(na), tile(), tile(n // na), tile(), tile(2), tile(), tile(4),
             dma((4, 2)), dma((4, 2)), dma((2,)), dma((2, 2)), dma(()), dma(()), dma(()), dma(()), dma(()), dma(()),
@@ -462,7 +546,7 @@
             dma((na,)), dma((na,)), dma((n // na,)), dma((n // na,)), dma(()), dma((2,)), dma((4,)), dma((4,)),
         ],
         compiler_params=pltpu.CompilerParams(collective_id=3, has_side_effects=True),
-    )(part, din, hist)
+    )(occ, waves, din, hist)
 
 
 def _swap_kernel(stride, lo_ref, hi_ref, from_lo_ref, from_hi_ref, got_lo, got_hi, s_lo, s_hi, r_lo, r_hi):
@@ -569,10 +653,10 @@
 
 
 def local(orbitals, occupations, density_in, history_in, history_res, screening):
-    waves = orbitals.astype(jnp.float32)
-    partial_value = jnp.sum(occupations[:, None, None, None, None] * waves * waves, 0)
-    rho_block, charges, hist = symmetric_density(partial_value[0], density_in[0], history_res[:, 0])
-    residual, rho_opt, res_opt = mix(history_res[:, 0], history_in[:, 0], rho_block, density_in[0], charges, hist)
+    rho_block, charges, hist = symmetric_density(occupations, orbitals[:, 0], density_in[0], history_res[:, 0])
+    residual, rho_opt, res_opt, x_lo, x_hi, y_lo, y_hi = mix(
+        history_res[:, 0], history_in[:, 0], rho_block, density_in[0], charges, hist
+    )
     residual = residual[None]
     rho_opt = rho_opt[None]
     res_opt = res_opt[None]
@@ -584,10 +668,8 @@
     source = res_opt[0]
     h = SWEEPS - 1
     cx, cy, cz = source.shape
-    lo, hi = swap_faces(source[:h], source[-h:], 16, 4)
-    ext = jnp.concatenate([lo, source, hi], 0)
-    lo, hi = swap_faces(ext[:, :h], ext[:, -h:], 4, 5)
-    ext = jnp.concatenate([lo, ext, hi], 1)
+    ext = jnp.concatenate([x_lo, source, x_hi], 0)
+    ext = jnp.concatenate([y_lo[:, -h:], ext, y_hi[:, :h]], 1)
     lo, hi = swap_faces(jnp.transpose(ext[:, :, :h], (2, 0, 1)), jnp.transpose(ext[:, :, -h:], (2, 0, 1)), 1, 6)
     ext = jnp.concatenate([jnp.transpose(lo, (1, 2, 0)), ext, jnp.transpose(hi, (1, 2, 0))], 2)
 

time: 118 us -> 134 us (1.14)
  Pallas kernels: 98.6 us -> 120 us
  local copies, waits for them, and re-layouts: 9.25 us -> 6.68 us
  other arithmetic: 7.34 us -> 5.46 us
    pallas_call x1, Pallas kernels: 19.4 us -> 56.2 us  [mix(): pl.pallas_call(functools.partial(_mix_kernel, n), out_shape=(field, field...]
    pallas_call x3 -> x1, Pallas kernels: 21.4 us -> 5.49 us  [swap_faces(): pl.pallas_call(functools.partial(_swap_kernel, stride), out_shape=(face,...]
    reduce_sum x1 -> x0, other arithmetic: 2 us -> none  [local(): jnp.sum(occupations[:, None, None, None, None] * waves * waves, 0)]
    unnamed x21 -> x17, local copies, waits for them, and re-layouts: 5.51 us -> 4.17 us
where the time goes in v13:
time: 134 us; the launch traced here: 133 us
  Pallas kernels  120 us (90%)
  local copies, waits for them, and re-layouts  6.68 us (5%)
  other arithmetic  5.46 us (4%)
  between operations  1.5 us (1%)
    pallas_call x1, Pallas kernels, symmetric_density(): pl.pallas_call(_density_kernel, out_shape=(jax.ShapeDtypeStruct(part.shap...  58 us
    pallas_call x1, Pallas kernels, mix(): pl.pallas_call(functools.partial(_mix_kernel, n), out_shape=(field, field...  56.2 us
    pallas_call x1, Pallas kernels, swap_faces(): pl.pallas_call(functools.partial(_swap_kernel, stride), out_shape=(face,...  5.49 us
    unnamed x17, local copies, waits for them, and re-layouts  4.17 us

profile of v13, /device:TPU:1, one launch (start us, length us, event | category | flops | bytes accessed | tf_op | source)
XLA Modules:
  0.0 133.3 jit_solution(3037619158977904596)
XLA Ops:
  0.6 58.0 %shard_map.77 = (f32[16,32,128]{2,1,0:T(8,128)}, f32[8,128]{1,0:T(8,128)}, f32[16,128]{1,0:T(8,128)}) custom-call(f32[4]{0:T(128)} %occ_ref.1, bf16[4,16,32,128]{3,2,1,0:T(8,128)(2,1)} %bitcast.19, f32[16,32,128]{2,1,0:T(8,128)} %bitcast.17, bf16[8,16,32,128]{3,2,1,0:T(8,128)(2,1)} %bitcast.14), custom_call_target="tpu_custom_call" | custom-call | tf_op jit(solution)/shard_map/pallas_call | solution.py:531
  58.7 56.2 %shard_map.78 = (f32[16,32,128]{2,1,0:T(8,128)}, f32[16,32,128]{2,1,0:T(8,128)}, f32[16,32,128]{2,1,0:T(8,128)}, f32[3,32,128]{2,1,0:T(8,128)}, f32[3,32,128]{2,...) custom-call(bf16[8,16,32,128]{3,2,1,0:T(8,128)(2,1)} %bitcast.15, bf16[8,16,32,128]{3,2,1,0:T(8,128)(2,1)} %bitcast.16, ...), custom_call_target="tpu_custom_call" | custom-call | tf_op jit(solution)/shard_map/pallas_call | solution.py:217
  114.8 0.0 copy-start.6
  114.8 0.0 copy-start.4
  114.8 0.9 slice.87
  115.8 0.0 copy-start.3
  115.8 0.0 copy-done.6
  115.8 0.0 copy-done.4
  115.8 0.8 copy-done.3
  116.6 1.0 pad_maximum_fusion.1
  117.6 0.2 fusion.21
  117.8 0.9 copy.20
  118.7 0.9 copy.21
  119.5 5.5 %shard_map.79 = (f32[3,22,38]{2,1,0:T(8,128)}, f32[3,22,38]{2,1,0:T(8,128)}) custom-call(f32[3,22,38]{2,1,0:T(8,128)} %bitcast.21, f32[3,22,38]{2,1,0:T(8,128)} %bitcast.22), custom_call_target="tpu_custom_call" | custom-call | tf_op jit(solution)/shard_map/pallas_call | solution.py:614
  125.0 0.0 copy-start.5
  125.0 1.0 copy.18
  126.1 0.0 copy-done.5
  126.1 0.3 copy.19
  127.1 0.0 copy-start
  127.1 0.1 broadcast_in_dim.4
  127.2 0.9 copy-done
  128.1 1.0 fusion.7
  129.1 0.6 divide_select_fusion.1
  129.7 0.7 divide_select_fusion
  130.4 0.0 copy-start.2
  130.4 0.7 slice_add_fusion
  131.1 0.2 and_and_fusion
  131.3 0.1 copy-done.2
  131.3 0.0 copy-start.1
  131.3 1.3 fusion.20
  132.6 0.0 copy-done.1
  132.6 0.7 copy.24
  (4 shorter events, 0.0 us)
Async XLA Ops:
  114.8 1.0 copy-start.6
  114.8 1.0 copy-start.4
  115.8 0.8 copy-start.3
  125.0 1.1 copy-start.5
  127.1 1.0 copy-start
  130.4 1.0 copy-start.2
  131.3 1.3 copy-start.1

commit v14 on v12

--- a/solution.py
+++ b/solution.py
@@ -51,7 +51,7 @@
 
 def _mix_kernel(n, hres_ref, hin_ref, rho_ref, din_ref, ch_ref, hg_ref, res_ref, ropt_ref, sopt_ref,
                 xlo_ref, xhi_ref, ylo_ref, yhi_ref,
-                mine, buf_a, sum_a, buf_b, xlo_s, xhi_s, xext, ylo_s, yhi_s, sa, ra, sb, rb, hx, hy):
+                mine, buf_a, sum_a, buf_b, xlo_s, xhi_s, xext, ylo_s, yhi_s, sa, ra, sb, rb, hx, hy, entry=True):
     depth = hres_ref.shape[0]
     me = lax.axis_index("grid")
     band = lax.axis_index("band")
@@ -59,15 +59,16 @@
     nb = n // na
     row = me // na
     j = me % na
-    barrier = pltpu.get_barrier_semaphore()
-
-    def greet_a(k, c):
-        pl.semaphore_signal(barrier, inc=1, device_id=(row * na + lax.rem(j + k, na), band), device_id_type=MESH)
-        return c
-
-    lax.fori_loop(1, na, greet_a, 0)
-    for k in range(1, nb):
-        pl.semaphore_signal(barrier, inc=1, device_id=(lax.rem(row + k, nb) * na + j, band), device_id_type=MESH)
+    if entry:
+        barrier = pltpu.get_barrier_semaphore()
+
+        def greet_a(k, c):
+            pl.semaphore_signal(barrier, inc=1, device_id=(row * na + lax.rem(j + k, na), band), device_id_type=MESH)
+            return c
+
+        lax.fori_loop(1, na, greet_a, 0)
+        for k in range(1, nb):
+            pl.semaphore_signal(barrier, inc=1, device_id=(lax.rem(row + k, nb) * na + j, band), device_id_type=MESH)
 
     first = lax.broadcasted_iota(jnp.int32, ch_ref.shape, 0) == 0
     lane = lax.broadcasted_iota(jnp.int32, ch_ref.shape, 1)
@@ -83,7 +84,8 @@
         gram = gram + jnp.where(((t_row == i) & (t_col == depth)) | ((t_row == depth) & (t_col == i)), dot, 0.0)
     gram = gram + jnp.where((t_row == depth) & (t_col == depth), jnp.sum(residual * residual), 0.0)
     mine[...] = gram
-    pl.semaphore_wait(barrier, na - 1 + nb - 1)
+    if entry:
+        pl.semaphore_wait(barrier, na - 1 + nb - 1)
 
     def copy_a(src_slot, peer_j):
         return pltpu.make_async_remote_copy(
@@ -187,6 +189,51 @@
     by = j // 4
     exchange(xext.at[:, pl.ds(0, wy)], xext.at[:, pl.ds(cy - wy, wy)], ylo_s, yhi_s, hy,
              by > 0, by < 3, (me - 4, band), (me + 4, band), ylo_ref, yhi_ref)
+
+
+def _mix_scratch(n, shape, hist_shape, depth):
+    na = 16
+    dma = pltpu.SemaphoreType.DMA
+    cx, cy, cz = shape
+    h, wy = SWEEPS - 1, 8
+    xface = (h, cy, cz)
+    yface = (cx + 2 * h, wy, cz)
+    outs = tuple(jax.ShapeDtypeStruct(s, jnp.float32) for s in (shape, shape, shape, xface, xface, yface, yface))
+    scratch = [
+        pltpu.VMEM(hist_shape, jnp.float32),
+        pltpu.VMEM((na,) + hist_shape, jnp.float32),
+        pltpu.VMEM(hist_shape, jnp.float32),
+        pltpu.VMEM((n // na,) + hist_shape, jnp.float32),
+        pltpu.VMEM(xface, jnp.float32),
+        pltpu.VMEM(xface, jnp.float32),
+        pltpu.VMEM((cx + 2 * h, cy, cz), jnp.float32),
+        pltpu.VMEM(yface, jnp.float32),
+        pltpu.VMEM(yface, jnp.float32),
+        dma((na,)), dma((na,)), dma((n // na,)), dma((n // na,)), dma((4,)), dma((4,)),
+    ]
+    return outs, scratch
+
+
+def _step_kernel(n, n_dens, occ_ref, w_ref, d_ref, h_ref, hin_ref, o_ref, c_ref, hg_ref,
+                 res_ref, ropt_ref, sopt_ref, xlo_ref, xhi_ref, ylo_ref, yhi_ref, *scratch):
+    _density_kernel(occ_ref, w_ref, d_ref, h_ref, o_ref, c_ref, hg_ref, *scratch[:n_dens])
+    _mix_kernel(n, h_ref, hin_ref, o_ref, d_ref, c_ref, hg_ref, res_ref, ropt_ref, sopt_ref,
+                xlo_ref, xhi_ref, ylo_ref, yhi_ref, *scratch[n_dens:], entry=False)
+
+
+def density_step(occ, waves, din, hres, hin):
+    n = lax.axis_size("grid")
+    dens_outs, dens_scratch = _density_scratch(din)
+    mix_outs, mix_scratch = _mix_scratch(n, din.shape, (16, 128), hres.shape[0])
+    outs = pl.pallas_call(
+        functools.partial(_step_kernel, n, len(dens_scratch)),
+        out_shape=dens_outs + mix_outs,
+        in_specs=[pl.BlockSpec(memory_space=pltpu.SMEM)] + [pl.BlockSpec(memory_space=pltpu.VMEM)] * 4,
+        out_specs=(pl.BlockSpec(memory_space=pltpu.VMEM),) * (len(dens_outs) + len(mix_outs)),
+        scratch_shapes=dens_scratch + mix_scratch,
+        compiler_params=pltpu.CompilerParams(collective_id=3, has_side_effects=True),
+    )(occ, waves, din, hres, hin)
+    return outs[len(dens_outs):]
 
 
 def mix(hres, hin, rho, din, charges, hist):
@@ -506,6 +553,30 @@
     c_ref[...] = ((tx_in[0] + tx_in[1]) + tx_in[2]) + tx_in[3]
 
 
+def _density_scratch(din):
+    part = din
+    rest = part.shape[1:]
+    dma = pltpu.SemaphoreType.DMA
+    vm = lambda *s: pltpu.VMEM(s + rest, jnp.float32)
+    tile = lambda *s: pltpu.VMEM(s + (8, 128), jnp.float32)
+    n = lax.axis_size("grid")
+    na = 16
+    outs = (
+        jax.ShapeDtypeStruct(part.shape, jnp.float32),
+        jax.ShapeDtypeStruct((8, 128), jnp.float32),
+        jax.ShapeDtypeStruct((16, 128), jnp.float32),
+    )
+    scratch = [
+        vm(part.shape[0]),
+        vm(4, 4), vm(4), vm(2, 2), vm(2), vm(2), vm(2), vm(2), vm(2), vm(2), vm(2), vm(4), vm(part.shape[0]),
+        tile(na), tile(), tile(n // na), tile(), tile(2), tile(), tile(4),
+        dma((4, 2)), dma((4, 2)), dma((2,)), dma((2, 2)), dma(()), dma(()), dma(()), dma(()), dma(()), dma(()),
+        dma((2,)), dma((2,)), dma((4, 2)), dma((4, 2)),
+        dma((na,)), dma((na,)), dma((n // na,)), dma((n // na,)), dma(()), dma((2,)), dma((4,)), dma((4,)),
+    ]
+    return outs, scratch
+
+
 def symmetric_density(occ, waves, din, hist):
     part = din
     rest = part.shape[1:]
@@ -639,9 +710,8 @@
 
 
 def local(orbitals, occupations, density_in, history_in, history_res, screening):
-    rho_block, charges, hist = symmetric_density(occupations, orbitals[:, 0], density_in[0], history_res[:, 0])
-    residual, rho_opt, res_opt, x_lo, x_hi, y_lo, y_hi = mix(
-        history_res[:, 0], history_in[:, 0], rho_block, density_in[0], charges, hist
+    residual, rho_opt, res_opt, x_lo, x_hi, y_lo, y_hi = density_step(
+        occupations, orbitals[:, 0], density_in[0], history_res[:, 0], history_in[:, 0]
     )
     residual = residual[None]
     rho_opt = rho_opt[None]

time: 105 us -> 99.7 us (0.950)
  Pallas kernels: 91.2 us -> 85.5 us
    pallas_call x2 -> x1, Pallas kernels: 84.7 us -> 79 us  [density_step(): pl.pallas_call(functools.partial(_step_kernel, n, len(dens_scratch)), out...]
where the time goes in v14:
time: 99.7 us; the launch traced here: 99.2 us
  Pallas kernels  85.5 us (86%)
  local copies, waits for them, and re-layouts  6.68 us (7%)
  other arithmetic  5.46 us (5%)
  between operations  1.51 us (2%)
    pallas_call x1, Pallas kernels, density_step(): pl.pallas_call(functools.partial(_step_kernel, n, len(dens_scratch)), out...  79 us
    pallas_call x1, Pallas kernels, swap_faces(): pl.pallas_call(functools.partial(_swap_kernel, stride), out_shape=(face,...  6.53 us
    unnamed x17, local copies, waits for them, and re-layouts  4.17 us
    mul x3, other arithmetic, local(): field_u = (ext + beside) / (6.0 + kappa) * mask  2.32 us

profile of v14, /device:TPU:1, one launch (start us, length us, event | category | flops | bytes accessed | tf_op | source)
XLA Modules:
  0.0 99.2 jit_solution(1036261382499403831)
XLA Ops:
  0.7 79.0 %shard_map.77 = (f32[16,32,128]{2,1,0:T(8,128)}, f32[8,128]{1,0:T(8,128)}, f32[16,128]{1,0:T(8,128)}, f32[16,32,128]{2,1,0:T(8,128)}, f32[16,32,128]{2,1,0:T(8,1...) custom-call(f32[4]{0:T(128)} %occ_ref.1, ...), custom_call_target="tpu_custom_call" | custom-call | tf_op jit(solution)/shard_map/pallas_call | solution.py:228
  79.7 0.0 copy-start.6
  79.8 0.0 copy-start.4
  79.8 0.9 slice.87
  80.7 0.0 copy-start.3
  80.7 0.0 copy-done.6
  80.7 0.0 copy-done.4
  80.7 0.8 copy-done.3
  81.5 1.0 %pad_maximum_fusion.1 = f32[22,38,128]{2,1,0:T(8,128)S(1)} fusion(f32[22,3,128]{2,1,0:T(4,128)S(1)} %slice.88, f32[3,32,128]{2,1,0:T(8,128)S(1)} %copy-done.4, f32[16,32,128]{2,1,0:T(8,128)} %get-tuple-element.12, f32[3,32,128]{2,1,0:T(8,128)S(1)} %copy-done.3, f32[22,3,128]{2,1,0:T(4,128)S(1)} %slice.87), kind=kLoop, calls=%fused_computation.37 | loop fusion | flops 428032 | bytes 856064 | tf_op jit(solution)/shard_map/concatenate | solution.py:728
  82.5 0.2 fusion.21
  82.7 0.9 copy.20
  83.6 0.9 copy.21
  84.4 6.5 %shard_map.78 = (f32[3,22,38]{2,1,0:T(8,128)}, f32[3,22,38]{2,1,0:T(8,128)}) custom-call(f32[3,22,38]{2,1,0:T(8,128)} %bitcast.19, f32[3,22,38]{2,1,0:T(8,128)} %bitcast.20), custom_call_target="tpu_custom_call" | custom-call | tf_op jit(solution)/shard_map/pallas_call | solution.py:671
  91.0 0.0 copy-start.5
  91.0 1.0 %copy.18 = f32[22,38,3]{2,1,0:T(8,128)S(1)} copy(f32[22,38,3]{1,0,2:T(8,128)} %bitcast.22) | data formatting | bytes 20064 | tf_op jit(solution)/shard_map/transpose | solution.py:730
  92.0 0.0 copy-done.5
  92.0 0.3 copy.19
  93.0 0.0 copy-start
  93.0 0.1 broadcast_in_dim.4
  93.1 0.9 copy-done
  93.9 1.0 %fusion.7 = (f32[22,38,134]{2,1,0:T(8,128)S(1)}, f32[22,38,134]{2,1,0:T(8,128)S(1)}) fusion(f32[22,38,134]{2,1,0:T(8,128)S(1)} %broadcast_in_dim.4, f32[]{:T(128)S(6)} %add.142, pred[134]{0:T(512)(128)(4,1)S(1)} %compare_and_fusion, pred[38]{0:T(512)(128)(4,1)S(1)} %compare_and_fusion.1, pred[22]{0:T(512)(128)(4,1)S(1)} %compare_and_fusion.2, ...), kind=kLoop, calls=%fused_computation.13 | loop fusion | flops 1792384 | bytes 1792582 | tf_op jit(solution)/shard_map/mul | solution.py:745
  95.0 0.6 divide_select_fusion.1
  95.6 0.7 divide_select_fusion
  96.3 0.0 copy-start.2
  96.3 0.7 slice_add_fusion
  97.0 0.2 and_and_fusion
  97.2 0.1 copy-done.2
  97.2 0.0 copy-start.1
  97.2 1.3 %fusion.20 = f32[1,16,32,128]{3,2,1,0:T(8,128)} fusion(f32[16,32,128]{2,1,0:T(8,128)S(1)} %copy-done.2, f32[16,32,128]{2,1,0:T(8,128)S(1)} %copy-done, f32[22,38,134]{2,1,0:T(8,128)S(1)} %get-tuple-element.27, f32[22,38,134]{2,1,0:T(8,128)S(1)} %get-tuple-element.26, f32[22,38,134]{2,1,0:T(8,128)S(1)} %get-tuple-element.25, ...), kind=kLoop, calls=%fused_computation.48 | loop fusion | flops 655360 | bytes 2162696 | tf_op jit(solution)/shard_map/add | solution.py:747
  98.5 0.0 copy-done.1
  98.5 0.7 copy.24
  (4 shorter events, 0.0 us)
Async XLA Ops:
  79.7 1.0 copy-start.6
  79.8 1.0 copy-start.4
  80.7 0.8 copy-start.3
  91.0 1.1 %copy-start.5 = (f32[3,22,38]{2,1,0:T(8,128)S(1)}, f32[3,22,38]{2,1,0:T(8,128)}, u32[]{:S(2)}) copy-start(f32[3,22,38]{2,1,0:T(8,128)} %get-tuple-element.18) | copy-start | bytes 30100
  93.0 1.0 copy-start
  96.3 1.0 copy-start.2
  97.2 1.3 %copy-start.1 = (f32[16,32,128]{2,1,0:T(8,128)S(1)}, f32[16,32,128]{2,1,0:T(8,128)}, u32[]{:S(2)}) copy-start(f32[16,32,128]{2,1,0:T(8,128)} %get-tuple-element.19) | copy-start | bytes 786436

commit v15 on v14

--- a/solution.py
+++ b/solution.py
@@ -51,7 +51,8 @@
 
 def _mix_kernel(n, hres_ref, hin_ref, rho_ref, din_ref, ch_ref, hg_ref, res_ref, ropt_ref, sopt_ref,
                 xlo_ref, xhi_ref, ylo_ref, yhi_ref,
-                mine, buf_a, sum_a, buf_b, xlo_s, xhi_s, xext, ylo_s, yhi_s, sa, ra, sb, rb, hx, hy, entry=True):
+                mine, buf_a, sum_a, buf_b, xlo_s, xhi_s, xext, ylo_s, yhi_s, sa, ra, sb, rb, hx, hy, entry=True,
+                z_refs=None):
     depth = hres_ref.shape[0]
     me = lax.axis_index("grid")
     band = lax.axis_index("band")
@@ -189,6 +190,32 @@
     by = j // 4
     exchange(xext.at[:, pl.ds(0, wy)], xext.at[:, pl.ds(cy - wy, wy)], ylo_s, yhi_s, hy,
              by > 0, by < 3, (me - 4, band), (me + 4, band), ylo_ref, yhi_ref)
+    if z_refs is None:
+        return
+    zlo_ref, zhi_ref, zs_lo, zs_hi, zr_lo, zr_hi, hz = z_refs
+    cz = sopt_ref.shape[2]
+    s_row = lax.broadcasted_iota(jnp.int32, (8, cz), 0)
+    s_lane = lax.broadcasted_iota(jnp.int32, (8, cz), 1)
+    sel_lo = jnp.where((s_row < h) & (s_lane == s_row), 1.0, 0.0)
+    sel_hi = jnp.where((s_row < h) & (s_lane == cz - h + s_row), 1.0, 0.0)
+    pieces = (
+        (xext[...].reshape(-1, cz), 0),
+        (ylo_ref[...].reshape(-1, cz), 768),
+        (yhi_ref[...].reshape(-1, cz), 1024),
+    )
+    zs_lo[...] = jnp.zeros(zs_lo.shape, jnp.float32)
+    zs_hi[...] = jnp.zeros(zs_hi.shape, jnp.float32)
+    for piece, at in pieces:
+        width = piece.shape[0]
+        dims = (((1,), (1,)), ((), ()))
+        zs_lo[:, pl.ds(at, width)] = lax.dot_general(
+            sel_lo, piece, dims, precision=lax.Precision.HIGHEST, preferred_element_type=jnp.float32
+        )
+        zs_hi[:, pl.ds(at, width)] = lax.dot_general(
+            sel_hi, piece, dims, precision=lax.Precision.HIGHEST, preferred_element_type=jnp.float32
+        )
+    bzz = me % 4
+    exchange(zs_lo, zs_hi, zr_lo, zr_hi, hz, bzz > 0, bzz < 3, (me - 1, band), (me + 1, band), zlo_ref, zhi_ref)
 
 
 def _mix_scratch(n, shape, hist_shape, depth):
@@ -215,16 +242,21 @@
 
 
 def _step_kernel(n, n_dens, occ_ref, w_ref, d_ref, h_ref, hin_ref, o_ref, c_ref, hg_ref,
-                 res_ref, ropt_ref, sopt_ref, xlo_ref, xhi_ref, ylo_ref, yhi_ref, *scratch):
+                 res_ref, ropt_ref, sopt_ref, xlo_ref, xhi_ref, ylo_ref, yhi_ref, zlo_ref, zhi_ref, *scratch):
     _density_kernel(occ_ref, w_ref, d_ref, h_ref, o_ref, c_ref, hg_ref, *scratch[:n_dens])
+    mix_scratch = scratch[n_dens:-5]
     _mix_kernel(n, h_ref, hin_ref, o_ref, d_ref, c_ref, hg_ref, res_ref, ropt_ref, sopt_ref,
-                xlo_ref, xhi_ref, ylo_ref, yhi_ref, *scratch[n_dens:], entry=False)
+                xlo_ref, xhi_ref, ylo_ref, yhi_ref, *mix_scratch, entry=False,
+                z_refs=(zlo_ref, zhi_ref) + tuple(scratch[-5:]))
 
 
 def density_step(occ, waves, din, hres, hin):
     n = lax.axis_size("grid")
     dens_outs, dens_scratch = _density_scratch(din)
     mix_outs, mix_scratch = _mix_scratch(n, din.shape, (16, 128), hres.shape[0])
+    zface = jax.ShapeDtypeStruct((8, 1280), jnp.float32)
+    mix_outs = mix_outs + (zface, zface)
+    mix_scratch = mix_scratch + [pltpu.VMEM((8, 1280), jnp.float32)] * 4 + [pltpu.SemaphoreType.DMA((4,))]
     outs = pl.pallas_call(
         functools.partial(_step_kernel, n, len(dens_scratch)),
         out_shape=dens_outs + mix_outs,
@@ -710,7 +742,7 @@
 
 
 def local(orbitals, occupations, density_in, history_in, history_res, screening):
-    residual, rho_opt, res_opt, x_lo, x_hi, y_lo, y_hi = density_step(
+    residual, rho_opt, res_opt, x_lo, x_hi, y_lo, y_hi, z_lo, z_hi = density_step(
         occupations, orbitals[:, 0], density_in[0], history_res[:, 0], history_in[:, 0]
     )
     residual = residual[None]
@@ -726,8 +758,15 @@
     cx, cy, cz = source.shape
     ext = jnp.concatenate([x_lo, source, x_hi], 0)
     ext = jnp.concatenate([y_lo[:, -h:], ext, y_hi[:, :h]], 1)
-    lo, hi = swap_faces(jnp.transpose(ext[:, :, :h], (2, 0, 1)), jnp.transpose(ext[:, :, -h:], (2, 0, 1)), 1, 6)
-    ext = jnp.concatenate([jnp.transpose(lo, (1, 2, 0)), ext, jnp.transpose(hi, (1, 2, 0))], 2)
+
+    def z_face(t):
+        ex = ext.shape[0]
+        core = t[:h, : ex * cy].reshape(h, ex, cy)
+        y_low = t[:h, 768 : 768 + ex * 8].reshape(h, ex, 8)[:, :, 8 - h :]
+        y_high = t[:h, 1024 : 1024 + ex * 8].reshape(h, ex, 8)[:, :, :h]
+        return jnp.transpose(jnp.concatenate([y_low, core, y_high], 2), (1, 2, 0))
+
+    ext = jnp.concatenate([z_face(z_lo), ext, z_face(z_hi)], 2)
 
     def inside(block, size, n_blocks, axis):
         pos = block * size + lax.broadcasted_iota(jnp.int32, ext.shape, axis) - h

time: 99.7 us -> 97.5 us (0.978)
    pallas_call x1 -> x0, Pallas kernels: 6.53 us -> none  [swap_faces(): pl.pallas_call(functools.partial(_swap_kernel, stride), out_shape=(face,...]
    pallas_call x1, Pallas kernels: 79 us -> 84.9 us  [density_step(): pl.pallas_call(functools.partial(_step_kernel, n, len(dens_scratch)), out...]
    slice x1 -> x5, local copies, waits for them, and re-layouts: 0.19 us -> 2.38 us  [the longest x2 1.48 us: z_face(): core = t[:h, :ex * cy].reshape(h, ex, cy)]
    unnamed x17 -> x15, local copies, waits for them, and re-layouts: 4.17 us -> 2.53 us
    transpose x2 -> x0, local copies, waits for them, and re-layouts: 1.33 us -> none  [the longest x1 1.05 us: local(): jnp.transpose(lo, (1, 2, 0))]
where the time goes in v15:
time: 97.5 us; the launch traced here: 97.1 us
  Pallas kernels  84.9 us (87%)
  local copies, waits for them, and re-layouts  6.07 us (6%)
  other arithmetic  4.63 us (5%)
  between operations  1.51 us (2%)
    pallas_call x1, Pallas kernels, density_step(): pl.pallas_call(functools.partial(_step_kernel, n, len(dens_scratch)), out...  84.9 us
    unnamed x15, local copies, waits for them, and re-layouts  2.53 us
    mul x3, other arithmetic, local(): field_u = (ext + beside) / (6.0 + kappa) * mask  2.31 us

profile of v15, /device:TPU:1, one launch (start us, length us, event | category | flops | bytes accessed | tf_op | source)
XLA Modules:
  0.0 97.1 jit_solution(10252694110696585467)
XLA Ops:
  0.7 84.9 %shard_map.77 = (f32[16,32,128]{2,1,0:T(8,128)}, f32[8,128]{1,0:T(8,128)}, f32[16,128]{1,0:T(8,128)}, f32[16,32,128]{2,1,0:T(8,128)}, f32[16,32,128]{2,1,0:T(8,1...) custom-call(f32[4]{0:T(128)} %occ_ref.1, ...), custom_call_target="tpu_custom_call" | custom-call | tf_op jit(solution)/shard_map/pallas_call | solution.py:260
  85.6 0.8 fusion.21
  86.4 0.1 reshape.26
  86.5 0.1 slice.148
  86.6 0.1 reshape.28
  86.7 0.7 slice.113
  87.4 0.1 reshape.27
  87.5 0.1 pad_maximum_fusion.1
  87.6 0.3 copy.20
  87.9 0.1 reshape.29
  88.0 0.1 slice.150
  88.0 0.1 reshape.31
  88.1 0.7 slice.120
  88.9 0.1 reshape.30
  89.0 0.1 pad_maximum_fusion.2
  89.1 0.0 copy-start.6
  89.1 0.3 copy.21
  89.4 0.6 copy-done.6
  90.0 0.3 copy-done.5
  90.9 0.0 copy-start
  90.9 0.0 copy-start.3
  90.9 0.1 broadcast_in_dim.4
  91.0 0.9 copy-done
  91.9 0.0 copy-done.4
  91.9 1.0 %fusion.7 = (f32[22,38,134]{2,1,0:T(8,128)S(1)}, f32[22,38,134]{2,1,0:T(8,128)S(1)}) fusion(f32[22,38,134]{2,1,0:T(8,128)S(1)} %broadcast_in_dim.4, f32[]{:T(128)S(6)} %add.142, pred[134]{0:T(512)(128)(4,1)S(1)} %compare_and_fusion, pred[38]{0:T(512)(128)(4,1)S(1)} %compare_and_fusion.1, pred[22]{0:T(512)(128)(4,1)S(1)} %compare_and_fusion.2, ...), kind=kLoop, calls=%fused_computation.13 | loop fusion | flops 1792384 | bytes 1792582 | tf_op jit(solution)/shard_map/mul | solution.py:784
  92.9 0.6 divide_select_fusion.1
  93.5 0.7 divide_select_fusion
  94.2 0.7 slice_add_fusion
  94.9 0.2 and_and_fusion
  95.1 0.1 copy-done.2
  95.2 1.2 %fusion.20 = f32[1,16,32,128]{3,2,1,0:T(8,128)} fusion(f32[16,32,128]{2,1,0:T(8,128)S(1)} %copy-done.2, f32[16,32,128]{2,1,0:T(8,128)S(1)} %copy-done, f32[22,38,134]{2,1,0:T(8,128)S(1)} %get-tuple-element.25, f32[22,38,134]{2,1,0:T(8,128)S(1)} %get-tuple-element.24, f32[22,38,134]{2,1,0:T(8,128)S(1)} %get-tuple-element.23, ...), kind=kLoop, calls=%fused_computation.47 | loop fusion | flops 655360 | bytes 2162696 | tf_op jit(solution)/shard_map/add | solution.py:786
  96.4 0.7 copy.24
  (11 shorter events, 0.1 us)
Async XLA Ops:
  89.1 0.9 copy-start.6
  89.3 0.9 copy-start.5
  90.9 1.0 copy-start
  90.9 0.9 copy-start.3
  90.9 0.9 copy-start.4
  94.2 1.0 copy-start.2
  95.2 1.3 %copy-start.1 = (f32[16,32,128]{2,1,0:T(8,128)S(1)}, f32[16,32,128]{2,1,0:T(8,128)}, u32[]{:S(2)}) copy-start(f32[16,32,128]{2,1,0:T(8,128)} %get-tuple-element.19) | copy-start | bytes 786436

commit v16 on v15

--- a/solution.py
+++ b/solution.py
@@ -192,7 +192,7 @@
              by > 0, by < 3, (me - 4, band), (me + 4, band), ylo_ref, yhi_ref)
     if z_refs is None:
         return
-    zlo_ref, zhi_ref, zs_lo, zs_hi, zr_lo, zr_hi, hz = z_refs
+    zlo_refs, zhi_refs, zs_lo, zs_hi, zr_lo, zr_hi, zo_lo, zo_hi, hz = z_refs
     cz = sopt_ref.shape[2]
     s_row = lax.broadcasted_iota(jnp.int32, (8, cz), 0)
     s_lane = lax.broadcasted_iota(jnp.int32, (8, cz), 1)
@@ -215,7 +215,10 @@
             sel_hi, piece, dims, precision=lax.Precision.HIGHEST, preferred_element_type=jnp.float32
         )
     bzz = me % 4
-    exchange(zs_lo, zs_hi, zr_lo, zr_hi, hz, bzz > 0, bzz < 3, (me - 1, band), (me + 1, band), zlo_ref, zhi_ref)
+    exchange(zs_lo, zs_hi, zr_lo, zr_hi, hz, bzz > 0, bzz < 3, (me - 1, band), (me + 1, band), zo_lo, zo_hi)
+    for got, outs in ((zo_lo, zlo_refs), (zo_hi, zhi_refs)):
+        for (piece, at), out in zip(pieces, outs):
+            out[...] = got[pl.ds(0, h), pl.ds(at, piece.shape[0])]
 
 
 def _mix_scratch(n, shape, hist_shape, depth):
@@ -242,21 +245,25 @@
 
 
 def _step_kernel(n, n_dens, occ_ref, w_ref, d_ref, h_ref, hin_ref, o_ref, c_ref, hg_ref,
-                 res_ref, ropt_ref, sopt_ref, xlo_ref, xhi_ref, ylo_ref, yhi_ref, zlo_ref, zhi_ref, *scratch):
+                 res_ref, ropt_ref, sopt_ref, xlo_ref, xhi_ref, ylo_ref, yhi_ref, *rest):
+    z_outs = rest[:6]
+    scratch = rest[6:]
     _density_kernel(occ_ref, w_ref, d_ref, h_ref, o_ref, c_ref, hg_ref, *scratch[:n_dens])
-    mix_scratch = scratch[n_dens:-5]
+    mix_scratch = scratch[n_dens:-7]
     _mix_kernel(n, h_ref, hin_ref, o_ref, d_ref, c_ref, hg_ref, res_ref, ropt_ref, sopt_ref,
                 xlo_ref, xhi_ref, ylo_ref, yhi_ref, *mix_scratch, entry=False,
-                z_refs=(zlo_ref, zhi_ref) + tuple(scratch[-5:]))
+                z_refs=(z_outs[:3], z_outs[3:]) + tuple(scratch[-7:]))
 
 
 def density_step(occ, waves, din, hres, hin):
     n = lax.axis_size("grid")
     dens_outs, dens_scratch = _density_scratch(din)
     mix_outs, mix_scratch = _mix_scratch(n, din.shape, (16, 128), hres.shape[0])
-    zface = jax.ShapeDtypeStruct((8, 1280), jnp.float32)
-    mix_outs = mix_outs + (zface, zface)
-    mix_scratch = mix_scratch + [pltpu.VMEM((8, 1280), jnp.float32)] * 4 + [pltpu.SemaphoreType.DMA((4,))]
+    h = SWEEPS - 1
+    ex = din.shape[0] + 2 * h
+    zface = tuple(jax.ShapeDtypeStruct((h, w), jnp.float32) for w in (ex * din.shape[1], ex * 8, ex * 8))
+    mix_outs = mix_outs + zface + zface
+    mix_scratch = mix_scratch + [pltpu.VMEM((8, 1280), jnp.float32)] * 6 + [pltpu.SemaphoreType.DMA((4,))]
     outs = pl.pallas_call(
         functools.partial(_step_kernel, n, len(dens_scratch)),
         out_shape=dens_outs + mix_outs,
@@ -742,7 +749,7 @@
 
 
 def local(orbitals, occupations, density_in, history_in, history_res, screening):
-    residual, rho_opt, res_opt, x_lo, x_hi, y_lo, y_hi, z_lo, z_hi = density_step(
+    residual, rho_opt, res_opt, x_lo, x_hi, y_lo, y_hi, *z_parts = density_step(
         occupations, orbitals[:, 0], density_in[0], history_res[:, 0], history_in[:, 0]
     )
     residual = residual[None]
@@ -759,14 +766,14 @@
     ext = jnp.concatenate([x_lo, source, x_hi], 0)
     ext = jnp.concatenate([y_lo[:, -h:], ext, y_hi[:, :h]], 1)
 
-    def z_face(t):
+    def z_face(core, low, high):
         ex = ext.shape[0]
-        core = t[:h, : ex * cy].reshape(h, ex, cy)
-        y_low = t[:h, 768 : 768 + ex * 8].reshape(h, ex, 8)[:, :, 8 - h :]
-        y_high = t[:h, 1024 : 1024 + ex * 8].reshape(h, ex, 8)[:, :, :h]
+        core = core.reshape(h, ex, cy)
+        y_low = low.reshape(h, ex, 8)[:, :, 8 - h :]
+        y_high = high.reshape(h, ex, 8)[:, :, :h]
         return jnp.transpose(jnp.concatenate([y_low, core, y_high], 2), (1, 2, 0))
 
-    ext = jnp.concatenate([z_face(z_lo), ext, z_face(z_hi)], 2)
+    ext = jnp.concatenate([z_face(*z_parts[:3]), ext, z_face(*z_parts[3:])], 2)
 
     def inside(block, size, n_blocks, axis):
         pos = block * size + lax.broadcasted_iota(jnp.int32, ext.shape, axis) - h

time: 97.5 us -> 98.9 us (1.014)
  local copies, waits for them, and re-layouts: 6.07 us -> 7.32 us
    unnamed x15 -> x25, local copies, waits for them, and re-layouts: 2.53 us -> 5.35 us
    slice x5 -> x2, local copies, waits for them, and re-layouts: 2.38 us -> 0.15 us  [z_face(): y_low = low.reshape(h, ex, 8)[:, :, 8 - h:]]
where the time goes in v16:
time: 98.9 us; the launch traced here: 98.4 us
  Pallas kernels  84.9 us (86%)
  local copies, waits for them, and re-layouts  7.32 us (7%)
  other arithmetic  4.63 us (5%)
  between operations  1.53 us (2%)
    pallas_call x1, Pallas kernels, density_step(): pl.pallas_call(functools.partial(_step_kernel, n, len(dens_scratch)), out...  84.9 us
    unnamed x25, local copies, waits for them, and re-layouts  5.35 us
    mul x3, other arithmetic, local(): field_u = (ext + beside) / (6.0 + kappa) * mask  2.31 us

profile of v16, /device:TPU:1, one launch (start us, length us, event | category | flops | bytes accessed | tf_op | source)
XLA Modules:
  0.0 98.4 jit_solution(986080967706797952)
XLA Ops:
  0.7 84.9 %shard_map.77 = (f32[16,32,128]{2,1,0:T(8,128)}, f32[8,128]{1,0:T(8,128)}, f32[16,128]{1,0:T(8,128)}, f32[16,32,128]{2,1,0:T(8,128)}, f32[16,32,128]{2,1,0:T(8,1...) custom-call(f32[4]{0:T(128)} %occ_ref.1, ...), custom_call_target="tpu_custom_call" | custom-call | tf_op jit(solution)/shard_map/pallas_call | solution.py:267
  85.7 0.8 reshape.26
  86.4 0.0 copy-start.11
  86.4 0.1 slice.124
  86.5 0.6 copy-done.11
  87.1 0.1 reshape.28
  87.2 0.6 copy-done.8
  87.8 0.1 reshape.27
  87.9 0.1 pad_maximum_fusion.1
  88.0 0.0 copy-start.10
  88.0 0.3 copy.20
  88.3 0.4 copy-done.10
  88.7 0.1 reshape.29
  88.8 0.1 slice.126
  88.9 0.6 copy-done.9
  89.5 0.1 reshape.31
  89.6 0.6 copy-done.7
  90.2 0.1 reshape.30
  90.3 0.1 pad_maximum_fusion.2
  90.4 0.3 copy.21
  90.6 0.6 copy-done.6
  91.3 0.3 copy-done.5
  92.2 0.1 broadcast_in_dim.4
  92.3 0.9 copy-done
  93.2 1.0 %fusion.7 = (f32[22,38,134]{2,1,0:T(8,128)S(1)}, f32[22,38,134]{2,1,0:T(8,128)S(1)}) fusion(f32[22,38,134]{2,1,0:T(8,128)S(1)} %broadcast_in_dim.4, f32[]{:T(128)S(6)} %add.142, pred[134]{0:T(512)(128)(4,1)S(1)} %compare_and_fusion, pred[38]{0:T(512)(128)(4,1)S(1)} %compare_and_fusion.1, pred[22]{0:T(512)(128)(4,1)S(1)} %compare_and_fusion.2, ...), kind=kLoop, calls=%fused_computation.13 | loop fusion | flops 1792384 | bytes 1792582 | tf_op jit(solution)/shard_map/mul | solution.py:791
  94.2 0.6 divide_select_fusion.1
  94.8 0.7 divide_select_fusion
  95.5 0.7 slice_add_fusion
  96.2 0.2 and_and_fusion
  96.4 0.1 copy-done.2
  96.5 1.2 %fusion.20 = f32[1,16,32,128]{3,2,1,0:T(8,128)} fusion(f32[16,32,128]{2,1,0:T(8,128)S(1)} %copy-done.2, f32[16,32,128]{2,1,0:T(8,128)S(1)} %copy-done, f32[22,38,134]{2,1,0:T(8,128)S(1)} %get-tuple-element.33, f32[22,38,134]{2,1,0:T(8,128)S(1)} %get-tuple-element.32, f32[22,38,134]{2,1,0:T(8,128)S(1)} %get-tuple-element.31, ...), kind=kLoop, calls=%fused_computation.47 | loop fusion | flops 655360 | bytes 2162696 | tf_op jit(solution)/shard_map/add | solution.py:793
  97.7 0.7 copy.24
  (18 shorter events, 0.1 us)
Async XLA Ops:
  86.4 0.7 copy-start.11
  87.1 0.7 copy-start.8
  88.0 0.7 copy-start.10
  88.8 0.7 copy-start.9
  89.5 0.7 copy-start.7
  90.4 0.9 copy-start.6
  90.6 0.9 copy-start.5
  92.2 1.0 copy-start
  92.2 0.9 copy-start.3
  92.2 0.9 copy-start.4
  95.5 1.0 copy-start.2
  96.4 1.3 %copy-start.1 = (f32[16,32,128]{2,1,0:T(8,128)S(1)}, f32[16,32,128]{2,1,0:T(8,128)}, u32[]{:S(2)}) copy-start(f32[16,32,128]{2,1,0:T(8,128)} %get-tuple-element.27) | copy-start | bytes 786436

commit v17 on v15

--- a/solution.py
+++ b/solution.py
@@ -129,19 +129,23 @@
     coeff = _solve_ones(acc, depth + 1)
     rows = lax.broadcasted_iota(jnp.int32, coeff.shape, 0)
     c = [jnp.sum(jnp.where(rows == m, coeff, 0.0)) for m in range(depth + 1)]
-    rho_opt = c[0] * hin_ref[0].astype(jnp.float32)
     res_opt = c[0] * hres_ref[0].astype(jnp.float32)
     for m in range(1, depth):
-        rho_opt = rho_opt + c[m] * hin_ref[m].astype(jnp.float32)
         res_opt = res_opt + c[m] * hres_ref[m].astype(jnp.float32)
-    ropt_ref[...] = rho_opt + c[depth] * din_ref[...]
     sopt_ref[...] = res_opt + c[depth] * residual
+
+    def finish_rho_opt():
+        rho_opt = c[0] * hin_ref[0].astype(jnp.float32)
+        for m in range(1, depth):
+            rho_opt = rho_opt + c[m] * hin_ref[m].astype(jnp.float32)
+        ropt_ref[...] = rho_opt + c[depth] * din_ref[...]
+
     h = xlo_s.shape[0]
     cx = sopt_ref.shape[0]
     cy = sopt_ref.shape[1]
     wy = ylo_s.shape[1]
 
-    def exchange(lo_src, hi_src, lo_dst, hi_dst, sems, has_lo, has_hi, lo_dev, hi_dev, lo_out, hi_out):
+    def exchange(lo_src, hi_src, lo_dst, hi_dst, sems, has_lo, has_hi, lo_dev, hi_dev, lo_out, hi_out, between=None):
         def to_lo(dev):
             return pltpu.make_async_remote_copy(
                 src_ref=lo_src, dst_ref=hi_dst, send_sem=sems.at[0], recv_sem=sems.at[3], device_id=dev,
@@ -162,6 +166,9 @@
         def _():
             to_hi(hi_dev).start()
 
+        if between is not None:
+            between()
+
         @pl.when(has_lo)
         def _():
             to_lo(lo_dev).wait_send()
@@ -183,37 +190,42 @@
             hi_out[...] = jnp.zeros(hi_out.shape, jnp.float32)
 
     exchange(sopt_ref.at[pl.ds(0, h)], sopt_ref.at[pl.ds(cx - h, h)], xlo_s, xhi_s, hx,
-             row > 0, row < nb - 1, ((row - 1) * na + j, band), ((row + 1) * na + j, band), xlo_ref, xhi_ref)
+             row > 0, row < nb - 1, ((row - 1) * na + j, band), ((row + 1) * na + j, band), xlo_ref, xhi_ref,
+             between=finish_rho_opt)
     xext[pl.ds(0, h)] = xlo_ref[...]
     xext[pl.ds(h, cx)] = sopt_ref[...]
     xext[pl.ds(h + cx, h)] = xhi_ref[...]
-    by = j // 4
-    exchange(xext.at[:, pl.ds(0, wy)], xext.at[:, pl.ds(cy - wy, wy)], ylo_s, yhi_s, hy,
-             by > 0, by < 3, (me - 4, band), (me + 4, band), ylo_ref, yhi_ref)
-    if z_refs is None:
-        return
-    zlo_ref, zhi_ref, zs_lo, zs_hi, zr_lo, zr_hi, hz = z_refs
     cz = sopt_ref.shape[2]
     s_row = lax.broadcasted_iota(jnp.int32, (8, cz), 0)
     s_lane = lax.broadcasted_iota(jnp.int32, (8, cz), 1)
     sel_lo = jnp.where((s_row < h) & (s_lane == s_row), 1.0, 0.0)
     sel_hi = jnp.where((s_row < h) & (s_lane == cz - h + s_row), 1.0, 0.0)
-    pieces = (
-        (xext[...].reshape(-1, cz), 0),
-        (ylo_ref[...].reshape(-1, cz), 768),
-        (yhi_ref[...].reshape(-1, cz), 1024),
-    )
-    zs_lo[...] = jnp.zeros(zs_lo.shape, jnp.float32)
-    zs_hi[...] = jnp.zeros(zs_hi.shape, jnp.float32)
-    for piece, at in pieces:
+    dims = (((1,), (1,)), ((), ()))
+
+    def z_piece(piece, at):
+        zlo_ref, zhi_ref, zs_lo, zs_hi, zr_lo, zr_hi, hz = z_refs
         width = piece.shape[0]
-        dims = (((1,), (1,)), ((), ()))
         zs_lo[:, pl.ds(at, width)] = lax.dot_general(
             sel_lo, piece, dims, precision=lax.Precision.HIGHEST, preferred_element_type=jnp.float32
         )
         zs_hi[:, pl.ds(at, width)] = lax.dot_general(
             sel_hi, piece, dims, precision=lax.Precision.HIGHEST, preferred_element_type=jnp.float32
         )
+
+    def z_core():
+        if z_refs is not None:
+            z_refs[2][...] = jnp.zeros(z_refs[2].shape, jnp.float32)
+            z_refs[3][...] = jnp.zeros(z_refs[3].shape, jnp.float32)
+            z_piece(xext[...].reshape(-1, cz), 0)
+
+    by = j // 4
+    exchange(xext.at[:, pl.ds(0, wy)], xext.at[:, pl.ds(cy - wy, wy)], ylo_s, yhi_s, hy,
+             by > 0, by < 3, (me - 4, band), (me + 4, band), ylo_ref, yhi_ref, between=z_core)
+    if z_refs is None:
+        return
+    zlo_ref, zhi_ref, zs_lo, zs_hi, zr_lo, zr_hi, hz = z_refs
+    z_piece(ylo_ref[...].reshape(-1, cz), 768)
+    z_piece(yhi_ref[...].reshape(-1, cz), 1024)
     bzz = me % 4
     exchange(zs_lo, zs_hi, zr_lo, zr_hi, hz, bzz > 0, bzz < 3, (me - 1, band), (me + 1, band), zlo_ref, zhi_ref)
 

time: 97.5 us -> 96.4 us (0.989)
  Pallas kernels: 84.9 us -> 83.7 us
    pallas_call x1, Pallas kernels: 84.9 us -> 83.7 us  [density_step(): pl.pallas_call(functools.partial(_step_kernel, n, len(dens_scratch)), out...]
where the time goes in v17:
time: 96.4 us; the launch traced here: 96 us
  Pallas kernels  83.7 us (87%)
  local copies, waits for them, and re-layouts  6.07 us (6%)
  other arithmetic  4.63 us (5%)
  between operations  1.51 us (2%)
    pallas_call x1, Pallas kernels, density_step(): pl.pallas_call(functools.partial(_step_kernel, n, len(dens_scratch)), out...  83.7 us
    unnamed x15, local copies, waits for them, and re-layouts  2.53 us
    mul x3, other arithmetic, local(): field_u = (ext + beside) / (6.0 + kappa) * mask  2.31 us

profile of v17, /device:TPU:1, one launch (start us, length us, event | category | flops | bytes accessed | tf_op | source)
XLA Modules:
  0.0 96.0 jit_solution(14037115880832677772)
XLA Ops:
  0.7 83.7 %shard_map.77 = (f32[16,32,128]{2,1,0:T(8,128)}, f32[8,128]{1,0:T(8,128)}, f32[16,128]{1,0:T(8,128)}, f32[16,32,128]{2,1,0:T(8,128)}, f32[16,32,128]{2,1,0:T(8,1...) custom-call(f32[4]{0:T(128)} %occ_ref.1, ...), custom_call_target="tpu_custom_call" | custom-call | tf_op jit(solution)/shard_map/pallas_call | solution.py:272
  84.5 0.8 fusion.21
  85.2 0.1 reshape.26
  85.3 0.1 slice.148
  85.4 0.1 reshape.28
  85.5 0.7 slice.113
  86.2 0.1 reshape.27
  86.3 0.1 pad_maximum_fusion.1
  86.4 0.3 copy.20
  86.7 0.1 reshape.29
  86.8 0.1 slice.150
  86.9 0.1 reshape.31
  87.0 0.7 slice.120
  87.7 0.1 reshape.30
  87.8 0.1 pad_maximum_fusion.2
  87.9 0.0 copy-start.6
  87.9 0.3 copy.21
  88.2 0.6 copy-done.6
  88.8 0.3 copy-done.5
  89.8 0.0 copy-start
  89.8 0.0 copy-start.3
  89.8 0.0 copy-start.4
  89.8 0.1 broadcast_in_dim.4
  89.9 0.9 copy-done
  90.7 1.0 %fusion.7 = (f32[22,38,134]{2,1,0:T(8,128)S(1)}, f32[22,38,134]{2,1,0:T(8,128)S(1)}) fusion(f32[22,38,134]{2,1,0:T(8,128)S(1)} %broadcast_in_dim.4, f32[]{:T(128)S(6)} %add.142, pred[134]{0:T(512)(128)(4,1)S(1)} %compare_and_fusion, pred[38]{0:T(512)(128)(4,1)S(1)} %compare_and_fusion.1, pred[22]{0:T(512)(128)(4,1)S(1)} %compare_and_fusion.2, ...), kind=kLoop, calls=%fused_computation.13 | loop fusion | flops 1792384 | bytes 1792582 | tf_op jit(solution)/shard_map/mul | solution.py:796
  91.8 0.6 divide_select_fusion.1
  92.4 0.7 divide_select_fusion
  93.1 0.7 slice_add_fusion
  93.7 0.2 and_and_fusion
  93.9 0.1 copy-done.2
  94.0 1.2 %fusion.20 = f32[1,16,32,128]{3,2,1,0:T(8,128)} fusion(f32[16,32,128]{2,1,0:T(8,128)S(1)} %copy-done.2, f32[16,32,128]{2,1,0:T(8,128)S(1)} %copy-done, f32[22,38,134]{2,1,0:T(8,128)S(1)} %get-tuple-element.25, f32[22,38,134]{2,1,0:T(8,128)S(1)} %get-tuple-element.24, f32[22,38,134]{2,1,0:T(8,128)S(1)} %get-tuple-element.23, ...), kind=kLoop, calls=%fused_computation.47 | loop fusion | flops 655360 | bytes 2162696 | tf_op jit(solution)/shard_map/add | solution.py:798
  95.2 0.7 copy.24
  (11 shorter events, 0.1 us)
Async XLA Ops:
  87.9 0.9 copy-start.6
  88.2 0.9 copy-start.5
  89.8 1.0 copy-start
  89.8 0.9 copy-start.3
  89.8 0.9 copy-start.4
  93.0 1.0 copy-start.2
  94.0 1.3 %copy-start.1 = (f32[16,32,128]{2,1,0:T(8,128)S(1)}, f32[16,32,128]{2,1,0:T(8,128)}, u32[]{:S(2)}) copy-start(f32[16,32,128]{2,1,0:T(8,128)} %get-tuple-element.19) | copy-start | bytes 786436

commit v18 on v17

--- a/solution.py
+++ b/solution.py
@@ -449,14 +449,14 @@
     for k in range(1, w_ref.shape[0]):
         part = part + occ_ref[k] * jnp.square(w_ref[k].astype(jnp.float32))
     p_ref[...] = part
-    pl.semaphore_wait(barrier, 7 + na - 1 + nb - 1)
 
     e = 2 * x + zhi
     lane = lax.broadcasted_iota(jnp.int32, ga_sum.shape, 1)
     first = lax.broadcasted_iota(jnp.int32, ga_sum.shape, 0) == 0
     din_pair = jnp.sum(d_ref[pl.ds(e, 1)]) + jnp.sum(d_ref[pl.ds(rows - 1 - e, 1)])
-    own = jnp.where(first & (lane == 0), jnp.sum(p_ref[...]), jnp.where(first & (lane == 1), din_pair, 0.0))
+    own = jnp.where(first & (lane == 0), jnp.sum(part), jnp.where(first & (lane == 1), din_pair, 0.0))
     ga_in[gj] = own
+    pl.semaphore_wait(barrier, 7 + na - 1 + nb - 1)
 
     def copy_ga(slot, peer_j):
         return pltpu.make_async_remote_copy(

time: 96.4 us -> 96.2 us (level)
  no operation moved by 1% of the time
where the time goes in v18:
time: 96.2 us; the launch traced here: 95.7 us
  Pallas kernels  83.5 us (87%)
  local copies, waits for them, and re-layouts  6.07 us (6%)
  other arithmetic  4.63 us (5%)
  between operations  1.51 us (2%)
    pallas_call x1, Pallas kernels, density_step(): pl.pallas_call(functools.partial(_step_kernel, n, len(dens_scratch)), out...  83.5 us
    unnamed x15, local copies, waits for them, and re-layouts  2.53 us
    mul x3, other arithmetic, local(): field_u = (ext + beside) / (6.0 + kappa) * mask  2.31 us

profile of v18, /device:TPU:1, one launch (start us, length us, event | category | flops | bytes accessed | tf_op | source)
XLA Modules:
  0.0 95.7 jit_solution(3369359465808241815)
XLA Ops:
  0.7 83.5 %shard_map.77 = (f32[16,32,128]{2,1,0:T(8,128)}, f32[8,128]{1,0:T(8,128)}, f32[16,128]{1,0:T(8,128)}, f32[16,32,128]{2,1,0:T(8,128)}, f32[16,32,128]{2,1,0:T(8,1...) custom-call(f32[4]{0:T(128)} %occ_ref.1, ...), custom_call_target="tpu_custom_call" | custom-call | tf_op jit(solution)/shard_map/pallas_call | solution.py:272
  84.3 0.8 fusion.21
  85.0 0.1 reshape.26
  85.1 0.1 slice.148
  85.2 0.1 reshape.28
  85.3 0.7 slice.113
  86.0 0.1 reshape.27
  86.1 0.1 pad_maximum_fusion.1
  86.2 0.3 copy.20
  86.5 0.1 reshape.29
  86.6 0.1 slice.150
  86.7 0.1 reshape.31
  86.8 0.7 slice.120
  87.5 0.1 reshape.30
  87.6 0.1 pad_maximum_fusion.2
  87.7 0.3 copy.21
  88.0 0.6 copy-done.6
  88.6 0.3 copy-done.5
  89.5 0.0 copy-start
  89.6 0.0 copy-start.3
  89.6 0.0 copy-start.4
  89.6 0.1 broadcast_in_dim.4
  89.6 0.9 copy-done
  90.5 0.0 copy-done.3
  90.5 1.0 %fusion.7 = (f32[22,38,134]{2,1,0:T(8,128)S(1)}, f32[22,38,134]{2,1,0:T(8,128)S(1)}) fusion(f32[22,38,134]{2,1,0:T(8,128)S(1)} %broadcast_in_dim.4, f32[]{:T(128)S(6)} %add.142, pred[134]{0:T(512)(128)(4,1)S(1)} %compare_and_fusion, pred[38]{0:T(512)(128)(4,1)S(1)} %compare_and_fusion.1, pred[22]{0:T(512)(128)(4,1)S(1)} %compare_and_fusion.2, ...), kind=kLoop, calls=%fused_computation.13 | loop fusion | flops 1792384 | bytes 1792582 | tf_op jit(solution)/shard_map/mul | solution.py:796
  91.5 0.6 divide_select_fusion.1
  92.2 0.7 divide_select_fusion
  92.8 0.7 slice_add_fusion
  93.5 0.2 and_and_fusion
  93.7 0.1 copy-done.2
  93.8 1.2 %fusion.20 = f32[1,16,32,128]{3,2,1,0:T(8,128)} fusion(f32[16,32,128]{2,1,0:T(8,128)S(1)} %copy-done.2, f32[16,32,128]{2,1,0:T(8,128)S(1)} %copy-done, f32[22,38,134]{2,1,0:T(8,128)S(1)} %get-tuple-element.25, f32[22,38,134]{2,1,0:T(8,128)S(1)} %get-tuple-element.24, f32[22,38,134]{2,1,0:T(8,128)S(1)} %get-tuple-element.23, ...), kind=kLoop, calls=%fused_computation.47 | loop fusion | flops 655360 | bytes 2162696 | tf_op jit(solution)/shard_map/add | solution.py:798
  95.0 0.7 copy.24
  (11 shorter events, 0.1 us)
Async XLA Ops:
  87.7 0.9 copy-start.6
  88.0 0.9 copy-start.5
  89.5 1.0 copy-start
  89.6 0.9 copy-start.3
  89.6 0.9 copy-start.4
  92.8 1.0 copy-start.2
  93.8 1.3 %copy-start.1 = (f32[16,32,128]{2,1,0:T(8,128)S(1)}, f32[16,32,128]{2,1,0:T(8,128)}, u32[]{:S(2)}) copy-start(f32[16,32,128]{2,1,0:T(8,128)} %get-tuple-element.19) | copy-start | bytes 786436

commit v19 on v18

--- a/solution.py
+++ b/solution.py
@@ -277,7 +277,7 @@
         scratch_shapes=dens_scratch + mix_scratch,
         compiler_params=pltpu.CompilerParams(collective_id=3, has_side_effects=True),
     )(occ, waves, din, hres, hin)
-    return outs[len(dens_outs):]
+    return outs[: len(dens_outs)] + outs[len(dens_outs):]
 
 
 def mix(hres, hin, rho, din, charges, hist):
@@ -754,10 +754,10 @@
 
 
 def local(orbitals, occupations, density_in, history_in, history_res, screening):
-    residual, rho_opt, res_opt, x_lo, x_hi, y_lo, y_hi, z_lo, z_hi = density_step(
+    rho_block, charges, _, _, rho_opt, res_opt, x_lo, x_hi, y_lo, y_hi, z_lo, z_hi = density_step(
         occupations, orbitals[:, 0], density_in[0], history_res[:, 0], history_in[:, 0]
     )
-    residual = residual[None]
+    residual = (charges[0, 1] / charges[0, 0]) * rho_block[None] - density_in
     rho_opt = rho_opt[None]
     res_opt = res_opt[None]
     kappa = screening[0]

time: 96.2 us -> 99.1 us (1.030)
  between operations: 1.51 us -> 2.9 us
    slice x0 -> x1, local copies, waits for them, and re-layouts: none -> 1.42 us  [local(): residual = charges[0, 1] / charges[0, 0] * rho_block[None] - density_in]
    unnamed x15 -> x16, local copies, waits for them, and re-layouts: 2.53 us -> 1.83 us
where the time goes in v19:
time: 99.1 us; the launch traced here: 98.6 us
  Pallas kernels  83.5 us (84%)
  local copies, waits for them, and re-layouts  6.79 us (7%)
  other arithmetic  5.38 us (5%)
  between operations  2.9 us (3%)
    pallas_call x1, Pallas kernels, density_step(): pl.pallas_call(functools.partial(_step_kernel, n, len(dens_scratch)), out...  83.5 us
    mul x3, other arithmetic, local(): field_u = (ext + beside) / (6.0 + kappa) * mask  2.31 us

profile of v19, /device:TPU:1, one launch (start us, length us, event | category | flops | bytes accessed | tf_op | source)
XLA Modules:
  0.0 98.6 jit_solution(16665670752866791778)
XLA Ops:
  0.7 83.5 %shard_map.77 = (f32[16,32,128]{2,1,0:T(8,128)}, f32[8,128]{1,0:T(8,128)}, f32[16,128]{1,0:T(8,128)}, f32[16,32,128]{2,1,0:T(8,128)}, f32[16,32,128]{2,1,0:T(8,1...) custom-call(f32[4]{0:T(128)} %occ_ref.1, ...), custom_call_target="tpu_custom_call" | custom-call | tf_op jit(solution)/shard_map/pallas_call | solution.py:272
  84.3 0.8 fusion.21
  85.0 0.1 reshape.28
  85.1 0.1 slice.156
  85.2 0.1 reshape.30
  85.3 0.7 slice.119
  86.0 0.1 reshape.29
  86.1 0.1 pad_maximum_fusion.1
  86.2 0.3 copy.20
  86.5 0.1 reshape.31
  86.6 0.1 slice.158
  86.7 0.1 reshape.33
  86.8 0.7 slice.126
  87.5 0.1 reshape.32
  87.6 0.1 pad_maximum_fusion.2
  87.7 0.3 copy.21
  88.0 0.6 copy-done.7
  88.6 0.3 copy-done.6
  89.5 0.0 copy-start.1
  89.6 0.0 copy-start.4
  89.6 0.0 copy-start.5
  89.6 0.1 broadcast_in_dim.2
  89.6 0.9 copy-done.1
  90.5 1.0 %fusion.7 = (f32[22,38,134]{2,1,0:T(8,128)S(1)}, f32[22,38,134]{2,1,0:T(8,128)S(1)}) fusion(f32[22,38,134]{2,1,0:T(8,128)S(1)} %broadcast_in_dim.2, f32[]{:T(128)S(6)} %add.142, pred[134]{0:T(512)(128)(4,1)S(1)} %compare_and_fusion, pred[38]{0:T(512)(128)(4,1)S(1)} %compare_and_fusion.1, pred[22]{0:T(512)(128)(4,1)S(1)} %compare_and_fusion.2, ...), kind=kLoop, calls=%fused_computation.13 | loop fusion | flops 1792384 | bytes 1792582 | tf_op jit(solution)/shard_map/mul | solution.py:796
  91.5 0.6 divide_select_fusion.1
  92.2 0.7 divide_select_fusion
  92.8 0.7 slice_add_fusion
  93.5 0.2 and_and_fusion
  93.7 0.1 copy-done.3
  93.8 1.2 %fusion.20 = f32[1,16,32,128]{3,2,1,0:T(8,128)} fusion(f32[16,32,128]{2,1,0:T(8,128)S(1)} %copy-done.3, f32[16,32,128]{2,1,0:T(8,128)S(1)} %copy-done.1, f32[22,38,134]{2,1,0:T(8,128)S(1)} %get-tuple-element.27, f32[22,38,134]{2,1,0:T(8,128)S(1)} %get-tuple-element.26, f32[22,38,134]{2,1,0:T(8,128)S(1)} %get-tuple-element.25, ...), kind=kLoop, calls=%fused_computation.48 | loop fusion | flops 655360 | bytes 2162696 | tf_op jit(solution)/shard_map/add | solution.py:798
  95.0 1.4 %fusion.23 = (f32[1,1]{1,0:T(1,128)}, f32[1,1]{1,0:T(1,128)}) fusion(f32[8,128]{1,0:T(8,128)} %get-tuple-element.20), kind=kLoop, calls=%fused_computation.56 | loop fusion | bytes 16 | tf_op jit(solution)/shard_map/slice | solution.py:760
  97.9 0.7 bitcast_subtract_fusion
  (14 shorter events, 0.1 us)
Async XLA Ops:
  87.7 0.9 copy-start.7
  88.0 0.9 copy-start.6
  89.5 1.0 copy-start.1
  89.6 0.9 copy-start.4
  89.6 0.9 copy-start.5
  92.8 1.0 copy-start.3
  93.8 4.1 %copy-start = (f32[1,16,32,128]{3,2,1,0:T(8,128)S(1)}, f32[1,16,32,128]{3,2,1,0:T(8,128)}, u32[]{:S(2)}) copy-start(f32[1,16,32,128]{3,2,1,0:T(8,128)} %param.8) | copy-start | bytes 786436
  93.8 4.1 %copy-start.2 = (f32[16,32,128]{2,1,0:T(8,128)S(1)}, f32[16,32,128]{2,1,0:T(8,128)}, u32[]{:S(2)}) copy-start(f32[16,32,128]{2,1,0:T(8,128)} %get-tuple-element.21) | copy-start | bytes 786436

commit v20 on v18

--- a/solution.py
+++ b/solution.py
@@ -256,10 +256,20 @@
 def _step_kernel(n, n_dens, occ_ref, w_ref, d_ref, h_ref, hin_ref, o_ref, c_ref, hg_ref,
                  res_ref, ropt_ref, sopt_ref, xlo_ref, xhi_ref, ylo_ref, yhi_ref, zlo_ref, zhi_ref, *scratch):
     _density_kernel(occ_ref, w_ref, d_ref, h_ref, o_ref, c_ref, hg_ref, *scratch[:n_dens])
+    ropt_v, sopt_v, out_sem = scratch[-3:]
+    scratch = scratch[:-3]
     mix_scratch = scratch[n_dens:-5]
-    _mix_kernel(n, h_ref, hin_ref, o_ref, d_ref, c_ref, hg_ref, res_ref, ropt_ref, sopt_ref,
+    _mix_kernel(n, h_ref, hin_ref, o_ref, d_ref, c_ref, hg_ref, res_ref, ropt_v, sopt_v,
                 xlo_ref, xhi_ref, ylo_ref, yhi_ref, *mix_scratch, entry=False,
                 z_refs=(zlo_ref, zhi_ref) + tuple(scratch[-5:]))
+    to_hbm = [
+        pltpu.make_async_copy(ropt_v, ropt_ref, out_sem.at[0]),
+        pltpu.make_async_copy(sopt_v, sopt_ref, out_sem.at[1]),
+    ]
+    for c in to_hbm:
+        c.start()
+    for c in to_hbm:
+        c.wait()
 
 
 def density_step(occ, waves, din, hres, hin):
@@ -269,11 +279,17 @@
     zface = jax.ShapeDtypeStruct((8, 1280), jnp.float32)
     mix_outs = mix_outs + (zface, zface)
     mix_scratch = mix_scratch + [pltpu.VMEM((8, 1280), jnp.float32)] * 4 + [pltpu.SemaphoreType.DMA((4,))]
+    mix_scratch = mix_scratch + [pltpu.VMEM(din.shape, jnp.float32)] * 2 + [pltpu.SemaphoreType.DMA((2,))]
+    vmem = pl.BlockSpec(memory_space=pltpu.VMEM)
+    hbm = pl.BlockSpec(memory_space=pl.ANY)
+    out_specs = [vmem] * (len(dens_outs) + len(mix_outs))
+    out_specs[len(dens_outs) + 1] = hbm
+    out_specs[len(dens_outs) + 2] = hbm
     outs = pl.pallas_call(
         functools.partial(_step_kernel, n, len(dens_scratch)),
         out_shape=dens_outs + mix_outs,
         in_specs=[pl.BlockSpec(memory_space=pltpu.SMEM)] + [pl.BlockSpec(memory_space=pltpu.VMEM)] * 4,
-        out_specs=(pl.BlockSpec(memory_space=pltpu.VMEM),) * (len(dens_outs) + len(mix_outs)),
+        out_specs=tuple(out_specs),
         scratch_shapes=dens_scratch + mix_scratch,
         compiler_params=pltpu.CompilerParams(collective_id=3, has_side_effects=True),
     )(occ, waves, din, hres, hin)

time: 96.2 us -> 96.8 us (level)
  no operation moved by 1% of the time
where the time goes in v20:
time: 96.8 us; the launch traced here: 96.4 us
  Pallas kernels  84.2 us (87%)
  local copies, waits for them, and re-layouts  6.07 us (6%)
  other arithmetic  4.63 us (5%)
  between operations  1.51 us (2%)
    pallas_call x1, Pallas kernels, density_step(): pl.pallas_call(functools.partial(_step_kernel, n, len(dens_scratch)), out...  84.2 us
    unnamed x15, local copies, waits for them, and re-layouts  2.53 us
    mul x3, other arithmetic, local(): field_u = (ext + beside) / (6.0 + kappa) * mask  2.31 us

profile of v20, /device:TPU:1, one launch (start us, length us, event | category | flops | bytes accessed | tf_op | source)
XLA Modules:
  0.0 96.4 jit_solution(17829036732960531766)
XLA Ops:
  0.7 84.2 %shard_map.77 = (f32[16,32,128]{2,1,0:T(8,128)}, f32[8,128]{1,0:T(8,128)}, f32[16,128]{1,0:T(8,128)}, f32[16,32,128]{2,1,0:T(8,128)}, f32[16,32,128]{2,1,0:T(8,1...) custom-call(f32[4]{0:T(128)} %occ_ref.1, ...), custom_call_target="tpu_custom_call" | custom-call | tf_op jit(solution)/shard_map/pallas_call | solution.py:288
  84.9 0.8 fusion.21
  85.6 0.1 reshape.26
  85.7 0.1 slice.148
  85.8 0.1 reshape.28
  85.9 0.7 slice.113
  86.7 0.1 reshape.27
  86.7 0.1 pad_maximum_fusion.1
  86.8 0.3 copy.20
  87.1 0.1 reshape.29
  87.2 0.1 slice.150
  87.3 0.1 reshape.31
  87.4 0.7 slice.120
  88.1 0.1 reshape.30
  88.2 0.1 pad_maximum_fusion.2
  88.3 0.0 copy-start.6
  88.3 0.3 copy.21
  88.6 0.6 copy-done.6
  89.2 0.3 copy-done.5
  90.2 0.0 copy-start
  90.2 0.0 copy-start.3
  90.2 0.0 copy-start.4
  90.2 0.1 broadcast_in_dim.4
  90.3 0.9 copy-done
  91.1 1.0 %fusion.7 = (f32[22,38,134]{2,1,0:T(8,128)S(1)}, f32[22,38,134]{2,1,0:T(8,128)S(1)}) fusion(f32[22,38,134]{2,1,0:T(8,128)S(1)} %broadcast_in_dim.4, f32[]{:T(128)S(6)} %add.142, pred[134]{0:T(512)(128)(4,1)S(1)} %compare_and_fusion, pred[38]{0:T(512)(128)(4,1)S(1)} %compare_and_fusion.1, pred[22]{0:T(512)(128)(4,1)S(1)} %compare_and_fusion.2, ...), kind=kLoop, calls=%fused_computation.13 | loop fusion | flops 1792384 | bytes 1792582 | tf_op jit(solution)/shard_map/mul | solution.py:812
  92.2 0.6 divide_select_fusion.1
  92.8 0.7 divide_select_fusion
  93.5 0.7 slice_add_fusion
  94.1 0.2 and_and_fusion
  94.3 0.1 copy-done.2
  94.4 1.2 %fusion.20 = f32[1,16,32,128]{3,2,1,0:T(8,128)} fusion(f32[16,32,128]{2,1,0:T(8,128)S(1)} %copy-done.2, f32[16,32,128]{2,1,0:T(8,128)S(1)} %copy-done, f32[22,38,134]{2,1,0:T(8,128)S(1)} %get-tuple-element.25, f32[22,38,134]{2,1,0:T(8,128)S(1)} %get-tuple-element.24, f32[22,38,134]{2,1,0:T(8,128)S(1)} %get-tuple-element.23, ...), kind=kLoop, calls=%fused_computation.47 | loop fusion | flops 655360 | bytes 2162696 | tf_op jit(solution)/shard_map/add | solution.py:814
  95.7 0.7 copy.24
  (11 shorter events, 0.1 us)
Async XLA Ops:
  88.3 0.9 copy-start.6
  88.6 0.9 copy-start.5
  90.2 1.0 copy-start
  90.2 0.9 copy-start.3
  90.2 0.9 copy-start.4
  93.5 1.0 copy-start.2
  94.4 1.3 %copy-start.1 = (f32[16,32,128]{2,1,0:T(8,128)S(1)}, f32[16,32,128]{2,1,0:T(8,128)}, u32[]{:S(2)}) copy-start(f32[16,32,128]{2,1,0:T(8,128)} %get-tuple-element.19) | copy-start | bytes 786436

commit v21 on v18

--- a/solution.py
+++ b/solution.py
@@ -190,8 +190,7 @@
             hi_out[...] = jnp.zeros(hi_out.shape, jnp.float32)
 
     exchange(sopt_ref.at[pl.ds(0, h)], sopt_ref.at[pl.ds(cx - h, h)], xlo_s, xhi_s, hx,
-             row > 0, row < nb - 1, ((row - 1) * na + j, band), ((row + 1) * na + j, band), xlo_ref, xhi_ref,
-             between=finish_rho_opt)
+             row > 0, row < nb - 1, ((row - 1) * na + j, band), ((row + 1) * na + j, band), xlo_ref, xhi_ref)
     xext[pl.ds(0, h)] = xlo_ref[...]
     xext[pl.ds(h, cx)] = sopt_ref[...]
     xext[pl.ds(h + cx, h)] = xhi_ref[...]
@@ -213,6 +212,7 @@
         )
 
     def z_core():
+        finish_rho_opt()
         if z_refs is not None:
             z_refs[2][...] = jnp.zeros(z_refs[2].shape, jnp.float32)
             z_refs[3][...] = jnp.zeros(z_refs[3].shape, jnp.float32)

time: 96.2 us -> 96.2 us (level)
  no operation moved by 1% of the time
where the time goes in v21:
time: 96.2 us; the launch traced here: 95.7 us
  Pallas kernels  83.5 us (87%)
  local copies, waits for them, and re-layouts  6.07 us (6%)
  other arithmetic  4.63 us (5%)
  between operations  1.51 us (2%)
    pallas_call x1, Pallas kernels, density_step(): pl.pallas_call(functools.partial(_step_kernel, n, len(dens_scratch)), out...  83.5 us
    unnamed x15, local copies, waits for them, and re-layouts  2.53 us
    mul x3, other arithmetic, local(): field_u = (ext + beside) / (6.0 + kappa) * mask  2.31 us

profile of v21, /device:TPU:1, one launch (start us, length us, event | category | flops | bytes accessed | tf_op | source)
XLA Modules:
  0.0 95.7 jit_solution(13032204217091974214)
XLA Ops:
  0.7 83.5 %shard_map.77 = (f32[16,32,128]{2,1,0:T(8,128)}, f32[8,128]{1,0:T(8,128)}, f32[16,128]{1,0:T(8,128)}, f32[16,32,128]{2,1,0:T(8,128)}, f32[16,32,128]{2,1,0:T(8,1...) custom-call(f32[4]{0:T(128)} %occ_ref.1, ...), custom_call_target="tpu_custom_call" | custom-call | tf_op jit(solution)/shard_map/pallas_call | solution.py:272
  84.3 0.8 fusion.21
  85.0 0.1 reshape.26
  85.1 0.1 slice.148
  85.2 0.1 reshape.28
  85.3 0.7 slice.113
  86.0 0.1 reshape.27
  86.1 0.1 pad_maximum_fusion.1
  86.2 0.3 copy.20
  86.5 0.1 reshape.29
  86.6 0.1 slice.150
  86.7 0.1 reshape.31
  86.8 0.7 slice.120
  87.5 0.1 reshape.30
  87.6 0.1 pad_maximum_fusion.2
  87.7 0.3 copy.21
  88.0 0.6 copy-done.6
  88.6 0.3 copy-done.5
  89.5 0.0 copy-start
  89.6 0.0 copy-start.3
  89.6 0.0 copy-start.4
  89.6 0.1 broadcast_in_dim.4
  89.6 0.9 copy-done
  90.5 0.0 copy-done.3
  90.5 1.0 %fusion.7 = (f32[22,38,134]{2,1,0:T(8,128)S(1)}, f32[22,38,134]{2,1,0:T(8,128)S(1)}) fusion(f32[22,38,134]{2,1,0:T(8,128)S(1)} %broadcast_in_dim.4, f32[]{:T(128)S(6)} %add.142, pred[134]{0:T(512)(128)(4,1)S(1)} %compare_and_fusion, pred[38]{0:T(512)(128)(4,1)S(1)} %compare_and_fusion.1, pred[22]{0:T(512)(128)(4,1)S(1)} %compare_and_fusion.2, ...), kind=kLoop, calls=%fused_computation.13 | loop fusion | flops 1792384 | bytes 1792582 | tf_op jit(solution)/shard_map/mul | solution.py:796
  91.5 0.6 divide_select_fusion.1
  92.2 0.7 divide_select_fusion
  92.8 0.7 slice_add_fusion
  93.5 0.2 and_and_fusion
  93.7 0.1 copy-done.2
  93.8 1.2 %fusion.20 = f32[1,16,32,128]{3,2,1,0:T(8,128)} fusion(f32[16,32,128]{2,1,0:T(8,128)S(1)} %copy-done.2, f32[16,32,128]{2,1,0:T(8,128)S(1)} %copy-done, f32[22,38,134]{2,1,0:T(8,128)S(1)} %get-tuple-element.25, f32[22,38,134]{2,1,0:T(8,128)S(1)} %get-tuple-element.24, f32[22,38,134]{2,1,0:T(8,128)S(1)} %get-tuple-element.23, ...), kind=kLoop, calls=%fused_computation.47 | loop fusion | flops 655360 | bytes 2162696 | tf_op jit(solution)/shard_map/add | solution.py:798
  95.0 0.7 copy.24
  (11 shorter events, 0.1 us)
Async XLA Ops:
  87.7 0.9 copy-start.6
  88.0 0.9 copy-start.5
  89.5 1.0 copy-start
  89.6 0.9 copy-start.3
  89.6 0.9 copy-start.4
  92.8 1.0 copy-start.2
  93.8 1.3 %copy-start.1 = (f32[16,32,128]{2,1,0:T(8,128)S(1)}, f32[16,32,128]{2,1,0:T(8,128)}, u32[]{:S(2)}) copy-start(f32[16,32,128]{2,1,0:T(8,128)} %get-tuple-element.19) | copy-start | bytes 786436
